TPU v7x, 32 devices: a whole 2x2x4 slice. The times are simulated.
32 devices in a mesh: field: 2 (over x), soil: 4 (over y, core), stand: 4 (over z).
Axes of the slice: x: 2, y: 2, z: 4, core: 2. Of those that a mesh axis runs over, the one named last changes fastest.
Arguments:
- query_tokens: bfloat16 [4096, 1024], P(('field', 'stand', 'soil')), parts along dimension 0, may hold values from -80 to 80
- key_tokens: bfloat16 [4096, 1024], P(('field', 'soil')), parts along dimension 0, may hold values from -6 to 6
- w_in: bfloat16 [1024, 1536], replicated, may hold values from -0.1875 to 0.1875
- w_out: bfloat16 [512, 1024], replicated, may hold values from -0.25 to 0.25
- out_grad: bfloat16 [4096, 1024], P(('field', 'stand', 'soil')), parts along dimension 0, may hold values from -6 to 6
- crossing: int32 [32, 16], P(('field', 'stand', 'soil')), parts along dimension 0, may hold values from 0 to 1
- home: int32 [32], P(('field', 'stand', 'soil')), parts along dimension 0, may hold values from 0 to 15
Outputs:
- output: bfloat16 [4096, 1024], P(('field', 'stand', 'soil')), parts along dimension 0
- query_grad: bfloat16 [4096, 1024], P(('field', 'stand', 'soil')), parts along dimension 0
- key_grad: bfloat16 [4096, 1024], P(('field', 'soil')), parts along dimension 0
- w_in_grad: float32 [2048, 1536], P(('field', 'soil')), parts along dimension 0
- w_out_grad: float32 [1024, 1024], P(('field', 'soil')), parts along dimension 0
There are 2 independent parts, one for each index of `field`. A program takes and returns all parts, laid end to end along the dimension named above; an argument that names none is the same for every part. Nothing has to cross between parts.
All inputs are finite; a program needn't handle non-finite values.
Results may differ from a plain program's by a relative error of at most 0.039.
Values may be sent and summed in bfloat16 or wider, within the bound.
No kernel may reach another device: no remote copies, remote signals or barrier semaphores. Data moves between devices by JAX's collectives and lax.ppermute only.
A program may use at most 128 MiB of HBM per device.

v0:
```python
import math

import jax
import jax.numpy as jnp
from jax import lax
from jax.sharding import PartitionSpec as P

HEADS = 4
DH = 128
BLOCK = 128


NEG = -1e30


def from_behind(block, axis, distance):
    devices = range(lax.axis_size(axis))
    route = [((i - distance) % len(devices), i) for i in devices]
    return lax.ppermute(block, axis, route)


def tile_mask(allowed, offset, columns):
    key_blocks = allowed.shape[1]
    column_block = (offset + jnp.arange(columns, dtype=jnp.int32)) // BLOCK
    onehot = (jnp.arange(key_blocks, dtype=jnp.int32)[:, None] == column_block[None, :]).astype(
        jnp.float32
    )
    coarse = jnp.dot(allowed, onehot)
    expanded = jnp.broadcast_to(coarse[:, None, :], (coarse.shape[0], BLOCK, columns))
    return expanded.reshape(coarse.shape[0] * BLOCK, columns)


def guarded_update(update, allowed_mask, operands, carried):
    return update(*operands, allowed_mask, carried)


def forward_tile(queries, key_proj, values, allowed_mask, carried):
    row_best, row_total, summed = carried
    query_count = queries.shape[0]
    key_count = key_proj.shape[0]
    query_heads = queries.reshape(query_count, HEADS, DH)
    key_heads = key_proj.reshape(key_count, HEADS, DH)
    value_heads = values.reshape(key_count, HEADS, DH)
    scores = jnp.einsum(
        "qhd,khd->hqk", query_heads, key_heads, preferred_element_type=jnp.float32
    ) * (1.0 / math.sqrt(DH))
    guarded = jnp.where(allowed_mask[None, :, :] > 0, scores, NEG)
    new_best = jnp.maximum(row_best, jnp.max(guarded, axis=2))
    rescale = jnp.exp(row_best - new_best)
    weights = jnp.exp(guarded - new_best[:, :, None]) * allowed_mask[None, :, :]
    row_total = row_total * rescale + jnp.sum(weights, axis=2)
    contrib = jnp.einsum(
        "hqk,khd->qhd",
        weights.astype(jnp.bfloat16),
        value_heads,
        preferred_element_type=jnp.float32,
    )
    summed = summed.reshape(query_count, HEADS, DH) * rescale.T[:, :, None] + contrib
    return (new_best, row_total, summed.reshape(query_count, HEADS * DH))


def backward_tile(queries, grad_att, log_total, spread, key_proj, values, allowed_mask, carried):
    grad_query, grad_key, grad_value = carried
    query_count = queries.shape[0]
    key_count = key_proj.shape[0]
    query_heads = queries.reshape(query_count, HEADS, DH)
    grad_heads = grad_att.reshape(query_count, HEADS, DH)
    key_heads = key_proj.reshape(key_count, HEADS, DH)
    value_heads = values.reshape(key_count, HEADS, DH)
    score_scale = 1.0 / math.sqrt(DH)
    scores = (
        jnp.einsum("qhd,khd->hqk", query_heads, key_heads, preferred_element_type=jnp.float32)
        * score_scale
    )
    probs = jnp.exp(jnp.where(allowed_mask[None, :, :] > 0, scores - log_total[:, :, None], NEG))
    grad_probs = jnp.einsum(
        "qhd,khd->hqk", grad_heads, value_heads, preferred_element_type=jnp.float32
    )
    grad_scores = (probs * (grad_probs - spread[:, :, None])).astype(jnp.bfloat16)
    query_step = (
        jnp.einsum("hqk,khd->qhd", grad_scores, key_heads, preferred_element_type=jnp.float32)
        * score_scale
    )
    key_step = (
        jnp.einsum("hqk,qhd->khd", grad_scores, query_heads, preferred_element_type=jnp.float32)
        * score_scale
    )
    value_step = jnp.einsum(
        "hqk,qhd->khd", probs.astype(jnp.bfloat16), grad_heads, preferred_element_type=jnp.float32
    )
    grad_query = grad_query + query_step.reshape(query_count, HEADS * DH)
    grad_key = grad_key + key_step.reshape(key_count, HEADS * DH)
    grad_value = grad_value + value_step.reshape(key_count, HEADS * DH)
    return (grad_query, grad_key, grad_value)


def body(query_tokens, key_tokens, w_in, w_out, out_grad, crossing, home):
    attn_width = HEADS * DH
    query_count = query_tokens.shape[0]
    key_count = key_tokens.shape[0]
    soil_count = lax.axis_size("soil")
    soil_index = lax.axis_index("soil")
    stand_count = lax.axis_size("stand")
    stand_index = lax.axis_index("stand")
    total_blocks = key_count * soil_count // BLOCK
    allowed = (
        (crossing > 0) | (home[:, None] == jnp.arange(total_blocks, dtype=jnp.int32)[None, :])
    ).astype(jnp.float32)
    queries = jnp.dot(
        query_tokens, w_in[:, :attn_width], preferred_element_type=jnp.float32
    ).astype(jnp.bfloat16)
    projected = jnp.dot(
        key_tokens, w_in[:, attn_width:], preferred_element_type=jnp.float32
    ).astype(jnp.bfloat16)
    key_proj = projected[:, :attn_width]
    values = projected[:, attn_width:]
    key_offset = soil_index * key_count
    start_state = (
        jnp.full((HEADS, query_count), NEG, jnp.float32),
        jnp.zeros((HEADS, query_count), jnp.float32),
        jnp.zeros((query_count, attn_width), jnp.float32),
    )

    def forward_turn(turn_index, carried):
        moving, running = carried
        allowed_mask = tile_mask(moving[1].astype(jnp.float32), key_offset, key_count)
        running = guarded_update(forward_tile, allowed_mask, (moving[0], key_proj, values), running)
        moving = from_behind((moving[0], moving[1]), "soil", 1)
        running = from_behind(running, "soil", 1)
        return (moving, running)

    moving, running = lax.fori_loop(
        0, soil_count, forward_turn, ((queries, allowed.astype(jnp.bfloat16)), start_state)
    )
    row_best, row_total, summed = running
    attended = (
        (summed.reshape(query_count, HEADS, DH) / row_total.T[:, :, None])
        .reshape(query_count, attn_width)
        .astype(jnp.bfloat16)
    )
    log_total = row_best + jnp.log(row_total)
    output = jnp.dot(attended, w_out, preferred_element_type=jnp.float32).astype(jnp.bfloat16)
    grad_attended = lax.dot_general(
        out_grad, w_out, (((1,), (1,)), ((), ())), preferred_element_type=jnp.float32
    ).astype(jnp.bfloat16)
    spread = jnp.sum(
        (grad_attended.astype(jnp.float32) * attended.astype(jnp.float32)).reshape(
            query_count, HEADS, DH
        ),
        axis=2,
    ).T
    zero_query = jnp.zeros((query_count, attn_width), jnp.float32)
    zero_key = jnp.zeros((key_count, attn_width), jnp.float32)

    def backward_turn(turn_index, carried):
        moving, query_stats, grad_key, grad_value = carried
        allowed_mask = tile_mask(moving[2].astype(jnp.float32), key_offset, key_count)
        grad_query, grad_key, grad_value = guarded_update(
            backward_tile,
            allowed_mask,
            (moving[0], moving[1], query_stats[0], query_stats[1], key_proj, values),
            (query_stats[2], grad_key, grad_value),
        )
        moving = from_behind((moving[0], moving[1], moving[2]), "soil", 1)
        query_stats = from_behind((query_stats[0], query_stats[1], grad_query), "soil", 1)
        return (moving, query_stats, grad_key, grad_value)

    moving, query_stats, grad_key, grad_value = lax.fori_loop(
        0,
        soil_count,
        backward_turn,
        (
            (queries, grad_attended, allowed.astype(jnp.bfloat16)),
            (log_total, spread, zero_query),
            zero_key,
            zero_key,
        ),
    )
    grad_query = query_stats[2]
    grad_key, grad_value = lax.psum((grad_key, grad_value), "stand")
    key_grad_in = jnp.concatenate([grad_key, grad_value], axis=1).astype(jnp.bfloat16)
    query_grad_in = grad_query.astype(jnp.bfloat16)
    query_grad = lax.dot_general(
        query_grad_in,
        w_in[:, :attn_width],
        (((1,), (1,)), ((), ())),
        preferred_element_type=jnp.float32,
    ).astype(jnp.bfloat16)
    key_grad = lax.dot_general(
        key_grad_in,
        w_in[:, attn_width:],
        (((1,), (1,)), ((), ())),
        preferred_element_type=jnp.float32,
    ).astype(jnp.bfloat16)
    stand_rows = key_count // stand_count
    key_slice = lax.dynamic_slice_in_dim(key_tokens, stand_index * stand_rows, stand_rows, 0)
    grad_slice = lax.dynamic_slice_in_dim(key_grad_in, stand_index * stand_rows, stand_rows, 0)
    query_part = lax.dot_general(
        query_tokens, query_grad_in, (((0,), (0,)), ((), ())), preferred_element_type=jnp.float32
    )
    key_part = lax.dot_general(
        key_slice, grad_slice, (((0,), (0,)), ((), ())), preferred_element_type=jnp.float32
    )
    w_in_part = lax.psum_scatter(
        jnp.concatenate([query_part, key_part], axis=1), "soil", scatter_dimension=0, tiled=True
    )
    w_out_part = lax.psum_scatter(
        lax.dot_general(
            attended, out_grad, (((0,), (0,)), ((), ())), preferred_element_type=jnp.float32
        ),
        "soil",
        scatter_dimension=0,
        tiled=True,
    )
    w_in_grad, w_out_grad = lax.psum((w_in_part, w_out_part), "stand")
    return (output, query_grad, key_grad, w_in_grad, w_out_grad)


def solution(mesh):
    in_specs = (
        P(("field", "stand", "soil"), None),
        P(("field", "soil"), None),
        P(),
        P(),
        P(("field", "stand", "soil"), None),
        P(("field", "stand", "soil"), None),
        P(("field", "stand", "soil")),
    )
    out_specs = (
        P(("field", "stand", "soil"), None),
        P(("field", "stand", "soil"), None),
        P(("field", "soil"), None),
        P(("field", "soil"), None),
        P(("field", "soil"), None),
    )
    return jax.shard_map(body, mesh=mesh, in_specs=in_specs, out_specs=out_specs, check_vma=False)
```

profile of v0, /device:TPU:14, one launch (start us, length us, event | category | flops | bytes accessed | tf_op | source)
XLA Modules:
  0.0 371.4 jit_solution(13370454203672751986)
XLA Ops:
  12.2 2.8 fusion.37
  17.2 32.6 %while.47 = (s32[]{:T(128)}, bf16[128,512]{1,0:T(8,128)(2,1)S(1)}, bf16[1,16]{1,0:T(2,128)(2,1)S(1)}, f32[4,128]{1,0:T(4,128)S(1)}, f32[4,128]{1,0:T(4,128)S(1)}...) while((s32[]{:T(128)}, bf16[128,512]{1,0:T(8,128)(2,1)S(1)}, ...), condition=%wide.region_3.4_spmd, body=%wide.region_0.3_spmd.sunk | while | flops 136742912 | bytes 6747665 | solution.py:132
  21.7 3.1 collective-permute-done.1
  29.3 4.1 %collective-permute-done.1 = bf16[1,16]{1,0:T(2,128)(2,1)S(1)} collective-permute-done((bf16[1,16]{1,0:T(2,128)(2,1)S(1)}, bf16[1,16]{1,0:T(2,128)(2,1)S(1)}, u32[]{:S(2)}, u32[]{:S(2)}) %collective-permute-start.1) | collective-permute-done | bytes 64 | tf_op jit(solution)/shard_map/while/body/eval_jaxpr/ppermute | solution.py:19
  38.0 3.1 collective-permute-done.1
  45.7 4.1 %collective-permute-done.1 = bf16[1,16]{1,0:T(2,128)(2,1)S(1)} collective-permute-done((bf16[1,16]{1,0:T(2,128)(2,1)S(1)}, bf16[1,16]{1,0:T(2,128)(2,1)S(1)}, u32[]{:S(2)}, u32[]{:S(2)}) %collective-permute-start.1) | collective-permute-done | bytes 64 | tf_op jit(solution)/shard_map/while/body/eval_jaxpr/ppermute | solution.py:19
  57.7 74.9 %while.48 = (s32[]{:T(128)}, bf16[128,512]{0,1:T(8,128)(2,1)S(1)}, bf16[128,512]{0,1:T(8,128)(2,1)}, bf16[1,16]{1,0:T(2,128)(2,1)}, f32[4,128]{1,0:T(4,128)S(1)}...) while((s32[]{:T(128)}, bf16[128,512]{0,1:T(8,128)(2,1)S(1)}, ...), condition=%wide.region_6.7_spmd.clone, body=%wide.region_5.6_spmd.clone.sunk | while | flops 338854400 | bytes 18912868 | solution.py:168
  72.1 6.8 %collective-permute-done.10 = f32[128,512]{0,1:T(8,128)} collective-permute-done((f32[128,512]{0,1:T(8,128)}, f32[128,512]{0,1:T(8,128)}, u32[]{:S(2)}, u32[]{:S(2)}) %collective-permute-start.10) | collective-permute-done | bytes 262176 | tf_op jit(solution)/shard_map/while/body/eval_jaxpr/ppermute | solution.py:19
  81.2 2.2 collective-permute-start.8
  90.7 3.3 bitcast_add_fusion.6
  94.1 2.7 collective-permute-done.10
  99.1 2.2 collective-permute-start.8
  108.6 3.3 bitcast_add_fusion.6
  112.0 2.7 collective-permute-done.10
  117.0 2.2 collective-permute-start.8
  126.5 3.3 bitcast_add_fusion.6
  129.9 2.7 collective-permute-done.10
  132.6 73.3 %all-reduce.6 = (bf16[512,512]{0,1:T(8,128)(2,1)S(1)}, bf16[512,512]{0,1:T(8,128)(2,1)S(1)}) all-reduce(f32[512,512]{0,1:T(8,128)} %get-tuple-element.278, f32[512,512]{0,1:T(8,128)} %get-tuple-element.277), channel_id=1, replica_groups=mesh['field'=2,'soil'=4,'stand'=4] {'stand'}, use_global_device_ids=true, to_apply=%region_8.9 | all-reduce | flops 524288 | bytes 3145728 | tf_op jit(solution)/shard_map/psum | solution.py:180
  208.2 3.8 %pad_maximum_fusion = f32[1024,1536]{0,1:T(8,128)} fusion(f32[1024,1024]{0,1:T(8,128)S(1)} %fusion.46, f32[1024,512]{0,1:T(8,128)S(1)} %convolution_bitcast_fusion.1), kind=kLoop, calls=%fused_computation.60 | loop fusion | flops 1572864 | bytes 12582912 | tf_op jit(solution)/shard_map/concatenate | solution.py:205
  212.1 60.0 %reduce-scatter.3.cloned.1.call-done = f32[256,1536]{0,1:T(8,128)} async-done(((f32[1024,1536]{0,1:T(8,128)}), f32[256,1536]{0,1:T(8,128)}) %reduce-scatter.3.cloned.1.call-update) | async-done | bytes 1572880 | tf_op jit(solution)/shard_map/reduce_scatter | solution.py:204
  273.2 2.5 convolution_convert_fusion
  275.7 3.9 %fusion.40 = bf16[512,1024]{1,0:T(8,128)(2,1)} fusion(bf16[1024,1536]{1,0:T(8,128)(2,1)} %param.13, bf16[512,512]{0,1:T(8,128)(2,1)S(1)} %get-tuple-element.412, bf16[512,512]{0,1:T(8,128)(2,1)S(1)} %get-tuple-element.413), kind=kOutput, calls=%fused_computation.67 | convolution fusion | flops 1076363264 | bytes 4194304 | tf_op jit(solution)/shard_map/dot_general | solution.py:189
  279.5 81.4 %all-reduce.5.cloned.1.call-done = (f32[256,1536]{0,1:T(8,128)}, f32[128,1024]{1,0:T(8,128)}) async-done(((f32[256,1536]{0,1:T(8,128)}, f32[128,1024]{1,0:T(8,128)}), (f32[256,1536]{0,1:T(8,128)}, f32[128,1024]{1,0:T(8,128)})) %all-reduce.5.cloned.1.call-update) | async-done | bytes 2097168 | tf_op jit(solution)/shard_map/psum | solution.py:215
  361.0 3.1 copy.38
  (231 shorter events, 79.2 us)
Async XLA Ops:
  7.2 204.9 %reduce-scatter.5.cloned.1.call-start = ((), (), s32[]{:S(2)}) async-start(), calls=%async_computation.3 | async-start | bytes 2621440 | tf_op jit(solution)/shard_map/reduce_scatter | solution.py:207
  54.5 217.6 %reduce-scatter.3.cloned.1.call-start = ((), (), s32[]{:S(2)}) async-start(), calls=%async_computation.2 | async-start | bytes 7864320 | tf_op jit(solution)/shard_map/reduce_scatter | solution.py:204
  57.7 14.4 %collective-permute-start.5 = (bf16[128,512]{0,1:T(8,128)(2,1)S(1)}, bf16[128,512]{0,1:T(8,128)(2,1)S(1)}, u32[]{:S(2)}, u32[]{:S(2)}) collective-permute-start(bf16[128,512]{0,1:T(8,128)(2,1)S(1)} %copy.98), channel_id=1, source_target_pairs={{12,0},{0,4},{4,8},{8,12},{13,1},{1,5},{5,9},{9,13},{14,2},{2,6},{... | collective-permute-start | bytes 393224 | tf_op jit(solution)/shard_map/while/body/eval_jaxpr/ppermute | solution.py:19
  58.6 13.4 %collective-permute-start.6 = (bf16[128,512]{0,1:T(8,128)(2,1)S(1)}, bf16[128,512]{0,1:T(8,128)(2,1)}, u32[]{:S(2)}, u32[]{:S(2)}) collective-permute-start(bf16[128,512]{0,1:T(8,128)(2,1)S(1)} %copy.99), channel_id=1, source_target_pairs={{12,0},{0,4},{4,8},{8,12},{13,1},{1,5},{5,9},{9,13},{14,2},{2,6},{... | collective-permute-start | bytes 393224 | tf_op jit(solution)/shard_map/while/body/eval_jaxpr/ppermute | solution.py:19
  60.5 9.1 %collective-permute-start.7 = (bf16[1,16]{1,0:T(2,128)(2,1)}, bf16[1,16]{1,0:T(2,128)(2,1)}, u32[]{:S(2)}, u32[]{:S(2)}) collective-permute-start(bf16[1,16]{1,0:T(2,128)(2,1)} %copy.100), channel_id=1, source_target_pairs={{12,0},{0,4},{4,8},{8,12},{13,1},{1,5},{5,9},{9,13},{14,2},{2,6},{... | collective-permute-start | bytes 104 | tf_op jit(solution)/shard_map/while/body/eval_jaxpr/ppermute | solution.py:19
  60.5 11.5 %collective-permute-start.8 = (f32[4,128]{1,0:T(4,128)S(1)}, f32[4,128]{1,0:T(4,128)S(1)}, u32[]{:S(2)}, u32[]{:S(2)}) collective-permute-start(f32[4,128]{1,0:T(4,128)S(1)} %copy.101), channel_id=1, source_target_pairs={{12,0},{0,4},{4,8},{8,12},{13,1},{1,5},{5,9},{9,13},{14,2},{2,6},{... | collective-permute-start | bytes 6152 | tf_op jit(solution)/shard_map/while/body/eval_jaxpr/ppermute | solution.py:19
  62.1 9.9 %collective-permute-start.9 = (f32[4,128]{1,0:T(4,128)S(1)}, f32[4,128]{1,0:T(4,128)S(1)}, u32[]{:S(2)}, u32[]{:S(2)}) collective-permute-start(f32[4,128]{1,0:T(4,128)S(1)} %copy.102), channel_id=1, source_target_pairs={{12,0},{0,4},{4,8},{8,12},{13,1},{1,5},{5,9},{9,13},{14,2},{2,6},{... | collective-permute-start | bytes 6152 | tf_op jit(solution)/shard_map/while/body/eval_jaxpr/ppermute | solution.py:19
  69.6 9.3 %collective-permute-start.10 = (f32[128,512]{0,1:T(8,128)}, f32[128,512]{0,1:T(8,128)}, u32[]{:S(2)}, u32[]{:S(2)}) collective-permute-start(f32[128,512]{0,1:T(8,128)} %bitcast_add_fusion.5), channel_id=1, source_target_pairs={{12,0},{0,4},{4,8},{8,12},{13,1},{1,5},{5,9},{9,13},{14,2},{2,6},{... | collective-permute-start | bytes 786440 | tf_op jit(solution)/shard_map/while/body/eval_jaxpr/ppermute | solution.py:19
  78.9 15.2 %collective-permute-start.5 = (bf16[128,512]{0,1:T(8,128)(2,1)S(1)}, bf16[128,512]{0,1:T(8,128)(2,1)S(1)}, u32[]{:S(2)}, u32[]{:S(2)}) collective-permute-start(bf16[128,512]{0,1:T(8,128)(2,1)S(1)} %copy.98), channel_id=1, source_target_pairs={{12,0},{0,4},{4,8},{8,12},{13,1},{1,5},{5,9},{9,13},{14,2},{2,6},{... | collective-permute-start | bytes 393224 | tf_op jit(solution)/shard_map/while/body/eval_jaxpr/ppermute | solution.py:19
  79.9 14.2 %collective-permute-start.6 = (bf16[128,512]{0,1:T(8,128)(2,1)S(1)}, bf16[128,512]{0,1:T(8,128)(2,1)}, u32[]{:S(2)}, u32[]{:S(2)}) collective-permute-start(bf16[128,512]{0,1:T(8,128)(2,1)S(1)} %copy.99), channel_id=1, source_target_pairs={{12,0},{0,4},{4,8},{8,12},{13,1},{1,5},{5,9},{9,13},{14,2},{2,6},{... | collective-permute-start | bytes 393224 | tf_op jit(solution)/shard_map/while/body/eval_jaxpr/ppermute | solution.py:19
  81.2 9.5 %collective-permute-start.7 = (bf16[1,16]{1,0:T(2,128)(2,1)}, bf16[1,16]{1,0:T(2,128)(2,1)}, u32[]{:S(2)}, u32[]{:S(2)}) collective-permute-start(bf16[1,16]{1,0:T(2,128)(2,1)} %copy.100), channel_id=1, source_target_pairs={{12,0},{0,4},{4,8},{8,12},{13,1},{1,5},{5,9},{9,13},{14,2},{2,6},{... | collective-permute-start | bytes 104 | tf_op jit(solution)/shard_map/while/body/eval_jaxpr/ppermute | solution.py:19
  81.2 12.9 %collective-permute-start.8 = (f32[4,128]{1,0:T(4,128)S(1)}, f32[4,128]{1,0:T(4,128)S(1)}, u32[]{:S(2)}, u32[]{:S(2)}) collective-permute-start(f32[4,128]{1,0:T(4,128)S(1)} %copy.101), channel_id=1, source_target_pairs={{12,0},{0,4},{4,8},{8,12},{13,1},{1,5},{5,9},{9,13},{14,2},{2,6},{... | collective-permute-start | bytes 6152 | tf_op jit(solution)/shard_map/while/body/eval_jaxpr/ppermute | solution.py:19
  83.4 10.7 %collective-permute-start.9 = (f32[4,128]{1,0:T(4,128)S(1)}, f32[4,128]{1,0:T(4,128)S(1)}, u32[]{:S(2)}, u32[]{:S(2)}) collective-permute-start(f32[4,128]{1,0:T(4,128)S(1)} %copy.102), channel_id=1, source_target_pairs={{12,0},{0,4},{4,8},{8,12},{13,1},{1,5},{5,9},{9,13},{14,2},{2,6},{... | collective-permute-start | bytes 6152 | tf_op jit(solution)/shard_map/while/body/eval_jaxpr/ppermute | solution.py:19
  96.8 15.2 %collective-permute-start.5 = (bf16[128,512]{0,1:T(8,128)(2,1)S(1)}, bf16[128,512]{0,1:T(8,128)(2,1)S(1)}, u32[]{:S(2)}, u32[]{:S(2)}) collective-permute-start(bf16[128,512]{0,1:T(8,128)(2,1)S(1)} %copy.98), channel_id=1, source_target_pairs={{12,0},{0,4},{4,8},{8,12},{13,1},{1,5},{5,9},{9,13},{14,2},{2,6},{... | collective-permute-start | bytes 393224 | tf_op jit(solution)/shard_map/while/body/eval_jaxpr/ppermute | solution.py:19
  97.8 14.2 %collective-permute-start.6 = (bf16[128,512]{0,1:T(8,128)(2,1)S(1)}, bf16[128,512]{0,1:T(8,128)(2,1)}, u32[]{:S(2)}, u32[]{:S(2)}) collective-permute-start(bf16[128,512]{0,1:T(8,128)(2,1)S(1)} %copy.99), channel_id=1, source_target_pairs={{12,0},{0,4},{4,8},{8,12},{13,1},{1,5},{5,9},{9,13},{14,2},{2,6},{... | collective-permute-start | bytes 393224 | tf_op jit(solution)/shard_map/while/body/eval_jaxpr/ppermute | solution.py:19
  99.1 9.5 %collective-permute-start.7 = (bf16[1,16]{1,0:T(2,128)(2,1)}, bf16[1,16]{1,0:T(2,128)(2,1)}, u32[]{:S(2)}, u32[]{:S(2)}) collective-permute-start(bf16[1,16]{1,0:T(2,128)(2,1)} %copy.100), channel_id=1, source_target_pairs={{12,0},{0,4},{4,8},{8,12},{13,1},{1,5},{5,9},{9,13},{14,2},{2,6},{... | collective-permute-start | bytes 104 | tf_op jit(solution)/shard_map/while/body/eval_jaxpr/ppermute | solution.py:19
  99.1 12.9 %collective-permute-start.8 = (f32[4,128]{1,0:T(4,128)S(1)}, f32[4,128]{1,0:T(4,128)S(1)}, u32[]{:S(2)}, u32[]{:S(2)}) collective-permute-start(f32[4,128]{1,0:T(4,128)S(1)} %copy.101), channel_id=1, source_target_pairs={{12,0},{0,4},{4,8},{8,12},{13,1},{1,5},{5,9},{9,13},{14,2},{2,6},{... | collective-permute-start | bytes 6152 | tf_op jit(solution)/shard_map/while/body/eval_jaxpr/ppermute | solution.py:19
  101.3 10.7 %collective-permute-start.9 = (f32[4,128]{1,0:T(4,128)S(1)}, f32[4,128]{1,0:T(4,128)S(1)}, u32[]{:S(2)}, u32[]{:S(2)}) collective-permute-start(f32[4,128]{1,0:T(4,128)S(1)} %copy.102), channel_id=1, source_target_pairs={{12,0},{0,4},{4,8},{8,12},{13,1},{1,5},{5,9},{9,13},{14,2},{2,6},{... | collective-permute-start | bytes 6152 | tf_op jit(solution)/shard_map/while/body/eval_jaxpr/ppermute | solution.py:19
  114.7 15.2 %collective-permute-start.5 = (bf16[128,512]{0,1:T(8,128)(2,1)S(1)}, bf16[128,512]{0,1:T(8,128)(2,1)S(1)}, u32[]{:S(2)}, u32[]{:S(2)}) collective-permute-start(bf16[128,512]{0,1:T(8,128)(2,1)S(1)} %copy.98), channel_id=1, source_target_pairs={{12,0},{0,4},{4,8},{8,12},{13,1},{1,5},{5,9},{9,13},{14,2},{2,6},{... | collective-permute-start | bytes 393224 | tf_op jit(solution)/shard_map/while/body/eval_jaxpr/ppermute | solution.py:19
  115.7 14.2 %collective-permute-start.6 = (bf16[128,512]{0,1:T(8,128)(2,1)S(1)}, bf16[128,512]{0,1:T(8,128)(2,1)}, u32[]{:S(2)}, u32[]{:S(2)}) collective-permute-start(bf16[128,512]{0,1:T(8,128)(2,1)S(1)} %copy.99), channel_id=1, source_target_pairs={{12,0},{0,4},{4,8},{8,12},{13,1},{1,5},{5,9},{9,13},{14,2},{2,6},{... | collective-permute-start | bytes 393224 | tf_op jit(solution)/shard_map/while/body/eval_jaxpr/ppermute | solution.py:19
  117.0 9.5 %collective-permute-start.7 = (bf16[1,16]{1,0:T(2,128)(2,1)}, bf16[1,16]{1,0:T(2,128)(2,1)}, u32[]{:S(2)}, u32[]{:S(2)}) collective-permute-start(bf16[1,16]{1,0:T(2,128)(2,1)} %copy.100), channel_id=1, source_target_pairs={{12,0},{0,4},{4,8},{8,12},{13,1},{1,5},{5,9},{9,13},{14,2},{2,6},{... | collective-permute-start | bytes 104 | tf_op jit(solution)/shard_map/while/body/eval_jaxpr/ppermute | solution.py:19
  117.0 12.9 %collective-permute-start.8 = (f32[4,128]{1,0:T(4,128)S(1)}, f32[4,128]{1,0:T(4,128)S(1)}, u32[]{:S(2)}, u32[]{:S(2)}) collective-permute-start(f32[4,128]{1,0:T(4,128)S(1)} %copy.101), channel_id=1, source_target_pairs={{12,0},{0,4},{4,8},{8,12},{13,1},{1,5},{5,9},{9,13},{14,2},{2,6},{... | collective-permute-start | bytes 6152 | tf_op jit(solution)/shard_map/while/body/eval_jaxpr/ppermute | solution.py:19
  119.2 10.7 %collective-permute-start.9 = (f32[4,128]{1,0:T(4,128)S(1)}, f32[4,128]{1,0:T(4,128)S(1)}, u32[]{:S(2)}, u32[]{:S(2)}) collective-permute-start(f32[4,128]{1,0:T(4,128)S(1)} %copy.102), channel_id=1, source_target_pairs={{12,0},{0,4},{4,8},{8,12},{13,1},{1,5},{5,9},{9,13},{14,2},{2,6},{... | collective-permute-start | bytes 6152 | tf_op jit(solution)/shard_map/while/body/eval_jaxpr/ppermute | solution.py:19
  212.0 149.0 %all-reduce.5.cloned.1.call-start = ((), (), s32[]{:S(2)}) async-start(), calls=%async_computation.4 | async-start | bytes 4194304 | tf_op jit(solution)/shard_map/psum | solution.py:215
  (32 other events, 295.1 us)
Sparse Core Ops, SparseCore 0:
  54.6 35.6 reduce-scatter.4
  212.1 59.9 reduce-scatter.2
  274.6 86.3 all-reduce.4
where the time goes:
time: 376 us; the launch traced here: 371 us
  waiting for transfers between devices  174 us (46%)
  blocking collectives  73.3 us (19%)
  matrix products  43.4 us (12%)
  other arithmetic  25.4 us (7%)
  local copies, waits for them, and re-layouts  20.3 us (5%)
  starting transfers between devices  20.1 us (5%)
  between operations  14.6 us (4%)
    psum x1, waiting for transfers between devices, body(): w_in_grad, w_out_grad = lax.psum((w_in_part, w_out_part), 'stand')  81.4 us
    psum x1, blocking collectives, body(): grad_key, grad_value = lax.psum((grad_key, grad_value), 'stand')  73.3 us
    reduce_scatter x1, waiting for transfers between devices, body(): lax.psum_scatter(jnp.concatenate([query_part, key_part], axis=1), 'soil',...  60 us
    ppermute x44, waiting for transfers between devices, from_behind(): return lax.ppermute(block, axis, route)  32.2 us
    ppermute x44, starting transfers between devices, from_behind(): return lax.ppermute(block, axis, route)  20 us
    add x4, other arithmetic, backward_tile(): grad_value = grad_value + value_step.reshape(key_count, HEADS * DH)  11.9 us
    while x24, local copies, waits for them, and re-layouts  8.69 us
    unnamed x26, local copies, waits for them, and re-layouts  8.11 us
  transfers between devices with their start and end apart: 47, of which 14 were waited for; matrix products, arithmetic and copies ran while one was open for 19% of the time, Pallas kernels for 0%

commit v1 on v0

--- a/solution.py
+++ b/solution.py
@@ -1,13 +1,401 @@
+import functools
 import math
 
 import jax
 import jax.numpy as jnp
 from jax import lax
+from jax.experimental import pallas as pl
+from jax.experimental.pallas import tpu as pltpu
 from jax.sharding import PartitionSpec as P
 
 HEADS = 4
 DH = 128
 BLOCK = 128
+MASK_ROWS = 16
+WIDTH = HEADS * DH
+F32 = jnp.float32
+BF16 = jnp.bfloat16
+NT = (((1,), (1,)), ((), ()))
+TN = (((0,), (0,)), ((), ()))
+NN = (((1,), (0,)), ((), ()))
+
+
+def mm(a, b, dims):
+    return lax.dot_general(a, b, dims, preferred_element_type=F32)
+
+
+def shape(rows, columns, dtype=BF16):
+    return jax.ShapeDtypeStruct((rows, columns), dtype)
+
+
+VMEM = pl.BlockSpec(memory_space=pltpu.VMEM)
+SMEM = pl.BlockSpec(memory_space=pltpu.SMEM)
+
+
+def columns_of(index, width):
+    return pl.ds(pl.multiple_of(index * width, width), width)
+
+
+def step_from(axis, distance):
+    size = lax.axis_size(axis)
+    return [((i - distance) % size, i) for i in range(size)]
+
+
+def sent(block, axis, distance):
+    return lax.ppermute(block, axis, step_from(axis, distance))
+
+
+def call(kernel, out_shape, in_specs, flops, traffic, scratch=(), grid_spec=None, limit=48):
+    options = dict(in_specs=in_specs, scratch_shapes=list(scratch)) if grid_spec is None else dict(grid_spec=grid_spec)
+    if grid_spec is None:
+        options["out_specs"] = jax.tree.map(lambda _: VMEM, out_shape)
+    return pl.pallas_call(
+        kernel,
+        out_shape=out_shape,
+        compiler_params=pltpu.CompilerParams(vmem_limit_bytes=limit << 20),
+        cost_estimate=pl.CostEstimate(flops=flops, bytes_accessed=traffic, transcendentals=0),
+        **options,
+    )
+
+
+def keys_kernel(place, tokens, w_key, w_value, kv):
+    kv[:, :DH] = mm(tokens[...], w_key[...], NN).astype(BF16)
+    kv[:, DH:] = mm(tokens[...], w_value[...], NN).astype(BF16)
+
+
+def project_keys(place, key_tokens, w_in):
+    rows, width = key_tokens.shape
+    return call(
+        keys_kernel,
+        shape(rows, 2 * DH),
+        None,
+        4 * rows * width * DH,
+        2 * (rows * width + 2 * width * DH + 2 * rows * DH),
+        grid_spec=pltpu.PrefetchScalarGridSpec(
+            num_scalar_prefetch=1,
+            grid=(1,),
+            in_specs=[
+                pl.BlockSpec((rows, width), lambda i, place: (0, 0)),
+                pl.BlockSpec((width, DH), lambda i, place: (0, HEADS + place[0])),
+                pl.BlockSpec((width, DH), lambda i, place: (0, 2 * HEADS + place[0])),
+            ],
+            out_specs=pl.BlockSpec((rows, 2 * DH), lambda i, place: (0, 0)),
+        ),
+    )(place, key_tokens, w_in, w_in)
+
+
+def queries_kernel(place, crossing, home, tokens, out_grad, w_in, w_out, *rest):
+    outs, (all_q, all_g) = rest[:HEADS], rest[HEADS:]
+    all_q[...] = mm(tokens[...], w_in[...], NN).astype(BF16)
+    all_g[...] = mm(out_grad[...], w_out[...], NT).astype(BF16)
+    lane = lax.broadcasted_iota(jnp.int32, (MASK_ROWS, 2 * DH), 1)
+    row = lax.broadcasted_iota(jnp.int32, (MASK_ROWS, 2 * DH), 0)
+    mask = jnp.zeros((MASK_ROWS, 2 * DH), F32)
+    for j in range(crossing.shape[1]):
+        bit = jnp.where((crossing[0, j] > 0) | (home[0] == j), 1.0, 0.0)
+        mask = jnp.where((lane == j) & (row == 0), bit, mask)
+    for d in range(HEADS):
+        head = columns_of(lax.rem(place[0] + d, HEADS), DH)
+        outs[d][:BLOCK, :DH] = all_q[:, head]
+        outs[d][:BLOCK, DH:] = all_g[:, head]
+        outs[d][BLOCK:, :] = mask.astype(BF16)
+
+
+def project_queries(place, query_tokens, out_grad, w_in, w_out, crossing, home):
+    rows, width = query_tokens.shape
+    whole = lambda *s: pl.BlockSpec(s, lambda i: (0, 0))
+    return pl.pallas_call(
+        queries_kernel,
+        out_shape=[shape(rows + MASK_ROWS, 2 * DH)] * HEADS,
+        grid=(1,),
+        in_specs=[
+            SMEM,
+            SMEM,
+            SMEM,
+            whole(rows, width),
+            whole(rows, width),
+            whole(width, WIDTH),
+            whole(WIDTH, width),
+        ],
+        out_specs=[whole(rows + MASK_ROWS, 2 * DH)] * HEADS,
+        scratch_shapes=[pltpu.VMEM((rows, WIDTH), BF16)] * 2,
+        compiler_params=pltpu.CompilerParams(vmem_limit_bytes=32 << 20),
+        cost_estimate=pl.CostEstimate(
+            flops=4 * rows * width * WIDTH,
+            bytes_accessed=4 * (rows * width + width * WIDTH + rows * WIDTH),
+            transcendentals=0,
+        ),
+    )(place, crossing, home, query_tokens, out_grad, w_in, w_out)
+
+
+def attention_kernel(place, *refs):
+    packs, refs = refs[:HEADS], refs[HEADS:]
+    kvs, refs = refs[:HEADS], refs[HEADS:]
+    grads, refs = refs[:HEADS], refs[HEADS:]
+    backs, (scores, bias, q_all, g_all) = refs[:HEADS], refs[HEADS:]
+    chunk = kvs[0].shape[0]
+    tiles = chunk // BLOCK
+    count = HEADS * BLOCK
+    scale = 1.0 / math.sqrt(DH)
+    ones = jnp.ones((MASK_ROWS, BLOCK), BF16)
+    for d in range(HEADS):
+        rows = slice(d * BLOCK, (d + 1) * BLOCK)
+        q_all[rows, :] = packs[d][:BLOCK, :DH]
+        g_all[rows, :] = packs[d][:BLOCK, DH:]
+        allowed = mm(packs[d][BLOCK:, :DH], ones, TN)
+        bias[:, rows] = (allowed - 1.0) * 1e30
+    q = q_all[...]
+    g = g_all[...]
+    best = jnp.full((1, count), -3e38, F32)
+    for c in range(HEADS):
+        soil = lax.rem(place[1] - c + HEADS, HEADS)
+        raw = mm(kvs[c][:, :DH], q, NT) * scale
+        for j in range(tiles):
+            tile = raw[j * BLOCK : (j + 1) * BLOCK, :] + bias[pl.ds(soil * tiles + j, 1), :]
+            scores[c * chunk + j * BLOCK : c * chunk + (j + 1) * BLOCK, :] = tile
+            best = jnp.maximum(best, jnp.max(tile, axis=0, keepdims=True))
+    total = jnp.zeros((1, count), F32)
+    summed = jnp.zeros((DH, count), F32)
+    for c in range(HEADS):
+        part = slice(c * chunk, (c + 1) * chunk)
+        weights = jnp.exp(scores[part, :] - best)
+        scores[part, :] = weights
+        total = total + jnp.sum(weights, axis=0, keepdims=True)
+        summed = summed + mm(kvs[c][:, DH:], weights.astype(BF16), TN)
+    share = 1.0 / total
+    attended = (summed * share).astype(BF16)
+    spread = jnp.sum(jnp.transpose(g.astype(F32)) * attended.astype(F32), axis=0, keepdims=True)
+    flat = jnp.transpose(attended.astype(F32)).astype(BF16)
+    for d in range(HEADS):
+        backs[d][:, :DH] = flat[d * BLOCK : (d + 1) * BLOCK, :]
+    query_sum = jnp.zeros((DH, count), F32)
+    for c in range(HEADS):
+        part = slice(c * chunk, (c + 1) * chunk)
+        probs = scores[part, :] * share
+        grad_probs = mm(kvs[c][:, DH:], g, NT)
+        slope = (probs * (grad_probs - spread)).astype(BF16)
+        grads[c][:, :DH] = (mm(slope, q, NN) * scale).astype(grads[c].dtype)
+        grads[c][:, DH:] = mm(probs.astype(BF16), g, NN).astype(grads[c].dtype)
+        query_sum = query_sum + mm(kvs[c][:, :DH], slope, TN)
+    flat = (jnp.transpose(query_sum) * scale).astype(BF16)
+    for d in range(HEADS):
+        backs[d][:, DH:] = flat[d * BLOCK : (d + 1) * BLOCK, :]
+
+
+def attention(place, packs, kvs):
+    chunk = kvs[0].shape[0]
+    count = HEADS * BLOCK
+    keys = HEADS * chunk
+    out = [shape(chunk, 2 * DH, F32)] + [shape(chunk, 2 * DH)] * (HEADS - 1) + [shape(BLOCK, 2 * DH)] * HEADS
+    return call(
+        attention_kernel,
+        out,
+        [SMEM] + [VMEM] * (2 * HEADS),
+        12 * keys * count * DH,
+        8 * keys * 2 * DH,
+        scratch=[
+            pltpu.VMEM((keys, count), F32),
+            pltpu.VMEM((BLOCK, count), F32),
+            pltpu.VMEM((count, DH), BF16),
+            pltpu.VMEM((count, DH), BF16),
+        ],
+    )(place, *packs, *kvs)
+
+
+def query_weights_kernel(place, *refs):
+    tokens, refs = refs[:HEADS], refs[HEADS:]
+    grads, refs = refs[:HEADS], refs[HEADS:]
+    backs, refs = refs[:HEADS], refs[HEADS:]
+    outs, (whole,) = refs[:HEADS], refs[HEADS:]
+    for half, (left, part) in enumerate(((tokens, slice(DH, 2 * DH)), (grads, slice(0, DH)))):
+        term = mm(left[0][...], backs[0][:, part], TN)
+        for d in range(1, HEADS):
+            term = term + mm(left[d][...], backs[d][:, part], TN)
+        whole[:, half * DH : (half + 1) * DH] = term
+    rows = whole.shape[0] // HEADS
+    for d in range(HEADS):
+        outs[d][...] = whole[columns_of(lax.rem(place[1] + d, HEADS), rows), :].astype(outs[d].dtype)
+
+
+def query_weights(place, tokens, grads, backs):
+    width = tokens[0].shape[1]
+    rows = width // HEADS
+    return call(
+        query_weights_kernel,
+        [shape(rows, 2 * DH, F32)] + [shape(rows, 2 * DH)] * (HEADS - 1),
+        [SMEM] + [VMEM] * (3 * HEADS),
+        4 * HEADS * BLOCK * width * DH,
+        4 * HEADS * BLOCK * width + 4 * width * DH,
+        scratch=[pltpu.VMEM((width, 2 * DH), F32)],
+    )(place, *tokens, *grads, *backs)
+
+
+def sum_kernel(own, *rest):
+    total = own[...]
+    for other in rest[: HEADS - 1]:
+        total = total + other[...].astype(F32)
+    outs = rest[HEADS - 1 :]
+    width = total.shape[1] // len(outs)
+    for i, out in enumerate(outs):
+        out[...] = total[:, i * width : (i + 1) * width].astype(BF16)
+
+
+def sum_parts(parts, pieces):
+    rows, width = parts[0].shape
+    return call(
+        sum_kernel,
+        [shape(rows, width // pieces)] * pieces,
+        [VMEM] * HEADS,
+        rows * width * HEADS,
+        12 * rows * width,
+    )(*parts)
+
+
+def key_weights_kernel(place, tokens, own, *rest):
+    others, grad, outs, whole = rest[: HEADS - 1], rest[HEADS - 1], rest[HEADS:-1], rest[-1]
+    total = own[...]
+    for other in others:
+        total = total + other[...].astype(F32)
+    rounded = total.astype(BF16)
+    grad[...] = rounded
+    whole[...] = mm(tokens[...], rounded, TN)
+    rows = whole.shape[0] // HEADS
+    for d in range(HEADS):
+        outs[d][...] = whole[columns_of(lax.rem(place[1] + d, HEADS), rows), :].astype(outs[d].dtype)
+
+
+def key_weights(place, key_tokens, parts):
+    count, width = key_tokens.shape
+    rows = width // HEADS
+    return call(
+        key_weights_kernel,
+        [shape(count, 2 * DH), shape(rows, 2 * DH, F32)] + [shape(rows, 2 * DH)] * (HEADS - 1),
+        [SMEM] + [VMEM] * (HEADS + 1),
+        4 * count * width * DH,
+        2 * count * width + 10 * count * 2 * DH,
+        scratch=[pltpu.VMEM((width, 2 * DH), F32)],
+    )(place, key_tokens, *parts)
+
+
+def query_out_kernel(place, *refs):
+    backs, refs = refs[:HEADS], refs[HEADS:]
+    w_in, w_out, output, query_grad, att, grad = refs
+    for d in range(HEADS):
+        head = columns_of(lax.rem(place[0] + d, HEADS), DH)
+        att[:, head] = backs[d][:, :DH]
+        grad[:, head] = backs[d][:, DH:]
+    output[...] = mm(att[...], w_out[...], NN).astype(BF16)
+    query_grad[...] = mm(grad[...], w_in[...], NT).astype(BF16)
+
+
+def query_outputs(place, backs, w_in, w_out):
+    width = w_in.shape[0]
+    whole = lambda *s: pl.BlockSpec(s, lambda i: (0, 0))
+    return pl.pallas_call(
+        query_out_kernel,
+        out_shape=[shape(BLOCK, width)] * 2,
+        grid=(1,),
+        in_specs=[SMEM] + [whole(BLOCK, 2 * DH)] * HEADS + [whole(width, WIDTH), whole(WIDTH, width)],
+        out_specs=[whole(BLOCK, width)] * 2,
+        scratch_shapes=[pltpu.VMEM((BLOCK, WIDTH), BF16)] * 2,
+        compiler_params=pltpu.CompilerParams(vmem_limit_bytes=32 << 20),
+        cost_estimate=pl.CostEstimate(
+            flops=4 * BLOCK * width * WIDTH,
+            bytes_accessed=4 * (BLOCK * width + width * WIDTH + BLOCK * WIDTH),
+            transcendentals=0,
+        ),
+    )(place, *backs, w_in, w_out)
+
+
+def key_out_kernel(place, *refs):
+    parts, refs = refs[:HEADS], refs[HEADS:]
+    w_key, w_value, out, keys, values = refs
+    for d in range(HEADS):
+        head = columns_of(lax.rem(place[0] - d + HEADS, HEADS), DH)
+        keys[:, head] = parts[d][:, :DH]
+        values[:, head] = parts[d][:, DH:]
+    out[...] = (mm(keys[...], w_key[...], NT) + mm(values[...], w_value[...], NT)).astype(BF16)
+
+
+def key_output(place, parts, w_in):
+    count = parts[0].shape[0]
+    width = w_in.shape[0]
+    at = lambda column, *s: pl.BlockSpec(s, lambda i: (0, column))
+    return pl.pallas_call(
+        key_out_kernel,
+        out_shape=shape(count, width),
+        grid=(1,),
+        in_specs=[SMEM] + [at(0, count, 2 * DH)] * HEADS + [at(1, width, WIDTH), at(2, width, WIDTH)],
+        out_specs=at(0, count, width),
+        scratch_shapes=[pltpu.VMEM((count, WIDTH), BF16)] * 2,
+        compiler_params=pltpu.CompilerParams(vmem_limit_bytes=48 << 20),
+        cost_estimate=pl.CostEstimate(
+            flops=4 * count * width * WIDTH,
+            bytes_accessed=4 * (count * width + width * WIDTH + count * WIDTH),
+            transcendentals=0,
+        ),
+    )(place, *parts, w_in, w_in)
+
+
+def place_weights_kernel(place, *refs):
+    queries, refs = refs[:HEADS], refs[HEADS:]
+    keys, refs = refs[:HEADS], refs[HEADS:]
+    outs, refs = refs[:HEADS], refs[HEADS:]
+    w_in_grad, w_out_grad = refs
+    rows = outs[0].shape[0]
+    for d in range(HEADS):
+        head = lax.rem(place[0] - d + HEADS, HEADS)
+        w_in_grad[:, columns_of(head, DH)] = queries[d][...].astype(F32)
+        w_in_grad[:, columns_of(HEADS + head, DH)] = keys[d][:, :DH].astype(F32)
+        w_in_grad[:, columns_of(2 * HEADS + head, DH)] = keys[d][:, DH:].astype(F32)
+        w_out_grad[:, columns_of(head, rows)] = jnp.transpose(outs[d][...].astype(F32))
+
+
+def place_weights(place, queries, keys, outs):
+    rows = queries[0].shape[0]
+    return call(
+        place_weights_kernel,
+        [shape(rows, 3 * WIDTH, F32), shape(DH, HEADS * rows, F32)],
+        [SMEM] + [VMEM] * (3 * HEADS),
+        rows * 4 * WIDTH,
+        6 * rows * 4 * WIDTH,
+    )(place, *queries, *keys, *outs)
+
+
+def head_body(query_tokens, key_tokens, w_in, w_out, out_grad, crossing, home):
+    place = jnp.stack([lax.axis_index("stand"), lax.axis_index("soil")]).astype(jnp.int32)
+    distances = range(1, HEADS)
+    kv = project_keys(place, key_tokens, w_in)
+    kvs = [kv] + [sent(kv, "soil", d) for d in distances]
+    packs = project_queries(place, query_tokens, out_grad, w_in, w_out, crossing, home)
+    packs = [packs[0]] + [sent(packs[d], "stand", d) for d in distances]
+    tokens = [query_tokens] + [sent(query_tokens, "stand", d) for d in distances]
+    grads = [out_grad] + [sent(out_grad, "stand", d) for d in distances]
+    results = attention(place, packs, kvs)
+    key_parts, backs = results[:HEADS], results[HEADS:]
+    key_parts = [key_parts[0]] + [sent(key_parts[d], "soil", HEADS - d) for d in distances]
+    query_parts = query_weights(place, tokens, grads, backs)
+    backs = [backs[0]] + [sent(backs[d], "stand", HEADS - d) for d in distances]
+    query_parts = [query_parts[0]] + [sent(query_parts[d], "soil", d) for d in distances]
+    key_grad_own, *key_weight_parts = key_weights(place, key_tokens, key_parts)
+    key_grads = [key_grad_own] + [sent(key_grad_own, "stand", d) for d in distances]
+    key_weight_parts = [key_weight_parts[0]] + [sent(key_weight_parts[d], "soil", d) for d in distances]
+    output, query_grad = query_outputs(place, backs, w_in, w_out)
+    query_weight, out_weight = sum_parts(query_parts, 2)
+    (key_weight,) = sum_parts(key_weight_parts, 1)
+    query_all = [query_weight] + [sent(query_weight, "stand", d) for d in distances]
+    key_all = [key_weight] + [sent(key_weight, "stand", d) for d in distances]
+    crosswise = []
+    for d in range(HEADS):
+        route = [
+            (soil * HEADS + stand, stand * HEADS + (soil + d) % HEADS)
+            for stand in range(HEADS)
+            for soil in range(HEADS)
+        ]
+        crosswise.append(lax.ppermute(out_weight, ("soil", "stand"), route))
+    key_grad = key_output(place, key_grads, w_in)
+    w_in_grad, w_out_grad = place_weights(place, query_all, key_all, crosswise)
+    return (output, query_grad, key_grad, w_in_grad, w_out_grad)
 
 
 NEG = -1e30
@@ -94,7 +482,7 @@
     return (grad_query, grad_key, grad_value)
 
 
-def body(query_tokens, key_tokens, w_in, w_out, out_grad, crossing, home):
+def ring_body(query_tokens, key_tokens, w_in, w_out, out_grad, crossing, home):
     attn_width = HEADS * DH
     query_count = query_tokens.shape[0]
     key_count = key_tokens.shape[0]
@@ -233,4 +621,6 @@
         P(("field", "soil"), None),
         P(("field", "soil"), None),
     )
+    square = mesh.shape["stand"] == HEADS and mesh.shape["soil"] == HEADS
+    body = head_body if square else ring_body
     return jax.shard_map(body, mesh=mesh, in_specs=in_specs, out_specs=out_specs, check_vma=False)

time: 376 us -> 137 us (0.36)
  waiting for transfers between devices: 174 us -> 68.4 us
  blocking collectives: 73.3 us -> 0 us
  matrix products: 43.4 us -> 0 us
  other arithmetic: 25.4 us -> 0.08 us
  starting transfers between devices: 20.1 us -> 42.5 us
  Pallas kernels: 0 us -> 16.8 us
  local copies, waits for them, and re-layouts: 20.3 us -> 5.69 us
  between operations: 14.6 us -> 1.46 us
    psum x1 -> x0, waiting for transfers between devices: 81.4 us -> none  [body(): w_in_grad, w_out_grad = lax.psum((w_in_part, w_out_part), 'stand')]
    psum x1 -> x0, blocking collectives: 73.3 us -> none  [body(): grad_key, grad_value = lax.psum((grad_key, grad_value), 'stand')]
    reduce_scatter x2 -> x0, waiting for transfers between devices: 60 us -> none  [the longest x1 60 us: body(): lax.psum_scatter(jnp.concatenate([query_part, key_part], axis=1), 'soil',...]
    dot_general x45 -> x0, matrix products: 43.4 us -> none  [the longest x4 5.85 us: backward_tile(): jnp.einsum('qhd,khd->hqk', query_heads, key_heads, preferred_element_type...]
    ppermute x44 -> x37, waiting for transfers between devices: 32.2 us -> 68.4 us  [the longest x33 55.3 us: sent(): return lax.ppermute(block, axis, step_from(axis, distance))]
    ppermute x44 -> x37, starting transfers between devices: 20 us -> 42.5 us  [the longest x33 38.1 us: sent(): return lax.ppermute(block, axis, step_from(axis, distance))]
    add x13 -> x0, other arithmetic: 18.6 us -> none  [the longest x4 11.9 us: backward_tile(): grad_value = grad_value + value_step.reshape(key_count, HEADS * DH)]
    pallas_call x0 -> x10, Pallas kernels: none -> 16.8 us  [the longest x1 4.57 us: attention(): call(attention_kernel, out, [SMEM] + [VMEM] * (2 * HEADS), 12 * keys * co...]
  transfers between devices with their start and end apart: 47 -> 37, of which waited for: 14 -> 16; matrix products, arithmetic and copies ran while one was open for 19% -> 0% of each run, Pallas kernels for 0% -> 10%
where the time goes in v1:
time: 137 us; the launch traced here: 135 us
  waiting for transfers between devices  68.4 us (50%)
  starting transfers between devices  42.5 us (31%)
  Pallas kernels  16.8 us (12%)
  local copies, waits for them, and re-layouts  5.69 us (4%)
  between operations  1.46 us (1%)
    ppermute x33, waiting for transfers between devices, sent(): return lax.ppermute(block, axis, step_from(axis, distance))  55.3 us
    ppermute x33, starting transfers between devices, sent(): return lax.ppermute(block, axis, step_from(axis, distance))  38.1 us
    ppermute x4, waiting for transfers between devices, head_body(): crosswise.append(lax.ppermute(out_weight, ('soil', 'stand'), route))  13.1 us
    unnamed x20, local copies, waits for them, and re-layouts  5.69 us
    pallas_call x1, Pallas kernels, attention(): call(attention_kernel, out, [SMEM] + [VMEM] * (2 * HEADS), 12 * keys * co...  4.57 us
    ppermute x4, starting transfers between devices, head_body(): crosswise.append(lax.ppermute(out_weight, ('soil', 'stand'), route))  4.43 us
    pallas_call x1, Pallas kernels, key_output(): pl.pallas_call(key_out_kernel, out_shape=shape(count, width), grid=(1,),...  2.89 us
  transfers between devices with their start and end apart: 37, of which 16 were waited for; matrix products, arithmetic and copies ran while one was open for 0% of the time, Pallas kernels for 10%

profile of v1, /device:TPU:14, one launch (start us, length us, event | category | flops | bytes accessed | tf_op | source)
XLA Modules:
  0.0 134.9 jit_solution(10039354347167018295)
XLA Ops:
  1.4 1.9 %copy-done = bf16[1024,1536]{1,0:T(8,128)(2,1)S(1)} copy-done((bf16[1024,1536]{1,0:T(8,128)(2,1)S(1)}, bf16[1024,1536]{1,0:T(8,128)(2,1)}, u32[]{:S(2)}) %copy-start) | copy-done | bytes 3145752
  16.1 7.8 %collective-permute-done.1.refs_2_ = bf16[144,256]{1,0:T(8,128)(2,1)S(1)} collective-permute-done((bf16[144,256]{1,0:T(8,128)(2,1)S(1)}, bf16[144,256]{1,0:T(8,128)(2,1)S(1)}, u32[]{:S(2)}, u32[]{:S(2)}) %collective-permute-start.1) | collective-permute-done | bytes 73760 | tf_op jit(solution)/shard_map/ppermute | solution.py:45
  23.9 2.9 %collective-permute-start.2 = (bf16[144,256]{1,0:T(8,128)(2,1)S(1)}, bf16[144,256]{1,0:T(8,128)(2,1)S(1)}, u32[]{:S(2)}, u32[]{:S(2)}) collective-permute-start(bf16[144,256]{1,0:T(8,128)(2,1)S(1)} %get-tuple-element.35), channel_id=1, source_target_pairs={{1,0},{2,1},{3,2},{0,3},{5,4},{6,5},{7,6},{4,7},{9,8},{10,9},{11,1... | collective-permute-start | bytes 221192 | tf_op jit(solution)/shard_map/ppermute | solution.py:45
  26.8 2.0 %collective-permute-done.2.refs_3_ = bf16[144,256]{1,0:T(8,128)(2,1)S(1)} collective-permute-done((bf16[144,256]{1,0:T(8,128)(2,1)S(1)}, bf16[144,256]{1,0:T(8,128)(2,1)S(1)}, u32[]{:S(2)}, u32[]{:S(2)}) %collective-permute-start.2) | collective-permute-done | bytes 73760 | tf_op jit(solution)/shard_map/ppermute | solution.py:45
  28.8 4.4 %collective-permute-start.16 = (bf16[128,1024]{1,0:T(8,128)(2,1)S(1)}, bf16[128,1024]{1,0:T(8,128)(2,1)S(1)}, u32[]{:S(2)}, u32[]{:S(2)}) collective-permute-start(bf16[128,1024]{1,0:T(8,128)(2,1)S(1)} %copy-done.6), channel_id=1, source_target_pairs={{2,0},{3,1},{0,2},{1,3},{6,4},{7,5},{4,6},{5,7},{10,8},{11,9},{8,1... | collective-permute-start | bytes 786440 | tf_op jit(solution)/shard_map/ppermute | solution.py:45
  33.2 2.0 %collective-permute-start.18 = (bf16[128,1024]{1,0:T(8,128)(2,1)S(1)}, bf16[128,1024]{1,0:T(8,128)(2,1)S(1)}, u32[]{:S(2)}, u32[]{:S(2)}) collective-permute-start(bf16[128,1024]{1,0:T(8,128)(2,1)S(1)} %copy-done.8), channel_id=1, source_target_pairs={{3,0},{0,1},{1,2},{2,3},{7,4},{4,5},{5,6},{6,7},{11,8},{8,9},{9,10... | collective-permute-start | bytes 786440 | tf_op jit(solution)/shard_map/ppermute | solution.py:45
  37.0 4.6 %shard_map.112 = (f32[512,256]{1,0:T(8,128)S(1)}, bf16[512,256]{1,0:T(8,128)(2,1)S(1)}, bf16[512,256]{1,0:T(8,128)(2,1)S(1)}, bf16[512,256]{1,0:T(8,128)(2,1)S(1...) custom-call(s32[2]{0:T(128)S(1)} %pad_add_fusion.place, ...), custom_call_target="tpu_custom_call" | custom-call | flops 1610612736 | bytes 4194304 | tf_op jit(solution)/shard_map/pallas_call | solution.py:190
  41.6 7.1 %collective-permute-done.16.refs_2_ = bf16[128,1024]{1,0:T(8,128)(2,1)S(1)} collective-permute-done((bf16[128,1024]{1,0:T(8,128)(2,1)S(1)}, bf16[128,1024]{1,0:T(8,128)(2,1)S(1)}, u32[]{:S(2)}, u32[]{:S(2)}) %collective-permute-start.16) | collective-permute-done | bytes 262176 | tf_op jit(solution)/shard_map/ppermute | solution.py:45
  49.5 10.3 %collective-permute-done.17.refs_3_ = bf16[128,1024]{1,0:T(8,128)(2,1)S(1)} collective-permute-done((bf16[128,1024]{1,0:T(8,128)(2,1)S(1)}, bf16[128,1024]{1,0:T(8,128)(2,1)S(1)}, u32[]{:S(2)}, u32[]{:S(2)}) %collective-permute-start.17) | collective-permute-done | bytes 262176 | tf_op jit(solution)/shard_map/ppermute | solution.py:45
  59.8 3.9 %collective-permute-done.18.refs_5_ = bf16[128,1024]{1,0:T(8,128)(2,1)S(1)} collective-permute-done((bf16[128,1024]{1,0:T(8,128)(2,1)S(1)}, bf16[128,1024]{1,0:T(8,128)(2,1)S(1)}, u32[]{:S(2)}, u32[]{:S(2)}) %collective-permute-start.18) | collective-permute-done | bytes 262176 | tf_op jit(solution)/shard_map/ppermute | solution.py:45
  64.0 5.2 %collective-permute-done.19.refs_6_ = bf16[128,1024]{1,0:T(8,128)(2,1)S(1)} collective-permute-done((bf16[128,1024]{1,0:T(8,128)(2,1)S(1)}, bf16[128,1024]{1,0:T(8,128)(2,1)S(1)}, u32[]{:S(2)}, u32[]{:S(2)}) %collective-permute-start.19) | collective-permute-done | bytes 262176 | tf_op jit(solution)/shard_map/ppermute | solution.py:45
  81.1 2.2 %collective-permute-start.25 = (bf16[256,128]{1,0:T(8,128)(2,1)S(1)}, bf16[256,128]{1,0:T(8,128)(2,1)S(1)}, u32[]{:S(2)}, u32[]{:S(2)}) collective-permute-start(bf16[256,128]{1,0:T(8,128)(2,1)S(1)} %get-tuple-element.51.refs_0_), channel_id=1, source_target_pairs={{2,0},{3,1},{0,2},{1,3},{6,4},{7,5},{4,6},{5,7},{10,8},{11,9},{8,1... | collective-permute-start | bytes 196616 | tf_op jit(solution)/shard_map/ppermute | solution.py:45
  85.6 2.5 %collective-permute-start.13 = (bf16[512,256]{1,0:T(8,128)(2,1)S(1)}, bf16[512,256]{1,0:T(8,128)(2,1)S(1)}, u32[]{:S(2)}, u32[]{:S(2)}) collective-permute-start(bf16[512,256]{1,0:T(8,128)(2,1)S(1)} %get-tuple-element.46.refs_0_), channel_id=1, source_target_pairs={{2,0},{3,1},{0,2},{1,3},{6,4},{7,5},{4,6},{5,7},{10,8},{11,9},{8,1... | collective-permute-start | bytes 786440 | tf_op jit(solution)/shard_map/ppermute | solution.py:45
  90.5 11.2 %collective-permute-done.26.refs_3_ = bf16[256,128]{1,0:T(8,128)(2,1)S(1)} collective-permute-done((bf16[256,128]{1,0:T(8,128)(2,1)S(1)}, bf16[256,128]{1,0:T(8,128)(2,1)S(1)}, u32[]{:S(2)}, u32[]{:S(2)}) %collective-permute-start.26) | collective-permute-done | bytes 65568 | tf_op jit(solution)/shard_map/ppermute | solution.py:45
  103.1 4.0 %collective-permute-done.28.rest_1_ = bf16[256,256]{1,0:T(8,128)(2,1)S(1)} collective-permute-done((bf16[256,256]{1,0:T(8,128)(2,1)S(1)}, bf16[256,256]{1,0:T(8,128)(2,1)S(1)}, u32[]{:S(2)}, u32[]{:S(2)}) %collective-permute-start.28) | collective-permute-done | bytes 131104 | tf_op jit(solution)/shard_map/ppermute | solution.py:45
  107.2 1.9 %collective-permute-start.33 = (bf16[256,128]{1,0:T(8,128)(2,1)S(1)}, bf16[256,128]{1,0:T(8,128)(2,1)S(1)}, u32[]{:S(2)}, u32[]{:S(2)}) collective-permute-start(bf16[256,128]{1,0:T(8,128)(2,1)S(1)} %get-tuple-element.56), channel_id=1, source_target_pairs={{0,0},{4,1},{8,2},{12,3},{1,4},{5,5},{9,6},{13,7},{2,8},{6,9},{10,... | collective-permute-start | bytes 196616 | tf_op jit(solution)/shard_map/ppermute | solution.py:395
  109.1 2.4 %collective-permute-start.34 = (bf16[256,128]{1,0:T(8,128)(2,1)S(1)}, bf16[256,128]{1,0:T(8,128)(2,1)S(1)}, u32[]{:S(2)}, u32[]{:S(2)}) collective-permute-start(bf16[256,128]{1,0:T(8,128)(2,1)S(1)} %get-tuple-element.56), channel_id=1, source_target_pairs={{0,1},{4,2},{8,3},{12,0},{1,5},{5,6},{9,7},{13,4},{2,9},{6,10},{10... | collective-permute-start | bytes 196616 | tf_op jit(solution)/shard_map/ppermute | solution.py:395
  111.6 6.5 %collective-permute-done.33.refs_8_ = bf16[256,128]{1,0:T(8,128)(2,1)S(1)} collective-permute-done((bf16[256,128]{1,0:T(8,128)(2,1)S(1)}, bf16[256,128]{1,0:T(8,128)(2,1)S(1)}, u32[]{:S(2)}, u32[]{:S(2)}) %collective-permute-start.33) | collective-permute-done | bytes 65568 | tf_op jit(solution)/shard_map/ppermute | solution.py:395
  118.9 3.1 %collective-permute-start.31 = (bf16[256,256]{1,0:T(8,128)(2,1)S(1)}, bf16[256,256]{1,0:T(8,128)(2,1)S(1)}, u32[]{:S(2)}, u32[]{:S(2)}) collective-permute-start(bf16[256,256]{1,0:T(8,128)(2,1)S(1)} %shard_map.118.refs_4_), channel_id=1, source_target_pairs={{2,0},{3,1},{0,2},{1,3},{6,4},{7,5},{4,6},{5,7},{10,8},{11,9},{8,1... | collective-permute-start | bytes 393224 | tf_op jit(solution)/shard_map/ppermute | solution.py:45
  122.0 1.9 %shard_map.113 = (bf16[128,1024]{1,0:T(8,128)(2,1)}, bf16[128,1024]{1,0:T(8,128)(2,1)}) custom-call(s32[2]{0:T(128)S(1)} %pad_add_fusion.place, bf16[128,256]{1,0:T(8,128)(2,1)S(1)} %get-tuple-element.36.refs_0_.refs_8_, bf16[128,256]{1,0:T(8,128)(2,1)S(1)} %collective-permute-done.6.refs_1_, bf16[128,256]{1,0:T(8,128)(2,1)S(1)} %collective-permute-done.7.refs_2_, ...), custom_call_target="tpu_custom_call" | custom-call | flops 268435456 | bytes 2883584 | tf_op jit(solution)/shard_map/pallas_call | solution.py:294
  124.0 2.9 %shard_map.115 = bf16[512,1024]{1,0:T(8,128)(2,1)} custom-call(s32[2]{0:T(128)S(1)} %pad_add_fusion.place, bf16[512,256]{1,0:T(8,128)(2,1)S(1)} %get-tuple-element.46.refs_0_, bf16[512,256]{1,0:T(8,128)(2,1)S(1)} %collective-permute-done.12.refs_1_, bf16[512,256]{1,0:T(8,128)(2,1)S(1)} %collective-permute-done.13.refs_2_, ...), custom_call_target="tpu_custom_call" | custom-call | flops 1073741824 | bytes 5242880 | tf_op jit(solution)/shard_map/pallas_call | solution.py:324
  126.9 2.4 %collective-permute-done.35.refs_10_ = bf16[256,128]{1,0:T(8,128)(2,1)S(1)} collective-permute-done((bf16[256,128]{1,0:T(8,128)(2,1)S(1)}, bf16[256,128]{1,0:T(8,128)(2,1)S(1)}, u32[]{:S(2)}, u32[]{:S(2)}) %collective-permute-start.35) | collective-permute-done | bytes 65568 | tf_op jit(solution)/shard_map/ppermute | solution.py:395
  129.3 3.4 %collective-permute-done.36.refs_11_ = bf16[256,128]{1,0:T(8,128)(2,1)S(1)} collective-permute-done((bf16[256,128]{1,0:T(8,128)(2,1)S(1)}, bf16[256,128]{1,0:T(8,128)(2,1)S(1)}, u32[]{:S(2)}, u32[]{:S(2)}) %collective-permute-start.36) | collective-permute-done | bytes 65568 | tf_op jit(solution)/shard_map/ppermute | solution.py:395
  132.8 2.1 %shard_map.119 = (f32[256,1536]{1,0:T(8,128)}, f32[128,1024]{1,0:T(8,128)}) custom-call(s32[2]{0:T(128)S(1)} %pad_add_fusion.place, bf16[256,128]{1,0:T(8,128)(2,1)S(1)} %get-tuple-element.51.refs_0_, bf16[256,128]{1,0:T(8,128)(2,1)S(1)} %collective-permute-done.24.refs_1_, bf16[256,128]{1,0:T(8,128)(2,1)S(1)} %collective-permute-done.25.refs_2_, ...), custom_call_target="tpu_custom_call" | custom-call | flops 524288 | bytes 3145728 | tf_op jit(solution)/shard_map/pallas_call | solution.py:356
  (81 shorter events, 34.7 us)
Async XLA Ops:
  11.3 21.9 %collective-permute-start.3 = (bf16[512,256]{1,0:T(8,128)(2,1)S(1)}, bf16[512,256]{1,0:T(8,128)(2,1)S(1)}, u32[]{:S(2)}, u32[]{:S(2)}) collective-permute-start(bf16[512,256]{1,0:T(8,128)(2,1)S(1)} %shard_map.111.refs_4_), channel_id=1, source_target_pairs={{12,0},{0,4},{4,8},{8,12},{13,1},{1,5},{5,9},{9,13},{14,2},{2,6},{... | collective-permute-start | bytes 786440 | tf_op jit(solution)/shard_map/ppermute | solution.py:45
  11.3 21.9 %collective-permute-start.4 = (bf16[512,256]{1,0:T(8,128)(2,1)S(1)}, bf16[512,256]{1,0:T(8,128)(2,1)S(1)}, u32[]{:S(2)}, u32[]{:S(2)}) collective-permute-start(bf16[512,256]{1,0:T(8,128)(2,1)S(1)} %shard_map.111.refs_4_), channel_id=1, source_target_pairs={{8,0},{12,4},{0,8},{4,12},{9,1},{13,5},{1,9},{5,13},{10,2},{14,6},... | collective-permute-start | bytes 786440 | tf_op jit(solution)/shard_map/ppermute | solution.py:45
  11.9 23.3 %collective-permute-start.5 = (bf16[512,256]{1,0:T(8,128)(2,1)S(1)}, bf16[512,256]{1,0:T(8,128)(2,1)S(1)}, u32[]{:S(2)}, u32[]{:S(2)}) collective-permute-start(bf16[512,256]{1,0:T(8,128)(2,1)S(1)} %shard_map.111.refs_4_), channel_id=1, source_target_pairs={{4,0},{8,4},{12,8},{0,12},{5,1},{9,5},{13,9},{1,13},{6,2},{10,6},{... | collective-permute-start | bytes 786440 | tf_op jit(solution)/shard_map/ppermute | solution.py:45
  13.3 23.7 %collective-permute-start.15 = (bf16[128,1024]{1,0:T(8,128)(2,1)S(1)}, bf16[128,1024]{1,0:T(8,128)(2,1)S(1)}, u32[]{:S(2)}, u32[]{:S(2)}) collective-permute-start(bf16[128,1024]{1,0:T(8,128)(2,1)S(1)} %copy-done.6), channel_id=1, source_target_pairs={{3,0},{0,1},{1,2},{2,3},{7,4},{4,5},{5,6},{6,7},{11,8},{8,9},{9,10... | collective-permute-start | bytes 786440 | tf_op jit(solution)/shard_map/ppermute | solution.py:45
  14.9 9.0 %collective-permute-start.1 = (bf16[144,256]{1,0:T(8,128)(2,1)S(1)}, bf16[144,256]{1,0:T(8,128)(2,1)S(1)}, u32[]{:S(2)}, u32[]{:S(2)}) collective-permute-start(bf16[144,256]{1,0:T(8,128)(2,1)S(1)} %get-tuple-element.34), channel_id=1, source_target_pairs={{2,0},{3,1},{0,2},{1,3},{6,4},{7,5},{4,6},{5,7},{10,8},{11,9},{8,1... | collective-permute-start | bytes 221192 | tf_op jit(solution)/shard_map/ppermute | solution.py:45
  28.8 19.9 %collective-permute-start.16 = (bf16[128,1024]{1,0:T(8,128)(2,1)S(1)}, bf16[128,1024]{1,0:T(8,128)(2,1)S(1)}, u32[]{:S(2)}, u32[]{:S(2)}) collective-permute-start(bf16[128,1024]{1,0:T(8,128)(2,1)S(1)} %copy-done.6), channel_id=1, source_target_pairs={{2,0},{3,1},{0,2},{1,3},{6,4},{7,5},{4,6},{5,7},{10,8},{11,9},{8,1... | collective-permute-start | bytes 786440 | tf_op jit(solution)/shard_map/ppermute | solution.py:45
  33.2 26.6 %collective-permute-start.17 = (bf16[128,1024]{1,0:T(8,128)(2,1)S(1)}, bf16[128,1024]{1,0:T(8,128)(2,1)S(1)}, u32[]{:S(2)}, u32[]{:S(2)}) collective-permute-start(bf16[128,1024]{1,0:T(8,128)(2,1)S(1)} %copy-done.6), channel_id=1, source_target_pairs={{1,0},{2,1},{3,2},{0,3},{5,4},{6,5},{7,6},{4,7},{9,8},{10,9},{11,1... | collective-permute-start | bytes 786440 | tf_op jit(solution)/shard_map/ppermute | solution.py:45
  33.2 30.5 %collective-permute-start.18 = (bf16[128,1024]{1,0:T(8,128)(2,1)S(1)}, bf16[128,1024]{1,0:T(8,128)(2,1)S(1)}, u32[]{:S(2)}, u32[]{:S(2)}) collective-permute-start(bf16[128,1024]{1,0:T(8,128)(2,1)S(1)} %copy-done.8), channel_id=1, source_target_pairs={{3,0},{0,1},{1,2},{2,3},{7,4},{4,5},{5,6},{6,7},{11,8},{8,9},{9,10... | collective-permute-start | bytes 786440 | tf_op jit(solution)/shard_map/ppermute | solution.py:45
  35.2 34.0 %collective-permute-start.19 = (bf16[128,1024]{1,0:T(8,128)(2,1)S(1)}, bf16[128,1024]{1,0:T(8,128)(2,1)S(1)}, u32[]{:S(2)}, u32[]{:S(2)}) collective-permute-start(bf16[128,1024]{1,0:T(8,128)(2,1)S(1)} %copy-done.8), channel_id=1, source_target_pairs={{2,0},{3,1},{0,2},{1,3},{6,4},{7,5},{4,6},{5,7},{10,8},{11,9},{8,1... | collective-permute-start | bytes 786440 | tf_op jit(solution)/shard_map/ppermute | solution.py:45
  37.0 33.9 %collective-permute-start.20 = (bf16[128,1024]{1,0:T(8,128)(2,1)S(1)}, bf16[128,1024]{1,0:T(8,128)(2,1)S(1)}, u32[]{:S(2)}, u32[]{:S(2)}) collective-permute-start(bf16[128,1024]{1,0:T(8,128)(2,1)S(1)} %copy-done.8), channel_id=1, source_target_pairs={{1,0},{2,1},{3,2},{0,3},{5,4},{6,5},{7,6},{4,7},{9,8},{10,9},{11,1... | collective-permute-start | bytes 786440 | tf_op jit(solution)/shard_map/ppermute | solution.py:45
  48.7 24.3 %collective-permute-start.10 = (bf16[512,256]{1,0:T(8,128)(2,1)S(1)}, bf16[512,256]{1,0:T(8,128)(2,1)S(1)}, u32[]{:S(2)}, u32[]{:S(2)}) collective-permute-start(bf16[512,256]{1,0:T(8,128)(2,1)S(1)} %get-tuple-element.44), channel_id=1, source_target_pairs={{8,0},{12,4},{0,8},{4,12},{9,1},{13,5},{1,9},{5,13},{10,2},{14,6},... | collective-permute-start | bytes 786440 | tf_op jit(solution)/shard_map/ppermute | solution.py:45
  59.8 14.7 %collective-permute-start.11 = (bf16[512,256]{1,0:T(8,128)(2,1)S(1)}, bf16[512,256]{1,0:T(8,128)(2,1)S(1)}, u32[]{:S(2)}, u32[]{:S(2)}) collective-permute-start(bf16[512,256]{1,0:T(8,128)(2,1)S(1)} %get-tuple-element.45), channel_id=1, source_target_pairs={{12,0},{0,4},{4,8},{8,12},{13,1},{1,5},{5,9},{9,13},{14,2},{2,6},{... | collective-permute-start | bytes 786440 | tf_op jit(solution)/shard_map/ppermute | solution.py:45
  63.7 10.8 %collective-permute-start.9 = (bf16[512,256]{1,0:T(8,128)(2,1)S(1)}, bf16[512,256]{1,0:T(8,128)(2,1)S(1)}, u32[]{:S(2)}, u32[]{:S(2)}) collective-permute-start(bf16[512,256]{1,0:T(8,128)(2,1)S(1)} %get-tuple-element.43), channel_id=1, source_target_pairs={{4,0},{8,4},{12,8},{0,12},{5,1},{9,5},{13,9},{1,13},{6,2},{10,6},{... | collective-permute-start | bytes 786440 | tf_op jit(solution)/shard_map/ppermute | solution.py:45
  74.5 8.8 %collective-permute-start.7 = (bf16[128,256]{1,0:T(8,128)(2,1)S(1)}, bf16[128,256]{1,0:T(8,128)(2,1)S(1)}, u32[]{:S(2)}, u32[]{:S(2)}) collective-permute-start(bf16[128,256]{1,0:T(8,128)(2,1)S(1)} %get-tuple-element.38.refs_10_), channel_id=1, source_target_pairs={{2,0},{3,1},{0,2},{1,3},{6,4},{7,5},{4,6},{5,7},{10,8},{11,9},{8,1... | collective-permute-start | bytes 196616 | tf_op jit(solution)/shard_map/ppermute | solution.py:45
  77.6 25.1 %collective-permute-start.27 = (bf16[256,256]{1,0:T(8,128)(2,1)S(1)}, bf16[256,256]{1,0:T(8,128)(2,1)S(1)}, u32[]{:S(2)}, u32[]{:S(2)}) collective-permute-start(bf16[256,256]{1,0:T(8,128)(2,1)S(1)} %get-tuple-element.53), channel_id=1, source_target_pairs={{12,0},{0,4},{4,8},{8,12},{13,1},{1,5},{5,9},{9,13},{14,2},{2,6},{... | collective-permute-start | bytes 393224 | tf_op jit(solution)/shard_map/ppermute | solution.py:45
  83.3 18.4 %collective-permute-start.26 = (bf16[256,128]{1,0:T(8,128)(2,1)S(1)}, bf16[256,128]{1,0:T(8,128)(2,1)S(1)}, u32[]{:S(2)}, u32[]{:S(2)}) collective-permute-start(bf16[256,128]{1,0:T(8,128)(2,1)S(1)} %get-tuple-element.51.refs_0_), channel_id=1, source_target_pairs={{1,0},{2,1},{3,2},{0,3},{5,4},{6,5},{7,6},{4,7},{9,8},{10,9},{11,1... | collective-permute-start | bytes 196616 | tf_op jit(solution)/shard_map/ppermute | solution.py:45
  83.9 38.2 %collective-permute-start.12 = (bf16[512,256]{1,0:T(8,128)(2,1)S(1)}, bf16[512,256]{1,0:T(8,128)(2,1)S(1)}, u32[]{:S(2)}, u32[]{:S(2)}) collective-permute-start(bf16[512,256]{1,0:T(8,128)(2,1)S(1)} %get-tuple-element.46.refs_0_), channel_id=1, source_target_pairs={{3,0},{0,1},{1,2},{2,3},{7,4},{4,5},{5,6},{6,7},{11,8},{8,9},{9,10... | collective-permute-start | bytes 786440 | tf_op jit(solution)/shard_map/ppermute | solution.py:45
  85.6 38.3 %collective-permute-start.13 = (bf16[512,256]{1,0:T(8,128)(2,1)S(1)}, bf16[512,256]{1,0:T(8,128)(2,1)S(1)}, u32[]{:S(2)}, u32[]{:S(2)}) collective-permute-start(bf16[512,256]{1,0:T(8,128)(2,1)S(1)} %get-tuple-element.46.refs_0_), channel_id=1, source_target_pairs={{2,0},{3,1},{0,2},{1,3},{6,4},{7,5},{4,6},{5,7},{10,8},{11,9},{8,1... | collective-permute-start | bytes 786440 | tf_op jit(solution)/shard_map/ppermute | solution.py:45
  88.7 35.2 %collective-permute-start.14 = (bf16[512,256]{1,0:T(8,128)(2,1)S(1)}, bf16[512,256]{1,0:T(8,128)(2,1)S(1)}, u32[]{:S(2)}, u32[]{:S(2)}) collective-permute-start(bf16[512,256]{1,0:T(8,128)(2,1)S(1)} %get-tuple-element.46.refs_0_), channel_id=1, source_target_pairs={{1,0},{2,1},{3,2},{0,3},{5,4},{6,5},{7,6},{4,7},{9,8},{10,9},{11,1... | collective-permute-start | bytes 786440 | tf_op jit(solution)/shard_map/ppermute | solution.py:45
  107.2 11.0 %collective-permute-start.33 = (bf16[256,128]{1,0:T(8,128)(2,1)S(1)}, bf16[256,128]{1,0:T(8,128)(2,1)S(1)}, u32[]{:S(2)}, u32[]{:S(2)}) collective-permute-start(bf16[256,128]{1,0:T(8,128)(2,1)S(1)} %get-tuple-element.56), channel_id=1, source_target_pairs={{0,0},{4,1},{8,2},{12,3},{1,4},{5,5},{9,6},{13,7},{2,8},{6,9},{10,... | collective-permute-start | bytes 196616 | tf_op jit(solution)/shard_map/ppermute | solution.py:395
  109.1 9.8 %collective-permute-start.34 = (bf16[256,128]{1,0:T(8,128)(2,1)S(1)}, bf16[256,128]{1,0:T(8,128)(2,1)S(1)}, u32[]{:S(2)}, u32[]{:S(2)}) collective-permute-start(bf16[256,128]{1,0:T(8,128)(2,1)S(1)} %get-tuple-element.56), channel_id=1, source_target_pairs={{0,1},{4,2},{8,3},{12,0},{1,5},{5,6},{9,7},{13,4},{2,9},{6,10},{10... | collective-permute-start | bytes 196616 | tf_op jit(solution)/shard_map/ppermute | solution.py:395
  118.1 14.6 %collective-permute-start.30 = (bf16[256,256]{1,0:T(8,128)(2,1)S(1)}, bf16[256,256]{1,0:T(8,128)(2,1)S(1)}, u32[]{:S(2)}, u32[]{:S(2)}) collective-permute-start(bf16[256,256]{1,0:T(8,128)(2,1)S(1)} %shard_map.118.refs_4_), channel_id=1, source_target_pairs={{3,0},{0,1},{1,2},{2,3},{7,4},{4,5},{5,6},{6,7},{11,8},{8,9},{9,10... | collective-permute-start | bytes 393224 | tf_op jit(solution)/shard_map/ppermute | solution.py:45
  118.9 13.8 %collective-permute-start.31 = (bf16[256,256]{1,0:T(8,128)(2,1)S(1)}, bf16[256,256]{1,0:T(8,128)(2,1)S(1)}, u32[]{:S(2)}, u32[]{:S(2)}) collective-permute-start(bf16[256,256]{1,0:T(8,128)(2,1)S(1)} %shard_map.118.refs_4_), channel_id=1, source_target_pairs={{2,0},{3,1},{0,2},{1,3},{6,4},{7,5},{4,6},{5,7},{10,8},{11,9},{8,1... | collective-permute-start | bytes 393224 | tf_op jit(solution)/shard_map/ppermute | solution.py:45
  122.0 10.7 %collective-permute-start.32 = (bf16[256,256]{1,0:T(8,128)(2,1)S(1)}, bf16[256,256]{1,0:T(8,128)(2,1)S(1)}, u32[]{:S(2)}, u32[]{:S(2)}) collective-permute-start(bf16[256,256]{1,0:T(8,128)(2,1)S(1)} %shard_map.118.refs_4_), channel_id=1, source_target_pairs={{1,0},{2,1},{3,2},{0,3},{5,4},{6,5},{7,6},{4,7},{9,8},{10,9},{11,1... | collective-permute-start | bytes 393224 | tf_op jit(solution)/shard_map/ppermute | solution.py:45
  (23 other events, 202.9 us)

commit v2 on v0

--- a/solution.py
+++ b/solution.py
@@ -3,11 +3,359 @@
 import jax
 import jax.numpy as jnp
 from jax import lax
+from jax.experimental import pallas as pl
+from jax.experimental.pallas import tpu as pltpu
 from jax.sharding import PartitionSpec as P
 
 HEADS = 4
 DH = 128
 BLOCK = 128
+MASK_ROWS = 16
+PACK = BLOCK + MASK_ROWS
+LIMIT = 60
+WIDTH = HEADS * DH
+F32 = jnp.float32
+BF16 = jnp.bfloat16
+NT = (((1,), (1,)), ((), ()))
+TN = (((0,), (0,)), ((), ()))
+NN = (((1,), (0,)), ((), ()))
+
+
+def mm(a, b, dims):
+    return lax.dot_general(a, b, dims, preferred_element_type=F32)
+
+
+def shape(rows, columns, dtype=BF16):
+    return jax.ShapeDtypeStruct((rows, columns), dtype)
+
+
+SMEM = pl.BlockSpec(memory_space=pltpu.SMEM)
+
+
+def columns_of(index, width):
+    return pl.ds(pl.multiple_of(index * width, width), width)
+
+
+def step_from(axis, distance):
+    size = lax.axis_size(axis)
+    return [((i - distance) % size, i) for i in range(size)]
+
+
+def sent(block, axis, distance):
+    return lax.ppermute(block, axis, step_from(axis, distance))
+
+
+def whole(block):
+    return pl.BlockSpec(block.shape, lambda *_: (0,) * len(block.shape))
+
+
+def call(kernel, out_shape, operands, flops, scratch=(), in_specs=None):
+    if in_specs is None:
+        in_specs = [SMEM if x.dtype == jnp.int32 else whole(x) for x in operands]
+    outs = jax.tree.leaves(out_shape)
+    traffic = sum(2 * math.prod(x.shape) for x in (*operands, *outs))
+    return pl.pallas_call(
+        kernel,
+        out_shape=out_shape,
+        grid=(1,),
+        in_specs=in_specs,
+        out_specs=jax.tree.map(whole, out_shape),
+        scratch_shapes=list(scratch),
+        compiler_params=pltpu.CompilerParams(vmem_limit_bytes=LIMIT << 20),
+        cost_estimate=pl.CostEstimate(flops=flops, bytes_accessed=traffic, transcendentals=0),
+    )(*operands)
+
+
+def keys_kernel(place, tokens, w_key, w_value, *refs):
+    outs, (keys, values) = refs[:HEADS], refs[HEADS:]
+    keys[...] = mm(tokens[...], w_key[...], NN).astype(BF16)
+    values[...] = mm(tokens[...], w_value[...], NN).astype(BF16)
+    for d in range(HEADS):
+        head = columns_of(lax.rem(place[1] + d, HEADS), DH)
+        outs[d][:, :DH] = keys[:, head]
+        outs[d][:, DH:] = values[:, head]
+
+
+def third(w_in, index):
+    return pl.BlockSpec((w_in.shape[0], WIDTH), lambda i: (0, index))
+
+
+def project_keys(place, key_tokens, w_in):
+    rows, width = key_tokens.shape
+    return call(
+        keys_kernel,
+        [shape(rows, 2 * DH)] * HEADS,
+        (place, key_tokens, w_in, w_in),
+        4 * rows * width * WIDTH,
+        scratch=[pltpu.VMEM((rows, WIDTH), BF16)] * 2,
+        in_specs=[SMEM, whole(key_tokens), third(w_in, 1), third(w_in, 2)],
+    )
+
+
+def queries_kernel(place, crossing, home, tokens, grad, w_in, w_out, packs, *slices):
+    lane = lax.broadcasted_iota(jnp.int32, (MASK_ROWS, 2 * DH), 1)
+    row = lax.broadcasted_iota(jnp.int32, (MASK_ROWS, 2 * DH), 0)
+    mask = jnp.zeros((MASK_ROWS, 2 * DH), F32)
+    for j in range(crossing.shape[1]):
+        bit = jnp.where((crossing[0, j] > 0) | (home[0] == j), 1.0, 0.0)
+        mask = jnp.where((lane == j) & (row == 0), bit, mask)
+    for half, product in enumerate((mm(tokens[...], w_in[...], NN), mm(grad[...], w_out[...], NT))):
+        product = product.astype(BF16)
+        for h in range(HEADS):
+            packs[h * PACK : h * PACK + BLOCK, half * DH : (half + 1) * DH] = product[:, h * DH : (h + 1) * DH]
+    part = tokens.shape[1] // HEADS
+    for d in range(HEADS):
+        packs[d * PACK + BLOCK : (d + 1) * PACK, :] = mask.astype(BF16)
+        columns = columns_of(lax.rem(place[0] + d, HEADS), part)
+        slices[d][:, :part] = tokens[:, columns]
+        slices[d][:, part:] = grad[:, columns]
+
+
+def project_queries(place, query_tokens, out_grad, w_in, w_out, crossing, home):
+    rows, width = query_tokens.shape
+    return call(
+        queries_kernel,
+        [shape(HEADS * PACK, 2 * DH)] + [shape(rows, 2 * width // HEADS)] * HEADS,
+        (place, crossing, home, query_tokens, out_grad, w_in, w_out),
+        4 * rows * width * WIDTH,
+        in_specs=[SMEM] * 3 + [whole(query_tokens), whole(out_grad), third(w_in, 0), whole(w_out)],
+    )
+
+
+def side_kernel(place, key_tokens, *refs):
+    slices, side = refs[:HEADS], refs[HEADS]
+    rows, width = slices[0].shape
+    for d in range(HEADS):
+        side[d * rows : (d + 1) * rows, :width] = slices[d][...]
+    part = width // 2
+    side[:, width:] = key_tokens[:, columns_of(place[0], part)]
+
+
+def joined(place, key_tokens, slices):
+    width = 3 * key_tokens.shape[1] // HEADS
+    return call(side_kernel, shape(key_tokens.shape[0], width), (place, key_tokens, *slices), 0)
+
+
+def attend(place, packs, kvs, back, scores, bias, q_all, g_all, emit):
+    chunk = kvs[0].shape[0]
+    tiles = chunk // BLOCK
+    count = HEADS * BLOCK
+    scale = 1.0 / math.sqrt(DH)
+    ones = jnp.ones((MASK_ROWS, BLOCK), BF16)
+    for d in range(HEADS):
+        rows = slice(d * BLOCK, (d + 1) * BLOCK)
+        q_all[rows, :] = packs[d * PACK : d * PACK + BLOCK, :DH]
+        g_all[rows, :] = packs[d * PACK : d * PACK + BLOCK, DH:]
+        allowed = mm(packs[d * PACK + BLOCK : (d + 1) * PACK, :DH], ones, TN)
+        bias[:, rows] = (allowed - 1.0) * 1e30
+    q = q_all[...]
+    g = g_all[...]
+    best = jnp.full((1, count), -3e38, F32)
+    for c in range(HEADS):
+        first = lax.rem(place[1] - c + HEADS, HEADS) * tiles
+        raw = mm(kvs[c][:, :DH], q, NT) * scale
+        for j in range(tiles):
+            tile = raw[j * BLOCK : (j + 1) * BLOCK, :] + bias[pl.ds(first + j, 1), :]
+            scores[c * chunk + j * BLOCK : c * chunk + (j + 1) * BLOCK, :] = tile
+            best = jnp.maximum(best, jnp.max(tile, axis=0, keepdims=True))
+    total = jnp.zeros((1, count), F32)
+    summed = jnp.zeros((DH, count), F32)
+    for c in range(HEADS):
+        part = slice(c * chunk, (c + 1) * chunk)
+        weights = jnp.exp(scores[part, :] - best)
+        scores[part, :] = weights
+        total = total + jnp.sum(weights, axis=0, keepdims=True)
+        summed = summed + mm(kvs[c][:, DH:], weights.astype(BF16), TN)
+    share = 1.0 / total
+    attended = (summed * share).astype(BF16)
+    spread = jnp.sum(jnp.transpose(g.astype(F32)) * attended.astype(F32), axis=0, keepdims=True)
+    back[:, :DH] = jnp.transpose(attended.astype(F32)).astype(BF16)
+    query_sum = jnp.zeros((DH, count), F32)
+    for c in range(HEADS):
+        part = slice(c * chunk, (c + 1) * chunk)
+        probs = scores[part, :] * share
+        grad_probs = mm(kvs[c][:, DH:], g, NT)
+        slope = (probs * (grad_probs - spread)).astype(BF16)
+        emit(c, mm(slope, q, NN), mm(probs.astype(BF16), g, NN))
+        query_sum = query_sum + mm(kvs[c][:, :DH], slope, TN)
+    back[:, DH:] = (jnp.transpose(query_sum) * scale).astype(BF16)
+
+
+def first_kernel(place, packs, *refs):
+    kvs, (back, total, *scratch) = refs[:HEADS], refs[HEADS:]
+    chunk = kvs[0].shape[0]
+
+    def emit(c, key_step, value_step):
+        total[c * chunk : (c + 1) * chunk, :DH] = key_step
+        total[c * chunk : (c + 1) * chunk, DH:] = value_step
+
+    attend(place, packs, kvs, back, *scratch, emit)
+
+
+def middle_kernel(place, packs, *refs):
+    kvs, (before, back, total, *scratch) = refs[:HEADS], refs[HEADS:]
+    chunk = kvs[0].shape[0]
+
+    def emit(c, key_step, value_step):
+        rows = slice(c * chunk, (c + 1) * chunk)
+        total[rows, :DH] = before[rows, :DH] + key_step
+        total[rows, DH:] = before[rows, DH:] + value_step
+
+    attend(place, packs, kvs, back, *scratch, emit)
+
+
+def last_kernel(place, packs, *refs):
+    kvs, (before, other, own_back, back, home_parts, *scratch) = refs[:HEADS], refs[HEADS:]
+    chunk = kvs[0].shape[0]
+    scale = 1.0 / math.sqrt(DH)
+
+    def emit(c, key_step, value_step):
+        rows = slice(c * chunk, (c + 1) * chunk)
+        start = lax.rem(place[1] - c + HEADS, HEADS) * (chunk + BLOCK)
+        out = pl.ds(pl.multiple_of(start, BLOCK), chunk)
+        key_sum = (before[rows, :DH] + key_step) + other[rows, :DH]
+        home_parts[out, :DH] = (key_sum * scale).astype(BF16)
+        home_parts[out, DH:] = ((before[rows, DH:] + value_step) + other[rows, DH:]).astype(BF16)
+
+    attend(place, packs, kvs, back, *scratch, emit)
+    for h in range(HEADS):
+        start = h * (chunk + BLOCK) + chunk
+        home_parts[start : start + BLOCK, :] = own_back[h * BLOCK : (h + 1) * BLOCK, :]
+
+
+def attention(kernel, place, packs, kvs, extra):
+    chunk = kvs[0].shape[0]
+    keys = HEADS * chunk
+    count = HEADS * BLOCK
+    last = shape(HEADS * (chunk + BLOCK), 2 * DH) if len(extra) == 3 else shape(keys, 2 * DH, F32)
+    return call(
+        kernel,
+        [shape(count, 2 * DH), last],
+        (place, packs, *kvs, *extra),
+        12 * keys * count * DH,
+        scratch=[
+            pltpu.VMEM((keys, count), F32),
+            pltpu.VMEM((BLOCK, count), F32),
+            pltpu.VMEM((count, DH), BF16),
+            pltpu.VMEM((count, DH), BF16),
+        ],
+    )
+
+
+def weights_kernel(place, home_parts, *refs):
+    backs, refs = refs[:HEADS], refs[HEADS:]
+    sides, (inner, outer) = refs[:HEADS], refs[HEADS:]
+    part = inner.shape[0]
+    chunk = sides[0].shape[0]
+    for_keys, for_queries, for_output = 0.0, 0.0, 0.0
+    for e in range(HEADS):
+        soil = lax.rem(place[1] - e + HEADS, HEADS)
+        rows = pl.ds(pl.multiple_of(soil * (chunk + BLOCK), BLOCK), chunk)
+        for_keys = for_keys + mm(sides[e][:, 2 * part :], home_parts[rows, :], TN)
+        block = columns_of(soil, BLOCK)
+        right = jnp.concatenate([backs[d][block, :] for d in range(HEADS)], axis=0)
+        for_queries = for_queries + mm(sides[e][:, :part], right[:, DH:], TN)
+        for_output = for_output + mm(sides[e][:, part : 2 * part], right[:, :DH], TN)
+    inner[:, : 2 * DH] = for_keys.astype(BF16)
+    inner[:, 2 * DH :] = for_queries.astype(BF16)
+    outer[...] = for_output.astype(BF16)
+
+
+def weights_of(place, home_parts, backs, sides):
+    part = sides[0].shape[1] // 3
+    return call(
+        weights_kernel,
+        [shape(part, 3 * DH), shape(part, DH)],
+        (place, home_parts, *backs, *sides),
+        8 * HEADS * sides[0].shape[0] * part * DH,
+    )
+
+
+def home_kernel(parts, w_query, w_key, w_value, w_out, key_grad, output, query_grad):
+    count = key_grad.shape[0]
+    chunks = [parts.at[h * (count + BLOCK) : (h + 1) * (count + BLOCK), :] for h in range(HEADS)]
+    keys = jnp.concatenate([x[:count, :DH] for x in chunks], axis=1)
+    values = jnp.concatenate([x[:count, DH:] for x in chunks], axis=1)
+    key_grad[...] = (mm(keys, w_key[...], NT) + mm(values, w_value[...], NT)).astype(BF16)
+    attended = jnp.concatenate([x[count:, :DH] for x in chunks], axis=1)
+    output[...] = mm(attended, w_out[...], NN).astype(BF16)
+    grad = jnp.concatenate([x[count:, DH:] for x in chunks], axis=1)
+    query_grad[...] = mm(grad, w_query[...], NT).astype(BF16)
+
+
+def home_outputs(parts, w_in, w_out):
+    width = w_in.shape[0]
+    count = parts.shape[0] // HEADS - BLOCK
+    return call(
+        home_kernel,
+        [shape(count, width), shape(BLOCK, width), shape(BLOCK, width)],
+        (parts, w_in, w_in, w_in, w_out),
+        4 * (count + BLOCK) * width * WIDTH,
+        in_specs=[whole(parts), third(w_in, 0), third(w_in, 1), third(w_in, 2), whole(w_out)],
+    )
+
+
+def place_weights_kernel(place, *refs):
+    inner, outer, (w_in_grad, w_out_grad) = refs[:HEADS], refs[HEADS : 2 * HEADS], refs[2 * HEADS :]
+    rows = inner[0].shape[0]
+    for d in range(HEADS):
+        index = lax.rem(place[0] - d + HEADS, HEADS)
+        w_in_grad[:, columns_of(index, DH)] = inner[d][:, 2 * DH :].astype(F32)
+        w_in_grad[:, columns_of(HEADS + index, DH)] = inner[d][:, :DH].astype(F32)
+        w_in_grad[:, columns_of(2 * HEADS + index, DH)] = inner[d][:, DH : 2 * DH].astype(F32)
+        w_out_grad[:, columns_of(index, rows)] = jnp.transpose(outer[d][...].astype(F32))
+
+
+def place_weights(place, inner, outer):
+    rows = inner[0].shape[0]
+    return call(
+        place_weights_kernel,
+        [shape(rows, 3 * WIDTH, F32), shape(DH, HEADS * rows, F32)],
+        (place, *inner, *outer),
+        rows * 4 * WIDTH,
+    )
+
+
+def after(value, *others):
+    return lax.optimization_barrier((value, *others))[0]
+
+
+def swapped(block, axis):
+    return lax.all_to_all(block, axis, 0, 0, tiled=True)
+
+
+def spread_to(block, axis):
+    return [block] + [sent(block, axis, d) for d in range(1, HEADS)]
+
+
+def head_body(query_tokens, key_tokens, w_in, w_out, out_grad, crossing, home):
+    place = jnp.stack([lax.axis_index("stand"), lax.axis_index("soil")]).astype(jnp.int32)
+    distances = range(1, HEADS)
+    packs, *slices = project_queries(place, query_tokens, out_grad, w_in, w_out, crossing, home)
+    packs = swapped(packs, "soil")
+    kvs = project_keys(place, key_tokens, w_in)
+    kvs = [kvs[0]] + [sent(kvs[d], "soil", d) for d in distances]
+    slices = [slices[0]] + [sent(slices[d], "stand", d) for d in distances]
+    planes = spread_to(packs, "stand")
+    sides = spread_to(joined(place, key_tokens, slices), "soil")
+    back_0, even = attention(first_kernel, place, planes[0], kvs, ())
+    back_1, odd = attention(first_kernel, place, planes[1], kvs, ())
+    back_3, odd = attention(middle_kernel, place, planes[3], kvs, (odd,))
+    back_2, home_parts = attention(last_kernel, place, planes[2], kvs, (even, odd, back_0))
+    inner, outer = weights_of(place, home_parts, [back_0, back_1, back_2, back_3], sides)
+    home_parts = swapped(home_parts, "soil")
+    key_grad, output, query_grad = home_outputs(home_parts, w_in, w_out)
+    outer = spread_to(outer, "stand")
+    crosswise = []
+    for d in range(HEADS):
+        route = [
+            (soil * HEADS + stand, stand * HEADS + (soil + d) % HEADS)
+            for stand in range(HEADS)
+            for soil in range(HEADS)
+        ]
+        crosswise.append(lax.ppermute(inner, ("soil", "stand"), route))
+    w_in_grad, w_out_grad = place_weights(place, crosswise, outer)
+    return (output, query_grad, key_grad, w_in_grad, w_out_grad)
 
 
 NEG = -1e30
@@ -94,7 +442,7 @@
     return (grad_query, grad_key, grad_value)
 
 
-def body(query_tokens, key_tokens, w_in, w_out, out_grad, crossing, home):
+def ring_body(query_tokens, key_tokens, w_in, w_out, out_grad, crossing, home):
     attn_width = HEADS * DH
     query_count = query_tokens.shape[0]
     key_count = key_tokens.shape[0]
@@ -233,4 +581,6 @@
         P(("field", "soil"), None),
         P(("field", "soil"), None),
     )
+    square = mesh.shape["stand"] == HEADS and mesh.shape["soil"] == HEADS
+    body = head_body if square else ring_body
     return jax.shard_map(body, mesh=mesh, in_specs=in_specs, out_specs=out_specs, check_vma=False)

time: 376 us -> 124 us (0.33)
  waiting for transfers between devices: 174 us -> 24.3 us
  blocking collectives: 73.3 us -> 0 us
  Pallas kernels: 0 us -> 50.3 us
  matrix products: 43.4 us -> 0 us
  other arithmetic: 25.4 us -> 0.6 us
  starting transfers between devices: 20.1 us -> 38.7 us
  local copies, waits for them, and re-layouts: 20.3 us -> 6.28 us
  between operations: 14.6 us -> 1.45 us
    psum x1 -> x0, waiting for transfers between devices: 81.4 us -> none  [body(): w_in_grad, w_out_grad = lax.psum((w_in_part, w_out_part), 'stand')]
    psum x1 -> x0, blocking collectives: 73.3 us -> none  [body(): grad_key, grad_value = lax.psum((grad_key, grad_value), 'stand')]
    reduce_scatter x2 -> x0, waiting for transfers between devices: 60 us -> none  [the longest x1 60 us: body(): lax.psum_scatter(jnp.concatenate([query_part, key_part], axis=1), 'soil',...]
    pallas_call x0 -> x10, Pallas kernels: none -> 50.3 us  [call(): pl.pallas_call(kernel, out_shape=out_shape, grid=(1,), in_specs=in_specs,...]
    dot_general x45 -> x0, matrix products: 43.4 us -> none  [the longest x4 5.85 us: backward_tile(): jnp.einsum('qhd,khd->hqk', query_heads, key_heads, preferred_element_type...]
    add x13 -> x0, other arithmetic: 18.6 us -> none  [the longest x4 11.9 us: backward_tile(): grad_value = grad_value + value_step.reshape(key_count, HEADS * DH)]
    ppermute x44 -> x19, starting transfers between devices: 20 us -> 30.3 us  [the longest x15 22.1 us: sent(): return lax.ppermute(block, axis, step_from(axis, distance))]
    while x26 -> x0, local copies, waits for them, and re-layouts: 10.1 us -> none
  transfers between devices with their start and end apart: 47 -> 21, of which waited for: 14 -> 4; matrix products, arithmetic and copies ran while one was open for 19% -> 0% of each run, Pallas kernels for 0% -> 35%
where the time goes in v2:
time: 124 us; the launch traced here: 122 us
  Pallas kernels  50.3 us (41%)
  starting transfers between devices  38.7 us (31%)
  waiting for transfers between devices  24.3 us (20%)
  local copies, waits for them, and re-layouts  6.28 us (5%)
  between operations  1.45 us (1%)
    pallas_call x10, Pallas kernels, call(): pl.pallas_call(kernel, out_shape=out_shape, grid=(1,), in_specs=in_specs,...  50.3 us
    ppermute x15, waiting for transfers between devices, sent(): return lax.ppermute(block, axis, step_from(axis, distance))  24.3 us
    ppermute x15, starting transfers between devices, sent(): return lax.ppermute(block, axis, step_from(axis, distance))  22.1 us
    all_to_all x2, starting transfers between devices, swapped(): return lax.all_to_all(block, axis, 0, 0, tiled=True)  8.35 us
    ppermute x4, starting transfers between devices, head_body(): crosswise.append(lax.ppermute(inner, ('soil', 'stand'), route))  8.21 us
    unnamed x42, local copies, waits for them, and re-layouts  6.28 us
  transfers between devices with their start and end apart: 21, of which 4 were waited for; matrix products, arithmetic and copies ran while one was open for 0% of the time, Pallas kernels for 35%

profile of v2, /device:TPU:14, one launch (start us, length us, event | category | flops | bytes accessed | tf_op | source)
XLA Modules:
  0.0 121.6 jit_solution(4654429134062595514)
XLA Ops:
  1.9 3.1 %shard_map.110 = (bf16[576,256]{1,0:T(8,128)(2,1)}, bf16[128,512]{1,0:T(8,128)(2,1)}, bf16[128,512]{1,0:T(8,128)(2,1)}, bf16[128,512]{1,0:T(8,128)(2,1)}, bf16[128,512]{1,0:T(8,128)(2,1)}) custom-call(s32[2]{0:T(128)} %pad_add_fusion.place, s32[1,16]{1,0:T(1,128)} %crossing.1, s32[1]{0:T(128)S(6)} %copy.12.home, bf16[128,1024]{1,0:T(8,128)(2,1)} %tokens.2, ...), custom_call_target="tpu_custom_call" | custom-call | flops 268435456 | bytes 5537830 | tf_op jit(solution)/shard_map/pallas_call | solution.py:57
  5.0 3.9 %all-to-all-start = ((bf16[4,144,256]{2,1,0:T(8,128)(2,1)}), bf16[4,144,256]{2,1,0:T(8,128)(2,1)S(1)}, u32[]{:S(2)}, u32[]{:S(2)}) async-start(bf16[4,144,256]{2,1,0:T(8,128)(2,1)} %bitcast.12), calls=%async_computation | async-start | bytes 589824 | tf_op jit(solution)/shard_map/all_to_all | solution.py:324
  8.9 1.6 %collective-permute-start.6 = (bf16[128,512]{1,0:T(8,128)(2,1)}, bf16[128,512]{1,0:T(8,128)(2,1)S(1)}, u32[]{:S(2)}, u32[]{:S(2)}) collective-permute-start(bf16[128,512]{1,0:T(8,128)(2,1)} %get-tuple-element.46), channel_id=1, source_target_pairs={{3,0},{0,1},{1,2},{2,3},{7,4},{4,5},{5,6},{6,7},{11,8},{8,9},{9,10... | collective-permute-start | bytes 393224 | tf_op jit(solution)/shard_map/ppermute | solution.py:45
  11.7 4.3 %shard_map.111 = (bf16[512,256]{1,0:T(8,128)(2,1)}, bf16[512,256]{1,0:T(8,128)(2,1)}, bf16[512,256]{1,0:T(8,128)(2,1)}, bf16[512,256]{1,0:T(8,128)(2,1)}) custom-call(s32[2]{0:T(128)} %pad_add_fusion.place, bf16[512,1024]{1,0:T(8,128)(2,1)} %key_tokens.1, bf16[1024,1536]{1,0:T(8,128)(2,1)} %w_value.3, bf16[1024,1536]{1,0:T(8,128)(2,1)} %w_value.3), custom_call_target="tpu_custom_call" | custom-call | flops 1073741824 | bytes 8388612 | tf_op jit(solution)/shard_map/pallas_call | solution.py:57
  16.2 1.7 %collective-permute-start.3 = (bf16[512,256]{1,0:T(8,128)(2,1)}, bf16[512,256]{1,0:T(8,128)(2,1)S(1)}, u32[]{:S(2)}, u32[]{:S(2)}) collective-permute-start(bf16[512,256]{1,0:T(8,128)(2,1)} %get-tuple-element.33), channel_id=1, source_target_pairs={{4,0},{8,4},{12,8},{0,12},{5,1},{9,5},{13,9},{1,13},{6,2},{10,6},{... | collective-permute-start | bytes 786440 | tf_op jit(solution)/shard_map/ppermute | solution.py:45
  17.9 2.0 %collective-permute-start.5 = (bf16[576,256]{1,0:T(8,128)(2,1)S(1)}, bf16[576,256]{1,0:T(8,128)(2,1)S(1)}, u32[]{:S(2)}, u32[]{:S(2)}) collective-permute-start(bf16[576,256]{1,0:T(8,128)(2,1)S(1)} %bitcast.8), channel_id=1, source_target_pairs={{3,0},{0,1},{1,2},{2,3},{7,4},{4,5},{5,6},{6,7},{11,8},{8,9},{9,10... | collective-permute-start | bytes 884744 | tf_op jit(solution)/shard_map/ppermute | solution.py:45
  20.0 2.6 %collective-permute-start.8 = (bf16[128,512]{1,0:T(8,128)(2,1)S(1)}, bf16[128,512]{1,0:T(8,128)(2,1)S(1)}, u32[]{:S(2)}, u32[]{:S(2)}) collective-permute-start(bf16[128,512]{1,0:T(8,128)(2,1)S(1)} %copy-done.20), channel_id=1, source_target_pairs={{1,0},{2,1},{3,2},{0,3},{5,4},{6,5},{7,6},{4,7},{9,8},{10,9},{11,1... | collective-permute-start | bytes 393224 | tf_op jit(solution)/shard_map/ppermute | solution.py:45
  22.6 8.4 %collective-permute-done.8.refs_3_ = bf16[128,512]{1,0:T(8,128)(2,1)S(1)} collective-permute-done((bf16[128,512]{1,0:T(8,128)(2,1)S(1)}, bf16[128,512]{1,0:T(8,128)(2,1)S(1)}, u32[]{:S(2)}, u32[]{:S(2)}) %collective-permute-start.8) | collective-permute-done | bytes 131104 | tf_op jit(solution)/shard_map/ppermute | solution.py:45
  31.6 2.3 %shard_map.117.refs_4_ = bf16[512,768]{1,0:T(8,128)(2,1)} custom-call(s32[2]{0:T(128)} %pad_add_fusion.place, bf16[512,1024]{1,0:T(8,128)(2,1)} %key_tokens.1, bf16[128,512]{1,0:T(8,128)(2,1)} %get-tuple-element.45.refs_0_, bf16[128,512]{1,0:T(8,128)(2,1)} %copy-done.8, bf16[128,512]{1,0:T(8,128)(2,1)} %copy-done.9, bf16[128,512]{1,0:T(8,128)(2,1)} %copy-done.10), custom_call_target="tpu_custom_call" | custom-call | bytes 2359300 | tf_op jit(solution)/shard_map/pallas_call | solution.py:57
  35.4 2.7 %collective-permute-start.4 = (bf16[576,256]{1,0:T(8,128)(2,1)S(1)}, bf16[576,256]{1,0:T(8,128)(2,1)S(1)}, u32[]{:S(2)}, u32[]{:S(2)}) collective-permute-start(bf16[576,256]{1,0:T(8,128)(2,1)S(1)} %bitcast.9), channel_id=1, source_target_pairs={{1,0},{2,1},{3,2},{0,3},{5,4},{6,5},{7,6},{4,7},{9,8},{10,9},{11,1... | collective-permute-start | bytes 884744 | tf_op jit(solution)/shard_map/ppermute | solution.py:45
  38.1 6.5 %shard_map.112 = (bf16[512,256]{1,0:T(8,128)(2,1)}, f32[2048,256]{1,0:T(8,128)}) custom-call(s32[2]{0:T(128)} %pad_add_fusion.place, bf16[576,256]{1,0:T(8,128)(2,1)} %bitcast.10, bf16[512,256]{1,0:T(8,128)(2,1)} %get-tuple-element.30.refs_0_, bf16[512,256]{1,0:T(8,128)(2,1)} %copy-done.17, bf16[512,256]{1,0:T(8,128)(2,1)} %copy-done.18, ...), custom_call_target="tpu_custom_call" | custom-call | flops 1610612736 | bytes 2654212 | tf_op jit(solution)/shard_map/pallas_call | solution.py:57
  45.4 6.6 %shard_map.113 = (bf16[512,256]{1,0:T(8,128)(2,1)}, f32[2048,256]{1,0:T(8,128)}) custom-call(s32[2]{0:T(128)} %pad_add_fusion.place, bf16[576,256]{1,0:T(8,128)(2,1)} %copy-done.14, bf16[512,256]{1,0:T(8,128)(2,1)} %get-tuple-element.30.refs_0_, bf16[512,256]{1,0:T(8,128)(2,1)} %copy-done.17, bf16[512,256]{1,0:T(8,128)(2,1)} %copy-done.18, ...), custom_call_target="tpu_custom_call" | custom-call | flops 1610612736 | bytes 2654212 | tf_op jit(solution)/shard_map/pallas_call | solution.py:57
  52.7 7.3 %shard_map.114 = (bf16[512,256]{1,0:T(8,128)(2,1)}, f32[2048,256]{1,0:T(8,128)}) custom-call(s32[2]{0:T(128)} %pad_add_fusion.place, bf16[576,256]{1,0:T(8,128)(2,1)} %copy-done.16, bf16[512,256]{1,0:T(8,128)(2,1)} %get-tuple-element.30.refs_0_, bf16[512,256]{1,0:T(8,128)(2,1)} %copy-done.17, bf16[512,256]{1,0:T(8,128)(2,1)} %copy-done.18, ...), custom_call_target="tpu_custom_call" | custom-call | flops 1610612736 | bytes 3702788 | tf_op jit(solution)/shard_map/pallas_call | solution.py:57
  60.7 8.0 %shard_map.115 = (bf16[512,256]{1,0:T(8,128)(2,1)}, bf16[2560,256]{1,0:T(8,128)(2,1)}) custom-call(s32[2]{0:T(128)} %pad_add_fusion.place, bf16[576,256]{1,0:T(8,128)(2,1)} %copy-done.15, bf16[512,256]{1,0:T(8,128)(2,1)} %get-tuple-element.30.refs_0_, bf16[512,256]{1,0:T(8,128)(2,1)} %copy-done.17, bf16[512,256]{1,0:T(8,128)(2,1)} %copy-done.18, ...), custom_call_target="tpu_custom_call" | custom-call | flops 1610612736 | bytes 5275652 | tf_op jit(solution)/shard_map/pallas_call | solution.py:57
  68.7 4.4 %all-to-all-start.1 = ((bf16[4,640,256]{2,1,0:T(8,128)(2,1)}), bf16[4,640,256]{2,1,0:T(8,128)(2,1)S(1)}, u32[]{:S(2)}, u32[]{:S(2)}) async-start(bf16[4,640,256]{2,1,0:T(8,128)(2,1)} %bitcast.6), calls=%async_computation.1 | async-start | bytes 2621440 | tf_op jit(solution)/shard_map/all_to_all | solution.py:324
  74.2 4.2 %shard_map.118 = (bf16[256,384]{1,0:T(8,128)(2,1)}, bf16[256,128]{1,0:T(8,128)(2,1)}) custom-call(s32[2]{0:T(128)} %pad_add_fusion.place, bf16[2560,256]{1,0:T(8,128)(2,1)} %get-tuple-element.38.home_parts, bf16[512,256]{1,0:T(8,128)(2,1)} %get-tuple-element.37.refs_6_.refs_0_, bf16[512,256]{1,0:T(8,128)(2,1)} %get-tuple-element.42.refs_1_, ...), custom_call_target="tpu_custom_call" | custom-call | flops 536870912 | bytes 5767172 | tf_op jit(solution)/shard_map/pallas_call | solution.py:57
  80.0 2.5 %collective-permute-start.12 = (bf16[256,384]{1,0:T(8,128)(2,1)}, bf16[256,384]{1,0:T(8,128)(2,1)S(1)}, u32[]{:S(2)}, u32[]{:S(2)}) collective-permute-start(bf16[256,384]{1,0:T(8,128)(2,1)} %get-tuple-element.49), channel_id=1, source_target_pairs={{0,0},{4,1},{8,2},{12,3},{1,4},{5,5},{9,6},{13,7},{2,8},{6,9},{10,... | collective-permute-start | bytes 589832 | tf_op jit(solution)/shard_map/ppermute | solution.py:356
  82.5 2.5 %collective-permute-start.13 = (bf16[256,384]{1,0:T(8,128)(2,1)}, bf16[256,384]{1,0:T(8,128)(2,1)S(1)}, u32[]{:S(2)}, u32[]{:S(2)}) collective-permute-start(bf16[256,384]{1,0:T(8,128)(2,1)} %get-tuple-element.49), channel_id=1, source_target_pairs={{0,1},{4,2},{8,3},{12,0},{1,5},{5,6},{9,7},{13,4},{2,9},{6,10},{10... | collective-permute-start | bytes 589832 | tf_op jit(solution)/shard_map/ppermute | solution.py:356
  84.9 1.8 %collective-permute-start.14 = (bf16[256,384]{1,0:T(8,128)(2,1)}, bf16[256,384]{1,0:T(8,128)(2,1)S(1)}, u32[]{:S(2)}, u32[]{:S(2)}) collective-permute-start(bf16[256,384]{1,0:T(8,128)(2,1)} %get-tuple-element.49), channel_id=1, source_target_pairs={{0,2},{4,3},{8,0},{12,1},{1,6},{5,7},{9,4},{13,5},{2,10},{6,11},{1... | collective-permute-start | bytes 589832 | tf_op jit(solution)/shard_map/ppermute | solution.py:356
  88.7 13.6 %collective-permute-done.17.refs_6_ = bf16[256,128]{1,0:T(8,128)(2,1)S(1)} collective-permute-done((bf16[256,128]{1,0:T(8,128)(2,1)}, bf16[256,128]{1,0:T(8,128)(2,1)S(1)}, u32[]{:S(2)}, u32[]{:S(2)}) %collective-permute-start.17) | collective-permute-done | bytes 65568 | tf_op jit(solution)/shard_map/ppermute | solution.py:45
  102.3 6.6 %collective-permute-start.18 = (bf16[256,128]{1,0:T(8,128)(2,1)}, bf16[256,128]{1,0:T(8,128)(2,1)S(1)}, u32[]{:S(2)}, u32[]{:S(2)}) collective-permute-start(bf16[256,128]{1,0:T(8,128)(2,1)} %get-tuple-element.50.refs_4_), channel_id=1, source_target_pairs={{1,0},{2,1},{3,2},{0,3},{5,4},{6,5},{7,6},{4,7},{9,8},{10,9},{11,1... | collective-permute-start | bytes 196616 | tf_op jit(solution)/shard_map/ppermute | solution.py:45
  108.9 2.2 %collective-permute-done.18.refs_7_ = bf16[256,128]{1,0:T(8,128)(2,1)S(1)} collective-permute-done((bf16[256,128]{1,0:T(8,128)(2,1)}, bf16[256,128]{1,0:T(8,128)(2,1)S(1)}, u32[]{:S(2)}, u32[]{:S(2)}) %collective-permute-start.18) | collective-permute-done | bytes 65568 | tf_op jit(solution)/shard_map/ppermute | solution.py:45
  112.6 2.8 %shard_map.119 = (f32[256,1536]{1,0:T(8,128)}, f32[128,1024]{1,0:T(8,128)}) custom-call(s32[2]{0:T(128)} %pad_add_fusion.place, bf16[256,384]{1,0:T(8,128)(2,1)} %copy-done.4, bf16[256,384]{1,0:T(8,128)(2,1)} %copy-done.5, bf16[256,384]{1,0:T(8,128)(2,1)} %copy-done.6, bf16[256,384]{1,0:T(8,128)(2,1)} %copy-done.7, ...), custom_call_target="tpu_custom_call" | custom-call | flops 524288 | bytes 2097156 | tf_op jit(solution)/shard_map/pallas_call | solution.py:57
  116.5 5.0 %shard_map.116 = (bf16[512,1024]{1,0:T(8,128)(2,1)}, bf16[128,1024]{1,0:T(8,128)(2,1)}, bf16[128,1024]{1,0:T(8,128)(2,1)}) custom-call(bf16[2560,256]{1,0:T(8,128)(2,1)} %bitcast.7, bf16[1024,1536]{1,0:T(8,128)(2,1)} %w_value.3, bf16[1024,1536]{1,0:T(8,128)(2,1)} %w_value.3, bf16[1024,1536]{1,0:T(8,128)(2,1)} %w_value.3, bf16[512,1024]{1,0:T(8,128)(2,1)} %w_out.3), custom_call_target="tpu_custom_call" | custom-call | flops 1342177280 | bytes 13369344 | tf_op jit(solution)/shard_map/pallas_call | solution.py:57
  (71 shorter events, 13.4 us)
Async XLA Ops:
  5.0 12.9 %all-to-all-start = ((bf16[4,144,256]{2,1,0:T(8,128)(2,1)}), bf16[4,144,256]{2,1,0:T(8,128)(2,1)S(1)}, u32[]{:S(2)}, u32[]{:S(2)}) async-start(bf16[4,144,256]{2,1,0:T(8,128)(2,1)} %bitcast.12), calls=%async_computation | async-start | bytes 589824 | tf_op jit(solution)/shard_map/all_to_all | solution.py:324
  8.9 8.9 %collective-permute-start.6 = (bf16[128,512]{1,0:T(8,128)(2,1)}, bf16[128,512]{1,0:T(8,128)(2,1)S(1)}, u32[]{:S(2)}, u32[]{:S(2)}) collective-permute-start(bf16[128,512]{1,0:T(8,128)(2,1)} %get-tuple-element.46), channel_id=1, source_target_pairs={{3,0},{0,1},{1,2},{2,3},{7,4},{4,5},{5,6},{6,7},{11,8},{8,9},{9,10... | collective-permute-start | bytes 393224 | tf_op jit(solution)/shard_map/ppermute | solution.py:45
  10.5 9.5 %collective-permute-start.7 = (bf16[128,512]{1,0:T(8,128)(2,1)}, bf16[128,512]{1,0:T(8,128)(2,1)S(1)}, u32[]{:S(2)}, u32[]{:S(2)}) collective-permute-start(bf16[128,512]{1,0:T(8,128)(2,1)} %get-tuple-element.47), channel_id=1, source_target_pairs={{2,0},{3,1},{0,2},{1,3},{6,4},{7,5},{4,6},{5,7},{10,8},{11,9},{8,1... | collective-permute-start | bytes 393224 | tf_op jit(solution)/shard_map/ppermute | solution.py:45
  16.1 18.6 %collective-permute-start.1 = (bf16[512,256]{1,0:T(8,128)(2,1)}, bf16[512,256]{1,0:T(8,128)(2,1)S(1)}, u32[]{:S(2)}, u32[]{:S(2)}) collective-permute-start(bf16[512,256]{1,0:T(8,128)(2,1)} %get-tuple-element.31), channel_id=1, source_target_pairs={{12,0},{0,4},{4,8},{8,12},{13,1},{1,5},{5,9},{9,13},{14,2},{2,6},{... | collective-permute-start | bytes 786440 | tf_op jit(solution)/shard_map/ppermute | solution.py:45
  16.1 19.3 %collective-permute-start.2 = (bf16[512,256]{1,0:T(8,128)(2,1)}, bf16[512,256]{1,0:T(8,128)(2,1)S(1)}, u32[]{:S(2)}, u32[]{:S(2)}) collective-permute-start(bf16[512,256]{1,0:T(8,128)(2,1)} %get-tuple-element.32), channel_id=1, source_target_pairs={{8,0},{12,4},{0,8},{4,12},{9,1},{13,5},{1,9},{5,13},{10,2},{14,6},... | collective-permute-start | bytes 786440 | tf_op jit(solution)/shard_map/ppermute | solution.py:45
  16.2 19.2 %collective-permute-start.3 = (bf16[512,256]{1,0:T(8,128)(2,1)}, bf16[512,256]{1,0:T(8,128)(2,1)S(1)}, u32[]{:S(2)}, u32[]{:S(2)}) collective-permute-start(bf16[512,256]{1,0:T(8,128)(2,1)} %get-tuple-element.33), channel_id=1, source_target_pairs={{4,0},{8,4},{12,8},{0,12},{5,1},{9,5},{13,9},{1,13},{6,2},{10,6},{... | collective-permute-start | bytes 786440 | tf_op jit(solution)/shard_map/ppermute | solution.py:45
  17.9 13.1 %copy-start.8 = (bf16[128,512]{1,0:T(8,128)(2,1)}, bf16[128,512]{1,0:T(8,128)(2,1)S(1)}, u32[]{:S(2)}) copy-start(bf16[128,512]{1,0:T(8,128)(2,1)S(1)} %collective-permute-done.6.refs_1_) | copy-start | bytes 393220
  17.9 20.2 %copy-start.3 = (bf16[4,144,256]{2,1,0:T(8,128)(2,1)}, bf16[4,144,256]{2,1,0:T(8,128)(2,1)S(1)}, u32[]{:S(2)}) copy-start(bf16[4,144,256]{2,1,0:T(8,128)(2,1)S(1)} %all-to-all-done) | copy-start | bytes 884740
  17.9 26.8 %collective-permute-start.5 = (bf16[576,256]{1,0:T(8,128)(2,1)S(1)}, bf16[576,256]{1,0:T(8,128)(2,1)S(1)}, u32[]{:S(2)}, u32[]{:S(2)}) collective-permute-start(bf16[576,256]{1,0:T(8,128)(2,1)S(1)} %bitcast.8), channel_id=1, source_target_pairs={{3,0},{0,1},{1,2},{2,3},{7,4},{4,5},{5,6},{6,7},{11,8},{8,9},{9,10... | collective-permute-start | bytes 884744 | tf_op jit(solution)/shard_map/ppermute | solution.py:45
  20.0 11.0 %collective-permute-start.8 = (bf16[128,512]{1,0:T(8,128)(2,1)S(1)}, bf16[128,512]{1,0:T(8,128)(2,1)S(1)}, u32[]{:S(2)}, u32[]{:S(2)}) collective-permute-start(bf16[128,512]{1,0:T(8,128)(2,1)S(1)} %copy-done.20), channel_id=1, source_target_pairs={{1,0},{2,1},{3,2},{0,3},{5,4},{6,5},{7,6},{4,7},{9,8},{10,9},{11,1... | collective-permute-start | bytes 393224 | tf_op jit(solution)/shard_map/ppermute | solution.py:45
  34.0 39.1 %collective-permute-start.10 = (bf16[512,768]{1,0:T(8,128)(2,1)}, bf16[512,768]{1,0:T(8,128)(2,1)S(1)}, u32[]{:S(2)}, u32[]{:S(2)}) collective-permute-start(bf16[512,768]{1,0:T(8,128)(2,1)} %shard_map.117.refs_4_), channel_id=1, source_target_pairs={{8,0},{12,4},{0,8},{4,12},{9,1},{13,5},{1,9},{5,13},{10,2},{14,6},... | collective-permute-start | bytes 2359304 | tf_op jit(solution)/shard_map/ppermute | solution.py:45
  34.7 38.4 %collective-permute-start.11 = (bf16[512,768]{1,0:T(8,128)(2,1)}, bf16[512,768]{1,0:T(8,128)(2,1)S(1)}, u32[]{:S(2)}, u32[]{:S(2)}) collective-permute-start(bf16[512,768]{1,0:T(8,128)(2,1)} %shard_map.117.refs_4_), channel_id=1, source_target_pairs={{4,0},{8,4},{12,8},{0,12},{5,1},{9,5},{13,9},{1,13},{6,2},{10,6},{... | collective-permute-start | bytes 2359304 | tf_op jit(solution)/shard_map/ppermute | solution.py:45
  35.4 37.7 %collective-permute-start.9 = (bf16[512,768]{1,0:T(8,128)(2,1)}, bf16[512,768]{1,0:T(8,128)(2,1)}, u32[]{:S(2)}, u32[]{:S(2)}) collective-permute-start(bf16[512,768]{1,0:T(8,128)(2,1)} %shard_map.117.refs_4_), channel_id=1, source_target_pairs={{12,0},{0,4},{4,8},{8,12},{13,1},{1,5},{5,9},{9,13},{14,2},{2,6},{... | collective-permute-start | bytes 2359304 | tf_op jit(solution)/shard_map/ppermute | solution.py:45
  35.4 16.6 %collective-permute-start.4 = (bf16[576,256]{1,0:T(8,128)(2,1)S(1)}, bf16[576,256]{1,0:T(8,128)(2,1)S(1)}, u32[]{:S(2)}, u32[]{:S(2)}) collective-permute-start(bf16[576,256]{1,0:T(8,128)(2,1)S(1)} %bitcast.9), channel_id=1, source_target_pairs={{1,0},{2,1},{3,2},{0,3},{5,4},{6,5},{7,6},{4,7},{9,8},{10,9},{11,1... | collective-permute-start | bytes 884744 | tf_op jit(solution)/shard_map/ppermute | solution.py:45
  44.7 15.3 %collective-permute-start = (bf16[576,256]{1,0:T(8,128)(2,1)}, bf16[576,256]{1,0:T(8,128)(2,1)S(1)}, u32[]{:S(2)}, u32[]{:S(2)}) collective-permute-start(bf16[576,256]{1,0:T(8,128)(2,1)} %bitcast.11), channel_id=1, source_target_pairs={{2,0},{3,1},{0,2},{1,3},{6,4},{7,5},{4,6},{5,7},{10,8},{11,9},{8,1... | collective-permute-start | bytes 884744 | tf_op jit(solution)/shard_map/ppermute | solution.py:45
  68.7 46.8 %all-to-all-start.1 = ((bf16[4,640,256]{2,1,0:T(8,128)(2,1)}), bf16[4,640,256]{2,1,0:T(8,128)(2,1)S(1)}, u32[]{:S(2)}, u32[]{:S(2)}) async-start(bf16[4,640,256]{2,1,0:T(8,128)(2,1)} %bitcast.6), calls=%async_computation.1 | async-start | bytes 2621440 | tf_op jit(solution)/shard_map/all_to_all | solution.py:324
  78.5 9.7 %collective-permute-start.16 = (bf16[256,128]{1,0:T(8,128)(2,1)}, bf16[256,128]{1,0:T(8,128)(2,1)S(1)}, u32[]{:S(2)}, u32[]{:S(2)}) collective-permute-start(bf16[256,128]{1,0:T(8,128)(2,1)} %get-tuple-element.50.refs_4_), channel_id=1, source_target_pairs={{3,0},{0,1},{1,2},{2,3},{7,4},{4,5},{5,6},{6,7},{11,8},{8,9},{9,10... | collective-permute-start | bytes 196616 | tf_op jit(solution)/shard_map/ppermute | solution.py:45
  80.0 31.2 %collective-permute-start.12 = (bf16[256,384]{1,0:T(8,128)(2,1)}, bf16[256,384]{1,0:T(8,128)(2,1)S(1)}, u32[]{:S(2)}, u32[]{:S(2)}) collective-permute-start(bf16[256,384]{1,0:T(8,128)(2,1)} %get-tuple-element.49), channel_id=1, source_target_pairs={{0,0},{4,1},{8,2},{12,3},{1,4},{5,5},{9,6},{13,7},{2,8},{6,9},{10,... | collective-permute-start | bytes 589832 | tf_op jit(solution)/shard_map/ppermute | solution.py:356
  82.5 28.7 %collective-permute-start.13 = (bf16[256,384]{1,0:T(8,128)(2,1)}, bf16[256,384]{1,0:T(8,128)(2,1)S(1)}, u32[]{:S(2)}, u32[]{:S(2)}) collective-permute-start(bf16[256,384]{1,0:T(8,128)(2,1)} %get-tuple-element.49), channel_id=1, source_target_pairs={{0,1},{4,2},{8,3},{12,0},{1,5},{5,6},{9,7},{13,4},{2,9},{6,10},{10... | collective-permute-start | bytes 589832 | tf_op jit(solution)/shard_map/ppermute | solution.py:356
  84.9 26.2 %collective-permute-start.14 = (bf16[256,384]{1,0:T(8,128)(2,1)}, bf16[256,384]{1,0:T(8,128)(2,1)S(1)}, u32[]{:S(2)}, u32[]{:S(2)}) collective-permute-start(bf16[256,384]{1,0:T(8,128)(2,1)} %get-tuple-element.49), channel_id=1, source_target_pairs={{0,2},{4,3},{8,0},{12,1},{1,6},{5,7},{9,4},{13,5},{2,10},{6,11},{1... | collective-permute-start | bytes 589832 | tf_op jit(solution)/shard_map/ppermute | solution.py:356
  86.7 24.4 %collective-permute-start.15 = (bf16[256,384]{1,0:T(8,128)(2,1)}, bf16[256,384]{1,0:T(8,128)(2,1)S(1)}, u32[]{:S(2)}, u32[]{:S(2)}) collective-permute-start(bf16[256,384]{1,0:T(8,128)(2,1)} %get-tuple-element.49), channel_id=1, source_target_pairs={{0,3},{4,0},{8,1},{12,2},{1,7},{5,4},{9,5},{13,6},{2,11},{6,8},{10... | collective-permute-start | bytes 589832 | tf_op jit(solution)/shard_map/ppermute | solution.py:356
  88.2 23.0 %copy-start.11 = (bf16[256,128]{1,0:T(8,128)(2,1)}, bf16[256,128]{1,0:T(8,128)(2,1)S(1)}, u32[]{:S(2)}) copy-start(bf16[256,128]{1,0:T(8,128)(2,1)S(1)} %collective-permute-done.16.refs_5_) | copy-start | bytes 196612
  88.2 14.1 %collective-permute-start.17 = (bf16[256,128]{1,0:T(8,128)(2,1)}, bf16[256,128]{1,0:T(8,128)(2,1)S(1)}, u32[]{:S(2)}, u32[]{:S(2)}) collective-permute-start(bf16[256,128]{1,0:T(8,128)(2,1)} %get-tuple-element.50.refs_4_), channel_id=1, source_target_pairs={{2,0},{3,1},{0,2},{1,3},{6,4},{7,5},{4,6},{5,7},{10,8},{11,9},{8,1... | collective-permute-start | bytes 196616 | tf_op jit(solution)/shard_map/ppermute | solution.py:45
  102.3 8.8 %collective-permute-start.18 = (bf16[256,128]{1,0:T(8,128)(2,1)}, bf16[256,128]{1,0:T(8,128)(2,1)S(1)}, u32[]{:S(2)}, u32[]{:S(2)}) collective-permute-start(bf16[256,128]{1,0:T(8,128)(2,1)} %get-tuple-element.50.refs_4_), channel_id=1, source_target_pairs={{1,0},{2,1},{3,2},{0,3},{5,4},{6,5},{7,6},{4,7},{9,8},{10,9},{11,1... | collective-permute-start | bytes 196616 | tf_op jit(solution)/shard_map/ppermute | solution.py:45
  (18 other events, 47.7 us)

commit v3 on v2

--- a/solution.py
+++ b/solution.py
@@ -1,3 +1,4 @@
+import functools
 import math
 
 import jax
@@ -30,6 +31,7 @@
 
 
 SMEM = pl.BlockSpec(memory_space=pltpu.SMEM)
+ANY = pl.BlockSpec(memory_space=pl.ANY)
 
 
 def columns_of(index, width):
@@ -49,7 +51,7 @@
     return pl.BlockSpec(block.shape, lambda *_: (0,) * len(block.shape))
 
 
-def call(kernel, out_shape, operands, flops, scratch=(), in_specs=None):
+def call(kernel, out_shape, operands, flops, scratch=(), in_specs=None, out_specs=None):
     if in_specs is None:
         in_specs = [SMEM if x.dtype == jnp.int32 else whole(x) for x in operands]
     outs = jax.tree.leaves(out_shape)
@@ -59,47 +61,27 @@
         out_shape=out_shape,
         grid=(1,),
         in_specs=in_specs,
-        out_specs=jax.tree.map(whole, out_shape),
+        out_specs=jax.tree.map(whole, out_shape) if out_specs is None else out_specs,
         scratch_shapes=list(scratch),
         compiler_params=pltpu.CompilerParams(vmem_limit_bytes=LIMIT << 20),
         cost_estimate=pl.CostEstimate(flops=flops, bytes_accessed=traffic, transcendentals=0),
     )(*operands)
 
 
-def keys_kernel(place, tokens, w_key, w_value, *refs):
-    outs, (keys, values) = refs[:HEADS], refs[HEADS:]
-    keys[...] = mm(tokens[...], w_key[...], NN).astype(BF16)
-    values[...] = mm(tokens[...], w_value[...], NN).astype(BF16)
-    for d in range(HEADS):
-        head = columns_of(lax.rem(place[1] + d, HEADS), DH)
-        outs[d][:, :DH] = keys[:, head]
-        outs[d][:, DH:] = values[:, head]
-
-
 def third(w_in, index):
     return pl.BlockSpec((w_in.shape[0], WIDTH), lambda i: (0, index))
 
 
-def project_keys(place, key_tokens, w_in):
-    rows, width = key_tokens.shape
-    return call(
-        keys_kernel,
-        [shape(rows, 2 * DH)] * HEADS,
-        (place, key_tokens, w_in, w_in),
-        4 * rows * width * WIDTH,
-        scratch=[pltpu.VMEM((rows, WIDTH), BF16)] * 2,
-        in_specs=[SMEM, whole(key_tokens), third(w_in, 1), third(w_in, 2)],
-    )
-
-
-def queries_kernel(place, crossing, home, tokens, grad, w_in, w_out, packs, *slices):
+def project_kernel(place, crossing, home, tokens, grad, w_query, w_out, key_tokens, w_key, w_value, packs, *refs):
+    slices, refs = refs[:HEADS], refs[HEADS:]
+    outs, (keys, values) = refs[:HEADS], refs[HEADS:]
     lane = lax.broadcasted_iota(jnp.int32, (MASK_ROWS, 2 * DH), 1)
     row = lax.broadcasted_iota(jnp.int32, (MASK_ROWS, 2 * DH), 0)
     mask = jnp.zeros((MASK_ROWS, 2 * DH), F32)
     for j in range(crossing.shape[1]):
         bit = jnp.where((crossing[0, j] > 0) | (home[0] == j), 1.0, 0.0)
         mask = jnp.where((lane == j) & (row == 0), bit, mask)
-    for half, product in enumerate((mm(tokens[...], w_in[...], NN), mm(grad[...], w_out[...], NT))):
+    for half, product in enumerate((mm(tokens[...], w_query[...], NN), mm(grad[...], w_out[...], NT))):
         product = product.astype(BF16)
         for h in range(HEADS):
             packs[h * PACK : h * PACK + BLOCK, half * DH : (half + 1) * DH] = product[:, h * DH : (h + 1) * DH]
@@ -109,17 +91,30 @@
         columns = columns_of(lax.rem(place[0] + d, HEADS), part)
         slices[d][:, :part] = tokens[:, columns]
         slices[d][:, part:] = grad[:, columns]
-
-
-def project_queries(place, query_tokens, out_grad, w_in, w_out, crossing, home):
+    keys[...] = mm(key_tokens[...], w_key[...], NN).astype(BF16)
+    values[...] = mm(key_tokens[...], w_value[...], NN).astype(BF16)
+    for d in range(HEADS):
+        head = columns_of(lax.rem(place[1] + d, HEADS), DH)
+        outs[d][:, :DH] = keys[:, head]
+        outs[d][:, DH:] = values[:, head]
+
+
+def project(place, query_tokens, key_tokens, out_grad, w_in, w_out, crossing, home):
     rows, width = query_tokens.shape
-    return call(
-        queries_kernel,
-        [shape(HEADS * PACK, 2 * DH)] + [shape(rows, 2 * width // HEADS)] * HEADS,
-        (place, crossing, home, query_tokens, out_grad, w_in, w_out),
-        4 * rows * width * WIDTH,
-        in_specs=[SMEM] * 3 + [whole(query_tokens), whole(out_grad), third(w_in, 0), whole(w_out)],
-    )
+    count = key_tokens.shape[0]
+    results = call(
+        project_kernel,
+        [shape(HEADS * PACK, 2 * DH)]
+        + [shape(rows, 2 * width // HEADS)] * HEADS
+        + [shape(count, 2 * DH)] * HEADS,
+        (place, crossing, home, query_tokens, out_grad, w_in, w_out, key_tokens, w_in, w_in),
+        4 * (rows + count) * width * WIDTH,
+        scratch=[pltpu.VMEM((count, WIDTH), BF16)] * 2,
+        in_specs=[SMEM] * 3
+        + [whole(query_tokens), whole(out_grad), third(w_in, 0), whole(w_out)]
+        + [whole(key_tokens), third(w_in, 1), third(w_in, 2)],
+    )
+    return results[0], results[1 : HEADS + 1], results[HEADS + 1 :]
 
 
 def side_kernel(place, key_tokens, *refs):
@@ -136,10 +131,10 @@
     return call(side_kernel, shape(key_tokens.shape[0], width), (place, key_tokens, *slices), 0)
 
 
-def attend(place, packs, kvs, back, scores, bias, q_all, g_all, emit):
-    chunk = kvs[0].shape[0]
+def attend(place, packs, kv, ready, back, scores, bias, q_all, g_all, emit):
+    keys, count = scores.shape
+    chunk = keys // HEADS
     tiles = chunk // BLOCK
-    count = HEADS * BLOCK
     scale = 1.0 / math.sqrt(DH)
     ones = jnp.ones((MASK_ROWS, BLOCK), BF16)
     for d in range(HEADS):
@@ -152,8 +147,9 @@
     g = g_all[...]
     best = jnp.full((1, count), -3e38, F32)
     for c in range(HEADS):
+        ready(c)
         first = lax.rem(place[1] - c + HEADS, HEADS) * tiles
-        raw = mm(kvs[c][:, :DH], q, NT) * scale
+        raw = mm(kv[c * chunk : (c + 1) * chunk, :DH], q, NT)
         for j in range(tiles):
             tile = raw[j * BLOCK : (j + 1) * BLOCK, :] + bias[pl.ds(first + j, 1), :]
             scores[c * chunk + j * BLOCK : c * chunk + (j + 1) * BLOCK, :] = tile
@@ -162,10 +158,10 @@
     summed = jnp.zeros((DH, count), F32)
     for c in range(HEADS):
         part = slice(c * chunk, (c + 1) * chunk)
-        weights = jnp.exp(scores[part, :] - best)
+        weights = jnp.exp2((scores[part, :] - best) * (scale * math.log2(math.e)))
         scores[part, :] = weights
         total = total + jnp.sum(weights, axis=0, keepdims=True)
-        summed = summed + mm(kvs[c][:, DH:], weights.astype(BF16), TN)
+        summed = summed + mm(kv[part, DH:], weights.astype(BF16), TN)
     share = 1.0 / total
     attended = (summed * share).astype(BF16)
     spread = jnp.sum(jnp.transpose(g.astype(F32)) * attended.astype(F32), axis=0, keepdims=True)
@@ -174,71 +170,124 @@
     for c in range(HEADS):
         part = slice(c * chunk, (c + 1) * chunk)
         probs = scores[part, :] * share
-        grad_probs = mm(kvs[c][:, DH:], g, NT)
+        grad_probs = mm(kv[part, DH:], g, NT)
         slope = (probs * (grad_probs - spread)).astype(BF16)
-        emit(c, mm(slope, q, NN), mm(probs.astype(BF16), g, NN))
-        query_sum = query_sum + mm(kvs[c][:, :DH], slope, TN)
+        emit(c, part, mm(slope, q, NN), mm(probs.astype(BF16), g, NN))
+        query_sum = query_sum + mm(kv[part, :DH], slope, TN)
     back[:, DH:] = (jnp.transpose(query_sum) * scale).astype(BF16)
 
 
-def first_kernel(place, packs, *refs):
-    kvs, (back, total, *scratch) = refs[:HEADS], refs[HEADS:]
-    chunk = kvs[0].shape[0]
-
-    def emit(c, key_step, value_step):
-        total[c * chunk : (c + 1) * chunk, :DH] = key_step
-        total[c * chunk : (c + 1) * chunk, DH:] = value_step
-
-    attend(place, packs, kvs, back, *scratch, emit)
-
-
-def middle_kernel(place, packs, *refs):
-    kvs, (before, back, total, *scratch) = refs[:HEADS], refs[HEADS:]
-    chunk = kvs[0].shape[0]
-
-    def emit(c, key_step, value_step):
-        rows = slice(c * chunk, (c + 1) * chunk)
-        total[rows, :DH] = before[rows, :DH] + key_step
-        total[rows, DH:] = before[rows, DH:] + value_step
-
-    attend(place, packs, kvs, back, *scratch, emit)
+def chunk_copies(sources, targets, sems):
+    return [pltpu.make_async_copy(a, b, sems.at[i]) for i, (a, b) in enumerate(zip(sources, targets))]
+
+
+def chunks_of(ref):
+    rows = ref.shape[0] // HEADS
+    return [ref.at[c * rows : (c + 1) * rows, :] for c in range(HEADS)]
+
+
+def planes_kernel(planes, place, *refs):
+    packs, refs = refs[:planes], refs[planes:]
+    kvs, refs = refs[:HEADS], refs[HEADS:]
+    backs, refs = refs[:planes], refs[planes:]
+    total, scores, bias, q_all, g_all, kv, sums, load_sems, store_sems = refs
+    loads = chunk_copies(kvs, chunks_of(kv), load_sems)
+    stores = chunk_copies(chunks_of(sums), chunks_of(total), store_sems)
+    for copy in loads:
+        copy.start()
+    for i in range(planes):
+
+        def ready(c):
+            if i == 0:
+                loads[c].wait()
+
+        def emit(c, rows, key_step, value_step):
+            if i == 0:
+                sums[rows, :DH] = key_step
+                sums[rows, DH:] = value_step
+            else:
+                sums[rows, :DH] += key_step
+                sums[rows, DH:] += value_step
+            if i == planes - 1:
+                stores[c].start()
+
+        attend(place, packs[i], kv, ready, backs[i], scores, bias, q_all, g_all, emit)
+    for copy in stores:
+        copy.wait()
 
 
 def last_kernel(place, packs, *refs):
-    kvs, (before, other, own_back, back, home_parts, *scratch) = refs[:HEADS], refs[HEADS:]
+    kvs, refs = refs[:HEADS], refs[HEADS:]
+    even_hbm, odd_hbm, own_back, back, home_parts, scores, bias, q_all, g_all, kv, even, odd, *sems = refs
     chunk = kvs[0].shape[0]
     scale = 1.0 / math.sqrt(DH)
-
-    def emit(c, key_step, value_step):
-        rows = slice(c * chunk, (c + 1) * chunk)
+    loads = chunk_copies(kvs, chunks_of(kv), sems[0])
+    evens = chunk_copies(chunks_of(even_hbm), chunks_of(even), sems[1])
+    odds = chunk_copies(chunks_of(odd_hbm), chunks_of(odd), sems[2])
+    for copy in loads + evens + odds:
+        copy.start()
+
+    def ready(c):
+        loads[c].wait()
+
+    def emit(c, rows, key_step, value_step):
+        evens[c].wait()
+        odds[c].wait()
         start = lax.rem(place[1] - c + HEADS, HEADS) * (chunk + BLOCK)
         out = pl.ds(pl.multiple_of(start, BLOCK), chunk)
-        key_sum = (before[rows, :DH] + key_step) + other[rows, :DH]
+        key_sum = (even[rows, :DH] + key_step) + odd[rows, :DH]
         home_parts[out, :DH] = (key_sum * scale).astype(BF16)
-        home_parts[out, DH:] = ((before[rows, DH:] + value_step) + other[rows, DH:]).astype(BF16)
-
-    attend(place, packs, kvs, back, *scratch, emit)
+        home_parts[out, DH:] = ((even[rows, DH:] + value_step) + odd[rows, DH:]).astype(BF16)
+
+    attend(place, packs, kv, ready, back, scores, bias, q_all, g_all, emit)
     for h in range(HEADS):
         start = h * (chunk + BLOCK) + chunk
         home_parts[start : start + BLOCK, :] = own_back[h * BLOCK : (h + 1) * BLOCK, :]
 
 
-def attention(kernel, place, packs, kvs, extra):
+def attention_scratch(kvs):
+    keys = HEADS * kvs[0].shape[0]
+    count = HEADS * BLOCK
+    return [
+        pltpu.VMEM((keys, count), F32),
+        pltpu.VMEM((BLOCK, count), F32),
+        pltpu.VMEM((count, DH), BF16),
+        pltpu.VMEM((count, DH), BF16),
+        pltpu.VMEM((keys, 2 * DH), BF16),
+        pltpu.VMEM((keys, 2 * DH), F32),
+    ]
+
+
+def plane_attention(place, packs, kvs):
+    planes = len(packs)
+    keys = HEADS * kvs[0].shape[0]
+    count = HEADS * BLOCK
+    backs = [shape(count, 2 * DH)] * planes
+    *backs, total = call(
+        functools.partial(planes_kernel, planes),
+        backs + [shape(keys, 2 * DH, F32)],
+        (place, *packs, *kvs),
+        12 * planes * keys * count * DH,
+        scratch=attention_scratch(kvs) + [pltpu.SemaphoreType.DMA((HEADS,))] * 2,
+        in_specs=[SMEM] + [whole(x) for x in packs] + [ANY] * HEADS,
+        out_specs=[whole(x) for x in backs] + [ANY],
+    )
+    return backs, total
+
+
+def last_attention(place, packs, kvs, even, odd, own_back):
     chunk = kvs[0].shape[0]
     keys = HEADS * chunk
     count = HEADS * BLOCK
-    last = shape(HEADS * (chunk + BLOCK), 2 * DH) if len(extra) == 3 else shape(keys, 2 * DH, F32)
     return call(
-        kernel,
-        [shape(count, 2 * DH), last],
-        (place, packs, *kvs, *extra),
+        last_kernel,
+        [shape(count, 2 * DH), shape(HEADS * (chunk + BLOCK), 2 * DH)],
+        (place, packs, *kvs, even, odd, own_back),
         12 * keys * count * DH,
-        scratch=[
-            pltpu.VMEM((keys, count), F32),
-            pltpu.VMEM((BLOCK, count), F32),
-            pltpu.VMEM((count, DH), BF16),
-            pltpu.VMEM((count, DH), BF16),
-        ],
+        scratch=attention_scratch(kvs)
+        + [pltpu.VMEM((keys, 2 * DH), F32)]
+        + [pltpu.SemaphoreType.DMA((HEADS,))] * 3,
+        in_specs=[SMEM, whole(packs)] + [ANY] * (HEADS + 2) + [whole(own_back)],
     )
 
 
@@ -331,17 +380,15 @@
 def head_body(query_tokens, key_tokens, w_in, w_out, out_grad, crossing, home):
     place = jnp.stack([lax.axis_index("stand"), lax.axis_index("soil")]).astype(jnp.int32)
     distances = range(1, HEADS)
-    packs, *slices = project_queries(place, query_tokens, out_grad, w_in, w_out, crossing, home)
+    packs, slices, kvs = project(place, query_tokens, key_tokens, out_grad, w_in, w_out, crossing, home)
     packs = swapped(packs, "soil")
-    kvs = project_keys(place, key_tokens, w_in)
     kvs = [kvs[0]] + [sent(kvs[d], "soil", d) for d in distances]
     slices = [slices[0]] + [sent(slices[d], "stand", d) for d in distances]
     planes = spread_to(packs, "stand")
     sides = spread_to(joined(place, key_tokens, slices), "soil")
-    back_0, even = attention(first_kernel, place, planes[0], kvs, ())
-    back_1, odd = attention(first_kernel, place, planes[1], kvs, ())
-    back_3, odd = attention(middle_kernel, place, planes[3], kvs, (odd,))
-    back_2, home_parts = attention(last_kernel, place, planes[2], kvs, (even, odd, back_0))
+    (back_0,), even = plane_attention(place, planes[:1], kvs)
+    (back_1, back_3), odd = plane_attention(place, [planes[1], planes[3]], kvs)
+    back_2, home_parts = last_attention(place, planes[2], kvs, even, odd, back_0)
     inner, outer = weights_of(place, home_parts, [back_0, back_1, back_2, back_3], sides)
     home_parts = swapped(home_parts, "soil")
     key_grad, output, query_grad = home_outputs(home_parts, w_in, w_out)
@@ -354,6 +401,7 @@
             for soil in range(HEADS)
         ]
         crosswise.append(lax.ppermute(inner, ("soil", "stand"), route))
+    crosswise[0] = after(crosswise[0], key_grad)
     w_in_grad, w_out_grad = place_weights(place, crosswise, outer)
     return (output, query_grad, key_grad, w_in_grad, w_out_grad)
 

time: 124 us -> 114 us (0.919)
  the two profiles are of different devices: /device:TPU:14 before, /device:TPU:0 now
where the time goes in v3:
time: 114 us
  Pallas kernels  48.5 us (43%)
  starting transfers between devices  40 us (35%)
  waiting for transfers between devices  17.4 us (15%)
  local copies, waits for them, and re-layouts  5.72 us (5%)
  between operations  1.48 us (1%)
    pallas_call x8, Pallas kernels, call(): pl.pallas_call(kernel, out_shape=out_shape, grid=(1,), in_specs=in_specs,...  48.5 us
    ppermute x15, starting transfers between devices, sent(): return lax.ppermute(block, axis, step_from(axis, distance))  25.1 us
    ppermute x15, waiting for transfers between devices, sent(): return lax.ppermute(block, axis, step_from(axis, distance))  17.3 us
    ppermute x4, starting transfers between devices, head_body(): crosswise.append(lax.ppermute(inner, ('soil', 'stand'), route))  7.87 us
    all_to_all x2, starting transfers between devices, swapped(): return lax.all_to_all(block, axis, 0, 0, tiled=True)  7 us
    unnamed x40, local copies, waits for them, and re-layouts  5.72 us
  transfers between devices with their start and end apart: 21, of which 3 were waited for; matrix products, arithmetic and copies ran while one was open for 0% of the time, Pallas kernels for 35%

profile of v3, /device:TPU:0, one launch (start us, length us, event | category | flops | bytes accessed | tf_op | source)
XLA Modules:
  0.0 113.7 jit_solution(9909451110090330784)
XLA Ops:
  1.9 5.8 %shard_map.110 = (bf16[576,256]{1,0:T(8,128)(2,1)}, bf16[128,512]{1,0:T(8,128)(2,1)}, bf16[128,512]{1,0:T(8,128)(2,1)}, bf16[128,512]{1,0:T(8,128)(2,1)}, bf16[1...) custom-call(s32[2]{0:T(128)} %pad_add_fusion.place, ...), custom_call_target="tpu_custom_call" | custom-call | flops 1342177280 | bytes 13926438 | tf_op jit(solution)/shard_map/pallas_call | solution.py:59
  7.8 3.0 %collective-permute-start.6 = (bf16[128,512]{1,0:T(8,128)(2,1)}, bf16[128,512]{1,0:T(8,128)(2,1)S(1)}, u32[]{:S(2)}, u32[]{:S(2)}) collective-permute-start(bf16[128,512]{1,0:T(8,128)(2,1)} %get-tuple-element.45), channel_id=1, source_target_pairs={{3,0},{0,1},{1,2},{2,3},{7,4},{4,5},{5,6},{6,7},{11,8},{8,9},{9,10... | collective-permute-start | bytes 393224 | tf_op jit(solution)/shard_map/ppermute | solution.py:47
  10.8 3.5 %all-to-all-start = ((bf16[4,144,256]{2,1,0:T(8,128)(2,1)}), bf16[4,144,256]{2,1,0:T(8,128)(2,1)S(1)}, u32[]{:S(2)}, u32[]{:S(2)}) async-start(bf16[4,144,256]{2,1,0:T(8,128)(2,1)} %bitcast.12), calls=%async_computation | async-start | bytes 589824 | tf_op jit(solution)/shard_map/all_to_all | solution.py:373
  14.2 2.7 %collective-permute-start.7 = (bf16[128,512]{1,0:T(8,128)(2,1)}, bf16[128,512]{1,0:T(8,128)(2,1)S(1)}, u32[]{:S(2)}, u32[]{:S(2)}) collective-permute-start(bf16[128,512]{1,0:T(8,128)(2,1)} %get-tuple-element.46), channel_id=1, source_target_pairs={{2,0},{3,1},{0,2},{1,3},{6,4},{7,5},{4,6},{5,7},{10,8},{11,9},{8,1... | collective-permute-start | bytes 393224 | tf_op jit(solution)/shard_map/ppermute | solution.py:47
  18.2 2.0 %collective-permute-start.2 = (bf16[512,256]{1,0:T(8,128)(2,1)}, bf16[512,256]{1,0:T(8,128)(2,1)S(1)}, u32[]{:S(2)}, u32[]{:S(2)}) collective-permute-start(bf16[512,256]{1,0:T(8,128)(2,1)} %get-tuple-element.32), channel_id=1, source_target_pairs={{8,0},{12,4},{0,8},{4,12},{9,1},{13,5},{1,9},{5,13},{10,2},{14,6},... | collective-permute-start | bytes 786440 | tf_op jit(solution)/shard_map/ppermute | solution.py:47
  21.6 2.9 %collective-permute-done.7.refs_2_ = bf16[128,512]{1,0:T(8,128)(2,1)S(1)} collective-permute-done((bf16[128,512]{1,0:T(8,128)(2,1)}, bf16[128,512]{1,0:T(8,128)(2,1)S(1)}, u32[]{:S(2)}, u32[]{:S(2)}) %collective-permute-start.7) | collective-permute-done | bytes 131104 | tf_op jit(solution)/shard_map/ppermute | solution.py:47
  24.5 1.7 %collective-permute-start.4 = (bf16[576,256]{1,0:T(8,128)(2,1)S(1)}, bf16[576,256]{1,0:T(8,128)(2,1)S(1)}, u32[]{:S(2)}, u32[]{:S(2)}) collective-permute-start(bf16[576,256]{1,0:T(8,128)(2,1)S(1)} %bitcast.8), channel_id=1, source_target_pairs={{3,0},{0,1},{1,2},{2,3},{7,4},{4,5},{5,6},{6,7},{11,8},{8,9},{9,10... | collective-permute-start | bytes 884744 | tf_op jit(solution)/shard_map/ppermute | solution.py:47
  26.2 2.8 %collective-permute-start.5 = (bf16[576,256]{1,0:T(8,128)(2,1)S(1)}, bf16[576,256]{1,0:T(8,128)(2,1)S(1)}, u32[]{:S(2)}, u32[]{:S(2)}) collective-permute-start(bf16[576,256]{1,0:T(8,128)(2,1)S(1)} %bitcast.9), channel_id=1, source_target_pairs={{1,0},{2,1},{3,2},{0,3},{5,4},{6,5},{7,6},{4,7},{9,8},{10,9},{11,1... | collective-permute-start | bytes 884744 | tf_op jit(solution)/shard_map/ppermute | solution.py:47
  29.1 2.3 %shard_map.115.refs_4_ = bf16[512,768]{1,0:T(8,128)(2,1)} custom-call(s32[2]{0:T(128)} %pad_add_fusion.place, bf16[512,1024]{1,0:T(8,128)(2,1)} %key_tokens.3, bf16[128,512]{1,0:T(8,128)(2,1)} %get-tuple-element.44.refs_0_, bf16[128,512]{1,0:T(8,128)(2,1)} %copy-done.8, bf16[128,512]{1,0:T(8,128)(2,1)} %copy-done.9, bf16[128,512]{1,0:T(8,128)(2,1)} %copy-done.10), custom_call_target="tpu_custom_call" | custom-call | bytes 2359300 | tf_op jit(solution)/shard_map/pallas_call | solution.py:59
  31.4 1.9 %collective-permute-start.10 = (bf16[512,768]{1,0:T(8,128)(2,1)}, bf16[512,768]{1,0:T(8,128)(2,1)S(1)}, u32[]{:S(2)}, u32[]{:S(2)}) collective-permute-start(bf16[512,768]{1,0:T(8,128)(2,1)} %shard_map.115.refs_4_), channel_id=1, source_target_pairs={{8,0},{12,4},{0,8},{4,12},{9,1},{13,5},{1,9},{5,13},{10,2},{14,6},... | collective-permute-start | bytes 2359304 | tf_op jit(solution)/shard_map/ppermute | solution.py:47
  34.5 7.7 %shard_map.111 = (bf16[512,256]{1,0:T(8,128)(2,1)}, f32[2048,256]{1,0:T(8,128)}) custom-call(s32[2]{0:T(128)} %pad_add_fusion.place, bf16[576,256]{1,0:T(8,128)(2,1)} %bitcast.10, bf16[512,256]{1,0:T(8,128)(2,1)} %get-tuple-element.30.refs_1_.refs_2_.refs_0_, bf16[512,256]{1,0:T(8,128)(2,1)} %copy-done.17, bf16[512,256]{1,0:T(8,128)(2,1)} %copy-done.18, ...), custom_call_target="tpu_custom_call" | custom-call | flops 1610612736 | bytes 2654212 | tf_op jit(solution)/shard_map/pallas_call | solution.py:59
  43.8 11.5 %shard_map.112 = (bf16[512,256]{1,0:T(8,128)(2,1)}, bf16[512,256]{1,0:T(8,128)(2,1)}, f32[2048,256]{1,0:T(8,128)}) custom-call(s32[2]{0:T(128)} %pad_add_fusion.place, bf16[576,256]{1,0:T(8,128)(2,1)} %copy-done.14, bf16[576,256]{1,0:T(8,128)(2,1)} %copy-done.15, bf16[512,256]{1,0:T(8,128)(2,1)} %get-tuple-element.30.refs_1_.refs_2_.refs_0_, ...), custom_call_target="tpu_custom_call" | custom-call | flops 3221225472 | bytes 3211268 | tf_op jit(solution)/shard_map/pallas_call | solution.py:59
  55.3 3.1 %collective-permute-done.packs = bf16[576,256]{1,0:T(8,128)(2,1)S(1)} collective-permute-done((bf16[576,256]{1,0:T(8,128)(2,1)}, bf16[576,256]{1,0:T(8,128)(2,1)S(1)}, u32[]{:S(2)}, u32[]{:S(2)}) %collective-permute-start) | collective-permute-done | bytes 294944 | tf_op jit(solution)/shard_map/ppermute | solution.py:47
  59.1 9.1 %shard_map.113 = (bf16[512,256]{1,0:T(8,128)(2,1)}, bf16[2560,256]{1,0:T(8,128)(2,1)}) custom-call(s32[2]{0:T(128)} %pad_add_fusion.place, bf16[576,256]{1,0:T(8,128)(2,1)} %copy-done.16, bf16[512,256]{1,0:T(8,128)(2,1)} %get-tuple-element.30.refs_1_.refs_2_.refs_0_, bf16[512,256]{1,0:T(8,128)(2,1)} %copy-done.17, bf16[512,256]{1,0:T(8,128)(2,1)} %copy-done.18, ...), custom_call_target="tpu_custom_call" | custom-call | flops 1610612736 | bytes 5275652 | tf_op jit(solution)/shard_map/pallas_call | solution.py:59
  68.1 3.6 %all-to-all-start.1 = ((bf16[4,640,256]{2,1,0:T(8,128)(2,1)}), bf16[4,640,256]{2,1,0:T(8,128)(2,1)S(1)}, u32[]{:S(2)}, u32[]{:S(2)}) async-start(bf16[4,640,256]{2,1,0:T(8,128)(2,1)} %bitcast.6), calls=%async_computation.1 | async-start | bytes 2621440 | tf_op jit(solution)/shard_map/all_to_all | solution.py:373
  72.9 4.2 %shard_map.116 = (bf16[256,384]{1,0:T(8,128)(2,1)}, bf16[256,128]{1,0:T(8,128)(2,1)}) custom-call(s32[2]{0:T(128)} %pad_add_fusion.place, bf16[2560,256]{1,0:T(8,128)(2,1)} %get-tuple-element.37.home_parts, bf16[512,256]{1,0:T(8,128)(2,1)} %get-tuple-element.36.refs_6_.refs_0_, bf16[512,256]{1,0:T(8,128)(2,1)} %get-tuple-element.41.refs_1_, ...), custom_call_target="tpu_custom_call" | custom-call | flops 536870912 | bytes 5767172 | tf_op jit(solution)/shard_map/pallas_call | solution.py:59
  77.1 1.6 %collective-permute-start.12 = (bf16[256,384]{1,0:T(8,128)(2,1)}, bf16[256,384]{1,0:T(8,128)(2,1)S(1)}, u32[]{:S(2)}, u32[]{:S(2)}) collective-permute-start(bf16[256,384]{1,0:T(8,128)(2,1)} %get-tuple-element.48), channel_id=1, source_target_pairs={{0,0},{4,1},{8,2},{12,3},{1,4},{5,5},{9,6},{13,7},{2,8},{6,9},{10,... | collective-permute-start | bytes 589832 | tf_op jit(solution)/shard_map/ppermute | solution.py:403
  78.7 2.5 %collective-permute-start.13 = (bf16[256,384]{1,0:T(8,128)(2,1)}, bf16[256,384]{1,0:T(8,128)(2,1)S(1)}, u32[]{:S(2)}, u32[]{:S(2)}) collective-permute-start(bf16[256,384]{1,0:T(8,128)(2,1)} %get-tuple-element.48), channel_id=1, source_target_pairs={{0,1},{4,2},{8,3},{12,0},{1,5},{5,6},{9,7},{13,4},{2,9},{6,10},{10... | collective-permute-start | bytes 589832 | tf_op jit(solution)/shard_map/ppermute | solution.py:403
  81.2 2.3 %collective-permute-start.14 = (bf16[256,384]{1,0:T(8,128)(2,1)}, bf16[256,384]{1,0:T(8,128)(2,1)S(1)}, u32[]{:S(2)}, u32[]{:S(2)}) collective-permute-start(bf16[256,384]{1,0:T(8,128)(2,1)} %get-tuple-element.48), channel_id=1, source_target_pairs={{0,2},{4,3},{8,0},{12,1},{1,6},{5,7},{9,4},{13,5},{2,10},{6,11},{1... | collective-permute-start | bytes 589832 | tf_op jit(solution)/shard_map/ppermute | solution.py:403
  83.5 1.5 %collective-permute-start.15 = (bf16[256,384]{1,0:T(8,128)(2,1)}, bf16[256,384]{1,0:T(8,128)(2,1)S(1)}, u32[]{:S(2)}, u32[]{:S(2)}) collective-permute-start(bf16[256,384]{1,0:T(8,128)(2,1)} %get-tuple-element.48), channel_id=1, source_target_pairs={{0,3},{4,0},{8,1},{12,2},{1,7},{5,4},{9,5},{13,6},{2,11},{6,8},{10... | collective-permute-start | bytes 589832 | tf_op jit(solution)/shard_map/ppermute | solution.py:403
  86.4 11.4 %collective-permute-done.16.refs_5_ = bf16[256,128]{1,0:T(8,128)(2,1)S(1)} collective-permute-done((bf16[256,128]{1,0:T(8,128)(2,1)}, bf16[256,128]{1,0:T(8,128)(2,1)S(1)}, u32[]{:S(2)}, u32[]{:S(2)}) %collective-permute-start.16) | collective-permute-done | bytes 65568 | tf_op jit(solution)/shard_map/ppermute | solution.py:47
  97.7 5.0 %collective-permute-start.17 = (bf16[256,128]{1,0:T(8,128)(2,1)}, bf16[256,128]{1,0:T(8,128)(2,1)S(1)}, u32[]{:S(2)}, u32[]{:S(2)}) collective-permute-start(bf16[256,128]{1,0:T(8,128)(2,1)} %get-tuple-element.50.refs_4_), channel_id=1, source_target_pairs={{2,0},{3,1},{0,2},{1,3},{6,4},{7,5},{4,6},{5,7},{10,8},{11,9},{8,1... | collective-permute-start | bytes 196616 | tf_op jit(solution)/shard_map/ppermute | solution.py:47
  104.3 5.0 %shard_map.114 = (bf16[512,1024]{1,0:T(8,128)(2,1)}, bf16[128,1024]{1,0:T(8,128)(2,1)}, bf16[128,1024]{1,0:T(8,128)(2,1)}) custom-call(bf16[2560,256]{1,0:T(8,128)(2,1)} %bitcast.7, bf16[1024,1536]{1,0:T(8,128)(2,1)} %w_value.3, bf16[1024,1536]{1,0:T(8,128)(2,1)} %w_value.3, bf16[1024,1536]{1,0:T(8,128)(2,1)} %w_value.3, bf16[512,1024]{1,0:T(8,128)(2,1)} %w_out.3), custom_call_target="tpu_custom_call" | custom-call | flops 1342177280 | bytes 13369344 | tf_op jit(solution)/shard_map/pallas_call | solution.py:59
  110.8 2.8 %shard_map.117 = (f32[256,1536]{1,0:T(8,128)}, f32[128,1024]{1,0:T(8,128)}) custom-call(s32[2]{0:T(128)} %pad_add_fusion.place, bf16[256,384]{1,0:T(8,128)(2,1)} %copy-done.4, bf16[256,384]{1,0:T(8,128)(2,1)} %copy-done.5, bf16[256,384]{1,0:T(8,128)(2,1)} %copy-done.6, bf16[256,384]{1,0:T(8,128)(2,1)} %copy-done.7, ...), custom_call_target="tpu_custom_call" | custom-call | flops 524288 | bytes 2097156 | tf_op jit(solution)/shard_map/pallas_call | solution.py:59
  (67 shorter events, 12.5 us)
Async XLA Ops:
  7.8 12.4 %collective-permute-start.6 = (bf16[128,512]{1,0:T(8,128)(2,1)}, bf16[128,512]{1,0:T(8,128)(2,1)S(1)}, u32[]{:S(2)}, u32[]{:S(2)}) collective-permute-start(bf16[128,512]{1,0:T(8,128)(2,1)} %get-tuple-element.45), channel_id=1, source_target_pairs={{3,0},{0,1},{1,2},{2,3},{7,4},{4,5},{5,6},{6,7},{11,8},{8,9},{9,10... | collective-permute-start | bytes 393224 | tf_op jit(solution)/shard_map/ppermute | solution.py:47
  10.8 13.8 %all-to-all-start = ((bf16[4,144,256]{2,1,0:T(8,128)(2,1)}), bf16[4,144,256]{2,1,0:T(8,128)(2,1)S(1)}, u32[]{:S(2)}, u32[]{:S(2)}) async-start(bf16[4,144,256]{2,1,0:T(8,128)(2,1)} %bitcast.12), calls=%async_computation | async-start | bytes 589824 | tf_op jit(solution)/shard_map/all_to_all | solution.py:373
  14.2 10.3 %collective-permute-start.7 = (bf16[128,512]{1,0:T(8,128)(2,1)}, bf16[128,512]{1,0:T(8,128)(2,1)S(1)}, u32[]{:S(2)}, u32[]{:S(2)}) collective-permute-start(bf16[128,512]{1,0:T(8,128)(2,1)} %get-tuple-element.46), channel_id=1, source_target_pairs={{2,0},{3,1},{0,2},{1,3},{6,4},{7,5},{4,6},{5,7},{10,8},{11,9},{8,1... | collective-permute-start | bytes 393224 | tf_op jit(solution)/shard_map/ppermute | solution.py:47
  16.9 9.3 %collective-permute-start.8 = (bf16[128,512]{1,0:T(8,128)(2,1)}, bf16[128,512]{1,0:T(8,128)(2,1)S(1)}, u32[]{:S(2)}, u32[]{:S(2)}) collective-permute-start(bf16[128,512]{1,0:T(8,128)(2,1)} %get-tuple-element.47), channel_id=1, source_target_pairs={{1,0},{2,1},{3,2},{0,3},{5,4},{6,5},{7,6},{4,7},{9,8},{10,9},{11,1... | collective-permute-start | bytes 393224 | tf_op jit(solution)/shard_map/ppermute | solution.py:47
  18.2 13.2 %collective-permute-start.1 = (bf16[512,256]{1,0:T(8,128)(2,1)}, bf16[512,256]{1,0:T(8,128)(2,1)S(1)}, u32[]{:S(2)}, u32[]{:S(2)}) collective-permute-start(bf16[512,256]{1,0:T(8,128)(2,1)} %get-tuple-element.31), channel_id=1, source_target_pairs={{12,0},{0,4},{4,8},{8,12},{13,1},{1,5},{5,9},{9,13},{14,2},{2,6},{... | collective-permute-start | bytes 786440 | tf_op jit(solution)/shard_map/ppermute | solution.py:47
  18.2 15.1 %collective-permute-start.2 = (bf16[512,256]{1,0:T(8,128)(2,1)}, bf16[512,256]{1,0:T(8,128)(2,1)S(1)}, u32[]{:S(2)}, u32[]{:S(2)}) collective-permute-start(bf16[512,256]{1,0:T(8,128)(2,1)} %get-tuple-element.32), channel_id=1, source_target_pairs={{8,0},{12,4},{0,8},{4,12},{9,1},{13,5},{1,9},{5,13},{10,2},{14,6},... | collective-permute-start | bytes 786440 | tf_op jit(solution)/shard_map/ppermute | solution.py:47
  20.2 8.9 %copy-start.8 = (bf16[128,512]{1,0:T(8,128)(2,1)}, bf16[128,512]{1,0:T(8,128)(2,1)S(1)}, u32[]{:S(2)}) copy-start(bf16[128,512]{1,0:T(8,128)(2,1)S(1)} %collective-permute-done.6.refs_1_) | copy-start | bytes 393220
  20.2 13.6 %collective-permute-start.3 = (bf16[512,256]{1,0:T(8,128)(2,1)}, bf16[512,256]{1,0:T(8,128)(2,1)S(1)}, u32[]{:S(2)}, u32[]{:S(2)}) collective-permute-start(bf16[512,256]{1,0:T(8,128)(2,1)} %get-tuple-element.33), channel_id=1, source_target_pairs={{4,0},{8,4},{12,8},{0,12},{5,1},{9,5},{13,9},{1,13},{6,2},{10,6},{... | collective-permute-start | bytes 786440 | tf_op jit(solution)/shard_map/ppermute | solution.py:47
  24.5 9.3 %copy-start.3 = (bf16[4,144,256]{2,1,0:T(8,128)(2,1)}, bf16[4,144,256]{2,1,0:T(8,128)(2,1)S(1)}, u32[]{:S(2)}) copy-start(bf16[4,144,256]{2,1,0:T(8,128)(2,1)S(1)} %all-to-all-done) | copy-start | bytes 884740
  24.5 17.6 %collective-permute-start.4 = (bf16[576,256]{1,0:T(8,128)(2,1)S(1)}, bf16[576,256]{1,0:T(8,128)(2,1)S(1)}, u32[]{:S(2)}, u32[]{:S(2)}) collective-permute-start(bf16[576,256]{1,0:T(8,128)(2,1)S(1)} %bitcast.8), channel_id=1, source_target_pairs={{3,0},{0,1},{1,2},{2,3},{7,4},{4,5},{5,6},{6,7},{11,8},{8,9},{9,10... | collective-permute-start | bytes 884744 | tf_op jit(solution)/shard_map/ppermute | solution.py:47
  26.2 16.8 %collective-permute-start.5 = (bf16[576,256]{1,0:T(8,128)(2,1)S(1)}, bf16[576,256]{1,0:T(8,128)(2,1)S(1)}, u32[]{:S(2)}, u32[]{:S(2)}) collective-permute-start(bf16[576,256]{1,0:T(8,128)(2,1)S(1)} %bitcast.9), channel_id=1, source_target_pairs={{1,0},{2,1},{3,2},{0,3},{5,4},{6,5},{7,6},{4,7},{9,8},{10,9},{11,1... | collective-permute-start | bytes 884744 | tf_op jit(solution)/shard_map/ppermute | solution.py:47
  31.4 40.3 %collective-permute-start.10 = (bf16[512,768]{1,0:T(8,128)(2,1)}, bf16[512,768]{1,0:T(8,128)(2,1)S(1)}, u32[]{:S(2)}, u32[]{:S(2)}) collective-permute-start(bf16[512,768]{1,0:T(8,128)(2,1)} %shard_map.115.refs_4_), channel_id=1, source_target_pairs={{8,0},{12,4},{0,8},{4,12},{9,1},{13,5},{1,9},{5,13},{10,2},{14,6},... | collective-permute-start | bytes 2359304 | tf_op jit(solution)/shard_map/ppermute | solution.py:47
  33.3 38.4 %collective-permute-start.11 = (bf16[512,768]{1,0:T(8,128)(2,1)}, bf16[512,768]{1,0:T(8,128)(2,1)S(1)}, u32[]{:S(2)}, u32[]{:S(2)}) collective-permute-start(bf16[512,768]{1,0:T(8,128)(2,1)} %shard_map.115.refs_4_), channel_id=1, source_target_pairs={{4,0},{8,4},{12,8},{0,12},{5,1},{9,5},{13,9},{1,13},{6,2},{10,6},{... | collective-permute-start | bytes 2359304 | tf_op jit(solution)/shard_map/ppermute | solution.py:47
  33.8 38.0 %collective-permute-start.9 = (bf16[512,768]{1,0:T(8,128)(2,1)}, bf16[512,768]{1,0:T(8,128)(2,1)}, u32[]{:S(2)}, u32[]{:S(2)}) collective-permute-start(bf16[512,768]{1,0:T(8,128)(2,1)} %shard_map.115.refs_4_), channel_id=1, source_target_pairs={{12,0},{0,4},{4,8},{8,12},{13,1},{1,5},{5,9},{9,13},{14,2},{2,6},{... | collective-permute-start | bytes 2359304 | tf_op jit(solution)/shard_map/ppermute | solution.py:47
  42.2 16.1 %collective-permute-start = (bf16[576,256]{1,0:T(8,128)(2,1)}, bf16[576,256]{1,0:T(8,128)(2,1)S(1)}, u32[]{:S(2)}, u32[]{:S(2)}) collective-permute-start(bf16[576,256]{1,0:T(8,128)(2,1)} %bitcast.11), channel_id=1, source_target_pairs={{2,0},{3,1},{0,2},{1,3},{6,4},{7,5},{4,6},{5,7},{10,8},{11,9},{8,1... | collective-permute-start | bytes 884744 | tf_op jit(solution)/shard_map/ppermute | solution.py:47
  68.1 35.1 %all-to-all-start.1 = ((bf16[4,640,256]{2,1,0:T(8,128)(2,1)}), bf16[4,640,256]{2,1,0:T(8,128)(2,1)S(1)}, u32[]{:S(2)}, u32[]{:S(2)}) async-start(bf16[4,640,256]{2,1,0:T(8,128)(2,1)} %bitcast.6), calls=%async_computation.1 | async-start | bytes 2621440 | tf_op jit(solution)/shard_map/all_to_all | solution.py:373
  77.1 25.6 %collective-permute-start.12 = (bf16[256,384]{1,0:T(8,128)(2,1)}, bf16[256,384]{1,0:T(8,128)(2,1)S(1)}, u32[]{:S(2)}, u32[]{:S(2)}) collective-permute-start(bf16[256,384]{1,0:T(8,128)(2,1)} %get-tuple-element.48), channel_id=1, source_target_pairs={{0,0},{4,1},{8,2},{12,3},{1,4},{5,5},{9,6},{13,7},{2,8},{6,9},{10,... | collective-permute-start | bytes 589832 | tf_op jit(solution)/shard_map/ppermute | solution.py:403
  78.7 30.7 %collective-permute-start.13 = (bf16[256,384]{1,0:T(8,128)(2,1)}, bf16[256,384]{1,0:T(8,128)(2,1)S(1)}, u32[]{:S(2)}, u32[]{:S(2)}) collective-permute-start(bf16[256,384]{1,0:T(8,128)(2,1)} %get-tuple-element.48), channel_id=1, source_target_pairs={{0,1},{4,2},{8,3},{12,0},{1,5},{5,6},{9,7},{13,4},{2,9},{6,10},{10... | collective-permute-start | bytes 589832 | tf_op jit(solution)/shard_map/ppermute | solution.py:403
  81.2 28.2 %collective-permute-start.14 = (bf16[256,384]{1,0:T(8,128)(2,1)}, bf16[256,384]{1,0:T(8,128)(2,1)S(1)}, u32[]{:S(2)}, u32[]{:S(2)}) collective-permute-start(bf16[256,384]{1,0:T(8,128)(2,1)} %get-tuple-element.48), channel_id=1, source_target_pairs={{0,2},{4,3},{8,0},{12,1},{1,6},{5,7},{9,4},{13,5},{2,10},{6,11},{1... | collective-permute-start | bytes 589832 | tf_op jit(solution)/shard_map/ppermute | solution.py:403
  83.5 25.9 %collective-permute-start.15 = (bf16[256,384]{1,0:T(8,128)(2,1)}, bf16[256,384]{1,0:T(8,128)(2,1)S(1)}, u32[]{:S(2)}, u32[]{:S(2)}) collective-permute-start(bf16[256,384]{1,0:T(8,128)(2,1)} %get-tuple-element.48), channel_id=1, source_target_pairs={{0,3},{4,0},{8,1},{12,2},{1,7},{5,4},{9,5},{13,6},{2,11},{6,8},{10... | collective-permute-start | bytes 589832 | tf_op jit(solution)/shard_map/ppermute | solution.py:403
  85.0 12.7 %collective-permute-start.16 = (bf16[256,128]{1,0:T(8,128)(2,1)}, bf16[256,128]{1,0:T(8,128)(2,1)S(1)}, u32[]{:S(2)}, u32[]{:S(2)}) collective-permute-start(bf16[256,128]{1,0:T(8,128)(2,1)} %get-tuple-element.50.refs_4_), channel_id=1, source_target_pairs={{3,0},{0,1},{1,2},{2,3},{7,4},{4,5},{5,6},{6,7},{11,8},{8,9},{9,10... | collective-permute-start | bytes 196616 | tf_op jit(solution)/shard_map/ppermute | solution.py:47
  97.7 11.7 %copy-start.11 = (bf16[256,128]{1,0:T(8,128)(2,1)}, bf16[256,128]{1,0:T(8,128)(2,1)S(1)}, u32[]{:S(2)}) copy-start(bf16[256,128]{1,0:T(8,128)(2,1)S(1)} %collective-permute-done.16.refs_5_) | copy-start | bytes 196612
  97.7 11.6 %collective-permute-start.17 = (bf16[256,128]{1,0:T(8,128)(2,1)}, bf16[256,128]{1,0:T(8,128)(2,1)S(1)}, u32[]{:S(2)}, u32[]{:S(2)}) collective-permute-start(bf16[256,128]{1,0:T(8,128)(2,1)} %get-tuple-element.50.refs_4_), channel_id=1, source_target_pairs={{2,0},{3,1},{0,2},{1,3},{6,4},{7,5},{4,6},{5,7},{10,8},{11,9},{8,1... | collective-permute-start | bytes 196616 | tf_op jit(solution)/shard_map/ppermute | solution.py:47
  102.7 6.7 %collective-permute-start.18 = (bf16[256,128]{1,0:T(8,128)(2,1)}, bf16[256,128]{1,0:T(8,128)(2,1)S(1)}, u32[]{:S(2)}, u32[]{:S(2)}) collective-permute-start(bf16[256,128]{1,0:T(8,128)(2,1)} %get-tuple-element.50.refs_4_), channel_id=1, source_target_pairs={{1,0},{2,1},{3,2},{0,3},{5,4},{6,5},{7,6},{4,7},{9,8},{10,9},{11,1... | collective-permute-start | bytes 196616 | tf_op jit(solution)/shard_map/ppermute | solution.py:47
  (17 other events, 26.8 us)

commit v4 on v3

--- a/solution.py
+++ b/solution.py
@@ -365,6 +365,34 @@
     )
 
 
+def finish_kernel(place, *refs):
+    pieces, refs = refs[: 2 * HEADS], refs[2 * HEADS :]
+    home, (w_in_grad, w_out_grad) = (*refs[:5], *refs[7:]), refs[5:7]
+    home_kernel(*home)
+    place_weights_kernel(place, *pieces, w_in_grad, w_out_grad)
+
+
+def finish(place, inner, outer, parts, w_in, w_out):
+    rows = inner[0].shape[0]
+    width = w_in.shape[0]
+    count = parts.shape[0] // HEADS - BLOCK
+    return call(
+        finish_kernel,
+        [
+            shape(rows, 3 * WIDTH, F32),
+            shape(DH, HEADS * rows, F32),
+            shape(count, width),
+            shape(BLOCK, width),
+            shape(BLOCK, width),
+        ],
+        (place, *inner, *outer, parts, w_in, w_in, w_in, w_out),
+        4 * (count + BLOCK) * width * WIDTH,
+        in_specs=[SMEM]
+        + [whole(x) for x in (*inner, *outer, parts)]
+        + [third(w_in, 0), third(w_in, 1), third(w_in, 2), whole(w_out)],
+    )
+
+
 def after(value, *others):
     return lax.optimization_barrier((value, *others))[0]
 
@@ -385,13 +413,13 @@
     kvs = [kvs[0]] + [sent(kvs[d], "soil", d) for d in distances]
     slices = [slices[0]] + [sent(slices[d], "stand", d) for d in distances]
     planes = spread_to(packs, "stand")
-    sides = spread_to(joined(place, key_tokens, slices), "soil")
+    side = joined(place, key_tokens, slices)
+    sides = [side, sent(side, "soil", 1), sent(after(side, planes[1]), "soil", 2), sent(side, "soil", 3)]
     (back_0,), even = plane_attention(place, planes[:1], kvs)
     (back_1, back_3), odd = plane_attention(place, [planes[1], planes[3]], kvs)
     back_2, home_parts = last_attention(place, planes[2], kvs, even, odd, back_0)
     inner, outer = weights_of(place, home_parts, [back_0, back_1, back_2, back_3], sides)
     home_parts = swapped(home_parts, "soil")
-    key_grad, output, query_grad = home_outputs(home_parts, w_in, w_out)
     outer = spread_to(outer, "stand")
     crosswise = []
     for d in range(HEADS):
@@ -400,9 +428,10 @@
             for stand in range(HEADS)
             for soil in range(HEADS)
         ]
-        crosswise.append(lax.ppermute(inner, ("soil", "stand"), route))
-    crosswise[0] = after(crosswise[0], key_grad)
-    w_in_grad, w_out_grad = place_weights(place, crosswise, outer)
+        held = inner if d < 2 else after(inner, outer[d - 1])
+        crosswise.append(lax.ppermute(held, ("soil", "stand"), route))
+    results = finish(place, crosswise, outer, home_parts, w_in, w_out)
+    w_in_grad, w_out_grad, key_grad, output, query_grad = results
     return (output, query_grad, key_grad, w_in_grad, w_out_grad)
 
 

time: 114 us -> 108 us (0.947)
  the two profiles are of different devices: /device:TPU:0 before, /device:TPU:14 now
where the time goes in v4:
time: 108 us
  Pallas kernels  47.2 us (44%)
  starting transfers between devices  31.1 us (29%)
  waiting for transfers between devices  23.7 us (22%)
  local copies, waits for them, and re-layouts  3.62 us (3%)
  between operations  1.51 us (1%)
    pallas_call x7, Pallas kernels, call(): pl.pallas_call(kernel, out_shape=out_shape, grid=(1,), in_specs=in_specs,...  47.2 us
    ppermute x15, waiting for transfers between devices, sent(): return lax.ppermute(block, axis, step_from(axis, distance))  23.7 us
    ppermute x15, starting transfers between devices, sent(): return lax.ppermute(block, axis, step_from(axis, distance))  16.4 us
    all_to_all x2, starting transfers between devices, swapped(): return lax.all_to_all(block, axis, 0, 0, tiled=True)  7.94 us
    ppermute x4, starting transfers between devices, head_body(): crosswise.append(lax.ppermute(held, ('soil', 'stand'), route))  6.73 us
    unnamed x40, local copies, waits for them, and re-layouts  3.62 us
  transfers between devices with their start and end apart: 21, of which 4 were waited for; matrix products, arithmetic and copies ran while one was open for 0% of the time, Pallas kernels for 32%

profile of v4, /device:TPU:14, one launch (start us, length us, event | category | flops | bytes accessed | tf_op | source)
XLA Modules:
  0.0 107.8 jit_solution(3326890642436449687)
XLA Ops:
  1.9 5.8 %shard_map.110 = (bf16[576,256]{1,0:T(8,128)(2,1)}, bf16[128,512]{1,0:T(8,128)(2,1)}, bf16[128,512]{1,0:T(8,128)(2,1)}, bf16[128,512]{1,0:T(8,128)(2,1)}, bf16[1...) custom-call(s32[2]{0:T(128)} %pad_add_fusion.place, ...), custom_call_target="tpu_custom_call" | custom-call | flops 1342177280 | bytes 13926438 | tf_op jit(solution)/shard_map/pallas_call | solution.py:59
  7.7 1.6 %collective-permute-start.6 = (bf16[128,512]{1,0:T(8,128)(2,1)}, bf16[128,512]{1,0:T(8,128)(2,1)S(1)}, u32[]{:S(2)}, u32[]{:S(2)}) collective-permute-start(bf16[128,512]{1,0:T(8,128)(2,1)} %get-tuple-element.44), channel_id=1, source_target_pairs={{3,0},{0,1},{1,2},{2,3},{7,4},{4,5},{5,6},{6,7},{11,8},{8,9},{9,10... | collective-permute-start | bytes 393224 | tf_op jit(solution)/shard_map/ppermute | solution.py:47
  9.3 3.9 %all-to-all-start = ((bf16[4,144,256]{2,1,0:T(8,128)(2,1)}), bf16[4,144,256]{2,1,0:T(8,128)(2,1)S(1)}, u32[]{:S(2)}, u32[]{:S(2)}) async-start(bf16[4,144,256]{2,1,0:T(8,128)(2,1)} %bitcast.12), calls=%async_computation | async-start | bytes 589824 | tf_op jit(solution)/shard_map/all_to_all | solution.py:401
  13.2 1.2 %collective-permute-start.7 = (bf16[128,512]{1,0:T(8,128)(2,1)}, bf16[128,512]{1,0:T(8,128)(2,1)S(1)}, u32[]{:S(2)}, u32[]{:S(2)}) collective-permute-start(bf16[128,512]{1,0:T(8,128)(2,1)} %get-tuple-element.45), channel_id=1, source_target_pairs={{2,0},{3,1},{0,2},{1,3},{6,4},{7,5},{4,6},{5,7},{10,8},{11,9},{8,1... | collective-permute-start | bytes 393224 | tf_op jit(solution)/shard_map/ppermute | solution.py:47
  14.4 1.8 %collective-permute-start.8 = (bf16[128,512]{1,0:T(8,128)(2,1)}, bf16[128,512]{1,0:T(8,128)(2,1)S(1)}, u32[]{:S(2)}, u32[]{:S(2)}) collective-permute-start(bf16[128,512]{1,0:T(8,128)(2,1)} %get-tuple-element.46), channel_id=1, source_target_pairs={{1,0},{2,1},{3,2},{0,3},{5,4},{6,5},{7,6},{4,7},{9,8},{10,9},{11,1... | collective-permute-start | bytes 393224 | tf_op jit(solution)/shard_map/ppermute | solution.py:47
  16.4 1.7 %collective-permute-start.3 = (bf16[512,256]{1,0:T(8,128)(2,1)}, bf16[512,256]{1,0:T(8,128)(2,1)S(1)}, u32[]{:S(2)}, u32[]{:S(2)}) collective-permute-start(bf16[512,256]{1,0:T(8,128)(2,1)} %get-tuple-element.35), channel_id=1, source_target_pairs={{4,0},{8,4},{12,8},{0,12},{5,1},{9,5},{13,9},{1,13},{6,2},{10,6},{... | collective-permute-start | bytes 786440 | tf_op jit(solution)/shard_map/ppermute | solution.py:47
  18.0 5.6 %collective-permute-done.7.refs_2_ = bf16[128,512]{1,0:T(8,128)(2,1)S(1)} collective-permute-done((bf16[128,512]{1,0:T(8,128)(2,1)}, bf16[128,512]{1,0:T(8,128)(2,1)S(1)}, u32[]{:S(2)}, u32[]{:S(2)}) %collective-permute-start.7) | collective-permute-done | bytes 131104 | tf_op jit(solution)/shard_map/ppermute | solution.py:47
  24.5 1.3 %collective-permute-start.5 = (bf16[576,256]{1,0:T(8,128)(2,1)S(1)}, bf16[576,256]{1,0:T(8,128)(2,1)S(1)}, u32[]{:S(2)}, u32[]{:S(2)}) collective-permute-start(bf16[576,256]{1,0:T(8,128)(2,1)S(1)} %bitcast.9), channel_id=1, source_target_pairs={{1,0},{2,1},{3,2},{0,3},{5,4},{6,5},{7,6},{4,7},{9,8},{10,9},{11,1... | collective-permute-start | bytes 884744 | tf_op jit(solution)/shard_map/ppermute | solution.py:47
  25.7 2.3 %shard_map.114.refs_4_ = bf16[512,768]{1,0:T(8,128)(2,1)} custom-call(s32[2]{0:T(128)} %pad_add_fusion.place, bf16[512,1024]{1,0:T(8,128)(2,1)} %key_tokens.3, bf16[128,512]{1,0:T(8,128)(2,1)} %get-tuple-element.43.refs_0_, bf16[128,512]{1,0:T(8,128)(2,1)} %copy-done.8, bf16[128,512]{1,0:T(8,128)(2,1)} %copy-done.9, bf16[128,512]{1,0:T(8,128)(2,1)} %copy-done.10), custom_call_target="tpu_custom_call" | custom-call | bytes 2359300 | tf_op jit(solution)/shard_map/pallas_call | solution.py:59
  28.1 2.1 %collective-permute-start.9 = (bf16[512,768]{1,0:T(8,128)(2,1)}, bf16[512,768]{1,0:T(8,128)(2,1)}, u32[]{:S(2)}, u32[]{:S(2)}) collective-permute-start(bf16[512,768]{1,0:T(8,128)(2,1)} %shard_map.114.refs_4_), channel_id=1, source_target_pairs={{12,0},{0,4},{4,8},{8,12},{13,1},{1,5},{5,9},{9,13},{14,2},{2,6},{... | collective-permute-start | bytes 2359304 | tf_op jit(solution)/shard_map/ppermute | solution.py:47
  30.2 1.7 %collective-permute-start = (bf16[576,256]{1,0:T(8,128)(2,1)S(1)}, bf16[576,256]{1,0:T(8,128)(2,1)S(1)}, u32[]{:S(2)}, u32[]{:S(2)}) collective-permute-start(bf16[576,256]{1,0:T(8,128)(2,1)S(1)} %bitcast.10), channel_id=1, source_target_pairs={{2,0},{3,1},{0,2},{1,3},{6,4},{7,5},{4,6},{5,7},{10,8},{11,9},{8,1... | collective-permute-start | bytes 884744 | tf_op jit(solution)/shard_map/ppermute | solution.py:47
  32.0 7.8 %shard_map.111 = (bf16[512,256]{1,0:T(8,128)(2,1)}, f32[2048,256]{1,0:T(8,128)}) custom-call(s32[2]{0:T(128)} %pad_add_fusion.place, bf16[576,256]{1,0:T(8,128)(2,1)} %bitcast.11, bf16[512,256]{1,0:T(8,128)(2,1)} %get-tuple-element.32.refs_1_.refs_2_.refs_0_, bf16[512,256]{1,0:T(8,128)(2,1)} %copy-done.17, bf16[512,256]{1,0:T(8,128)(2,1)} %copy-done.18, ...), custom_call_target="tpu_custom_call" | custom-call | flops 1610612736 | bytes 2654212 | tf_op jit(solution)/shard_map/pallas_call | solution.py:59
  39.9 1.4 %collective-permute-done.5.refs_1_ = bf16[576,256]{1,0:T(8,128)(2,1)S(1)} collective-permute-done((bf16[576,256]{1,0:T(8,128)(2,1)S(1)}, bf16[576,256]{1,0:T(8,128)(2,1)S(1)}, u32[]{:S(2)}, u32[]{:S(2)}) %collective-permute-start.5) | collective-permute-done | bytes 294944 | tf_op jit(solution)/shard_map/ppermute | solution.py:47
  42.1 11.5 %shard_map.112 = (bf16[512,256]{1,0:T(8,128)(2,1)}, bf16[512,256]{1,0:T(8,128)(2,1)}, f32[2048,256]{1,0:T(8,128)}) custom-call(s32[2]{0:T(128)} %pad_add_fusion.place, bf16[576,256]{1,0:T(8,128)(2,1)} %copy-done.14, bf16[576,256]{1,0:T(8,128)(2,1)} %copy-done.15, bf16[512,256]{1,0:T(8,128)(2,1)} %get-tuple-element.32.refs_1_.refs_2_.refs_0_, ...), custom_call_target="tpu_custom_call" | custom-call | flops 3221225472 | bytes 3211268 | tf_op jit(solution)/shard_map/pallas_call | solution.py:59
  54.3 9.1 %shard_map.113 = (bf16[512,256]{1,0:T(8,128)(2,1)}, bf16[2560,256]{1,0:T(8,128)(2,1)}) custom-call(s32[2]{0:T(128)} %pad_add_fusion.place, bf16[576,256]{1,0:T(8,128)(2,1)} %copy-done.16, bf16[512,256]{1,0:T(8,128)(2,1)} %get-tuple-element.32.refs_1_.refs_2_.refs_0_, bf16[512,256]{1,0:T(8,128)(2,1)} %copy-done.17, bf16[512,256]{1,0:T(8,128)(2,1)} %copy-done.18, ...), custom_call_target="tpu_custom_call" | custom-call | flops 1610612736 | bytes 5275652 | tf_op jit(solution)/shard_map/pallas_call | solution.py:59
  63.4 4.0 %all-to-all-start.1 = ((bf16[4,640,256]{2,1,0:T(8,128)(2,1)}), bf16[4,640,256]{2,1,0:T(8,128)(2,1)S(1)}, u32[]{:S(2)}, u32[]{:S(2)}) async-start(bf16[4,640,256]{2,1,0:T(8,128)(2,1)} %bitcast.7), calls=%async_computation.1 | async-start | bytes 2621440 | tf_op jit(solution)/shard_map/all_to_all | solution.py:401
  68.3 4.2 %shard_map.115 = (bf16[256,384]{1,0:T(8,128)(2,1)}, bf16[256,128]{1,0:T(8,128)(2,1)}) custom-call(s32[2]{0:T(128)} %pad_add_fusion.place, bf16[2560,256]{1,0:T(8,128)(2,1)} %get-tuple-element.39.home_parts, bf16[512,256]{1,0:T(8,128)(2,1)} %get-tuple-element.38.refs_6_.refs_0_, bf16[512,256]{1,0:T(8,128)(2,1)} %get-tuple-element.40.refs_1_, ...), custom_call_target="tpu_custom_call" | custom-call | flops 536870912 | bytes 5767172 | tf_op jit(solution)/shard_map/pallas_call | solution.py:59
  72.5 1.3 %collective-permute-start.16 = (bf16[256,128]{1,0:T(8,128)(2,1)}, bf16[256,128]{1,0:T(8,128)(2,1)S(1)}, u32[]{:S(2)}, u32[]{:S(2)}) collective-permute-start(bf16[256,128]{1,0:T(8,128)(2,1)} %get-tuple-element.49.refs_4_), channel_id=1, source_target_pairs={{2,0},{3,1},{0,2},{1,3},{6,4},{7,5},{4,6},{5,7},{10,8},{11,9},{8,1... | collective-permute-start | bytes 196616 | tf_op jit(solution)/shard_map/ppermute | solution.py:47
  74.6 2.2 %collective-permute-start.12 = (bf16[256,384]{1,0:T(8,128)(2,1)}, bf16[256,384]{1,0:T(8,128)(2,1)S(1)}, u32[]{:S(2)}, u32[]{:S(2)}) collective-permute-start(bf16[256,384]{1,0:T(8,128)(2,1)} %get-tuple-element.51), channel_id=1, source_target_pairs={{0,0},{4,1},{8,2},{12,3},{1,4},{5,5},{9,6},{13,7},{2,8},{6,9},{10,... | collective-permute-start | bytes 589832 | tf_op jit(solution)/shard_map/ppermute | solution.py:432
  76.9 2.5 %collective-permute-start.13 = (bf16[256,384]{1,0:T(8,128)(2,1)}, bf16[256,384]{1,0:T(8,128)(2,1)S(1)}, u32[]{:S(2)}, u32[]{:S(2)}) collective-permute-start(bf16[256,384]{1,0:T(8,128)(2,1)} %get-tuple-element.51), channel_id=1, source_target_pairs={{0,1},{4,2},{8,3},{12,0},{1,5},{5,6},{9,7},{13,4},{2,9},{6,10},{10... | collective-permute-start | bytes 589832 | tf_op jit(solution)/shard_map/ppermute | solution.py:432
  79.6 1.8 %collective-permute-start.15 = (bf16[256,384]{1,0:T(8,128)(2,1)}, bf16[256,384]{1,0:T(8,128)(2,1)S(1)}, u32[]{:S(2)}, u32[]{:S(2)}) collective-permute-start(bf16[256,384]{1,0:T(8,128)(2,1)} %get-tuple-element.51), channel_id=1, source_target_pairs={{0,2},{4,3},{8,0},{12,1},{1,6},{5,7},{9,4},{13,5},{2,10},{6,11},{1... | collective-permute-start | bytes 589832 | tf_op jit(solution)/shard_map/ppermute | solution.py:432
  81.4 2.6 %collective-permute-start.18 = (bf16[256,128]{1,0:T(8,128)(2,1)}, bf16[256,128]{1,0:T(8,128)(2,1)S(1)}, u32[]{:S(2)}, u32[]{:S(2)}) collective-permute-start(bf16[256,128]{1,0:T(8,128)(2,1)} %get-tuple-element.49.refs_4_), channel_id=1, source_target_pairs={{1,0},{2,1},{3,2},{0,3},{5,4},{6,5},{7,6},{4,7},{9,8},{10,9},{11,1... | collective-permute-start | bytes 196616 | tf_op jit(solution)/shard_map/ppermute | solution.py:47
  84.0 15.9 %collective-permute-done.18.refs_7_ = bf16[256,128]{1,0:T(8,128)(2,1)S(1)} collective-permute-done((bf16[256,128]{1,0:T(8,128)(2,1)}, bf16[256,128]{1,0:T(8,128)(2,1)S(1)}, u32[]{:S(2)}, u32[]{:S(2)}) %collective-permute-start.18) | collective-permute-done | bytes 65568 | tf_op jit(solution)/shard_map/ppermute | solution.py:47
  101.3 6.5 %shard_map.116 = (f32[256,1536]{1,0:T(8,128)}, f32[128,1024]{1,0:T(8,128)}, bf16[512,1024]{1,0:T(8,128)(2,1)}, bf16[128,1024]{1,0:T(8,128)(2,1)}, bf16[128,1024]{1,0:T(8,128)(2,1)}) custom-call(s32[2]{0:T(128)} %pad_add_fusion.place, bf16[256,384]{1,0:T(8,128)(2,1)} %copy-done.4, bf16[256,384]{1,0:T(8,128)(2,1)} %copy-done.5, bf16[256,384]{1,0:T(8,128)(2,1)} %copy-done.7, ...), custom_call_target="tpu_custom_call" | custom-call | flops 1342177280 | bytes 15466500 | tf_op jit(solution)/shard_map/pallas_call | solution.py:59
  (66 shorter events, 6.4 us)
Async XLA Ops:
  7.7 8.7 %collective-permute-start.6 = (bf16[128,512]{1,0:T(8,128)(2,1)}, bf16[128,512]{1,0:T(8,128)(2,1)S(1)}, u32[]{:S(2)}, u32[]{:S(2)}) collective-permute-start(bf16[128,512]{1,0:T(8,128)(2,1)} %get-tuple-element.44), channel_id=1, source_target_pairs={{3,0},{0,1},{1,2},{2,3},{7,4},{4,5},{5,6},{6,7},{11,8},{8,9},{9,10... | collective-permute-start | bytes 393224 | tf_op jit(solution)/shard_map/ppermute | solution.py:47
  9.3 14.4 %all-to-all-start = ((bf16[4,144,256]{2,1,0:T(8,128)(2,1)}), bf16[4,144,256]{2,1,0:T(8,128)(2,1)S(1)}, u32[]{:S(2)}, u32[]{:S(2)}) async-start(bf16[4,144,256]{2,1,0:T(8,128)(2,1)} %bitcast.12), calls=%async_computation | async-start | bytes 589824 | tf_op jit(solution)/shard_map/all_to_all | solution.py:401
  13.2 10.5 %collective-permute-start.7 = (bf16[128,512]{1,0:T(8,128)(2,1)}, bf16[128,512]{1,0:T(8,128)(2,1)S(1)}, u32[]{:S(2)}, u32[]{:S(2)}) collective-permute-start(bf16[128,512]{1,0:T(8,128)(2,1)} %get-tuple-element.45), channel_id=1, source_target_pairs={{2,0},{3,1},{0,2},{1,3},{6,4},{7,5},{4,6},{5,7},{10,8},{11,9},{8,1... | collective-permute-start | bytes 393224 | tf_op jit(solution)/shard_map/ppermute | solution.py:47
  14.4 10.0 %collective-permute-start.8 = (bf16[128,512]{1,0:T(8,128)(2,1)}, bf16[128,512]{1,0:T(8,128)(2,1)S(1)}, u32[]{:S(2)}, u32[]{:S(2)}) collective-permute-start(bf16[128,512]{1,0:T(8,128)(2,1)} %get-tuple-element.46), channel_id=1, source_target_pairs={{1,0},{2,1},{3,2},{0,3},{5,4},{6,5},{7,6},{4,7},{9,8},{10,9},{11,1... | collective-permute-start | bytes 393224 | tf_op jit(solution)/shard_map/ppermute | solution.py:47
  16.2 11.8 %collective-permute-start.1 = (bf16[512,256]{1,0:T(8,128)(2,1)}, bf16[512,256]{1,0:T(8,128)(2,1)S(1)}, u32[]{:S(2)}, u32[]{:S(2)}) collective-permute-start(bf16[512,256]{1,0:T(8,128)(2,1)} %get-tuple-element.33), channel_id=1, source_target_pairs={{12,0},{0,4},{4,8},{8,12},{13,1},{1,5},{5,9},{9,13},{14,2},{2,6},{... | collective-permute-start | bytes 786440 | tf_op jit(solution)/shard_map/ppermute | solution.py:47
  16.2 11.9 %collective-permute-start.2 = (bf16[512,256]{1,0:T(8,128)(2,1)}, bf16[512,256]{1,0:T(8,128)(2,1)S(1)}, u32[]{:S(2)}, u32[]{:S(2)}) collective-permute-start(bf16[512,256]{1,0:T(8,128)(2,1)} %get-tuple-element.34), channel_id=1, source_target_pairs={{8,0},{12,4},{0,8},{4,12},{9,1},{13,5},{1,9},{5,13},{10,2},{14,6},... | collective-permute-start | bytes 786440 | tf_op jit(solution)/shard_map/ppermute | solution.py:47
  16.4 9.3 %copy-start.8 = (bf16[128,512]{1,0:T(8,128)(2,1)}, bf16[128,512]{1,0:T(8,128)(2,1)S(1)}, u32[]{:S(2)}) copy-start(bf16[128,512]{1,0:T(8,128)(2,1)S(1)} %collective-permute-done.6.refs_1_) | copy-start | bytes 393220
  16.4 13.9 %collective-permute-start.3 = (bf16[512,256]{1,0:T(8,128)(2,1)}, bf16[512,256]{1,0:T(8,128)(2,1)S(1)}, u32[]{:S(2)}, u32[]{:S(2)}) collective-permute-start(bf16[512,256]{1,0:T(8,128)(2,1)} %get-tuple-element.35), channel_id=1, source_target_pairs={{4,0},{8,4},{12,8},{0,12},{5,1},{9,5},{13,9},{1,13},{6,2},{10,6},{... | collective-permute-start | bytes 786440 | tf_op jit(solution)/shard_map/ppermute | solution.py:47
  23.7 16.0 %collective-permute-start.4 = (bf16[576,256]{1,0:T(8,128)(2,1)S(1)}, bf16[576,256]{1,0:T(8,128)(2,1)S(1)}, u32[]{:S(2)}, u32[]{:S(2)}) collective-permute-start(bf16[576,256]{1,0:T(8,128)(2,1)S(1)} %bitcast.8), channel_id=1, source_target_pairs={{3,0},{0,1},{1,2},{2,3},{7,4},{4,5},{5,6},{6,7},{11,8},{8,9},{9,10... | collective-permute-start | bytes 884744 | tf_op jit(solution)/shard_map/ppermute | solution.py:47
  24.5 16.9 %collective-permute-start.5 = (bf16[576,256]{1,0:T(8,128)(2,1)S(1)}, bf16[576,256]{1,0:T(8,128)(2,1)S(1)}, u32[]{:S(2)}, u32[]{:S(2)}) collective-permute-start(bf16[576,256]{1,0:T(8,128)(2,1)S(1)} %bitcast.9), channel_id=1, source_target_pairs={{1,0},{2,1},{3,2},{0,3},{5,4},{6,5},{7,6},{4,7},{9,8},{10,9},{11,1... | collective-permute-start | bytes 884744 | tf_op jit(solution)/shard_map/ppermute | solution.py:47
  28.1 39.3 %collective-permute-start.11 = (bf16[512,768]{1,0:T(8,128)(2,1)}, bf16[512,768]{1,0:T(8,128)(2,1)S(1)}, u32[]{:S(2)}, u32[]{:S(2)}) collective-permute-start(bf16[512,768]{1,0:T(8,128)(2,1)} %shard_map.114.refs_4_), channel_id=1, source_target_pairs={{4,0},{8,4},{12,8},{0,12},{5,1},{9,5},{13,9},{1,13},{6,2},{10,6},{... | collective-permute-start | bytes 2359304 | tf_op jit(solution)/shard_map/ppermute | solution.py:47
  28.1 39.3 %collective-permute-start.9 = (bf16[512,768]{1,0:T(8,128)(2,1)}, bf16[512,768]{1,0:T(8,128)(2,1)}, u32[]{:S(2)}, u32[]{:S(2)}) collective-permute-start(bf16[512,768]{1,0:T(8,128)(2,1)} %shard_map.114.refs_4_), channel_id=1, source_target_pairs={{12,0},{0,4},{4,8},{8,12},{13,1},{1,5},{5,9},{9,13},{14,2},{2,6},{... | collective-permute-start | bytes 2359304 | tf_op jit(solution)/shard_map/ppermute | solution.py:47
  30.2 23.4 %collective-permute-start = (bf16[576,256]{1,0:T(8,128)(2,1)S(1)}, bf16[576,256]{1,0:T(8,128)(2,1)S(1)}, u32[]{:S(2)}, u32[]{:S(2)}) collective-permute-start(bf16[576,256]{1,0:T(8,128)(2,1)S(1)} %bitcast.10), channel_id=1, source_target_pairs={{2,0},{3,1},{0,2},{1,3},{6,4},{7,5},{4,6},{5,7},{10,8},{11,9},{8,1... | collective-permute-start | bytes 884744 | tf_op jit(solution)/shard_map/ppermute | solution.py:47
  39.7 27.7 %collective-permute-start.10 = (bf16[512,768]{1,0:T(8,128)(2,1)S(1)}, bf16[512,768]{1,0:T(8,128)(2,1)}, u32[]{:S(2)}, u32[]{:S(2)}) collective-permute-start(bf16[512,768]{1,0:T(8,128)(2,1)S(1)} %copy-done.1), channel_id=1, source_target_pairs={{8,0},{12,4},{0,8},{4,12},{9,1},{13,5},{1,9},{5,13},{10,2},{14,6},... | collective-permute-start | bytes 2359304 | tf_op jit(solution)/shard_map/ppermute | solution.py:47
  63.4 36.5 %all-to-all-start.1 = ((bf16[4,640,256]{2,1,0:T(8,128)(2,1)}), bf16[4,640,256]{2,1,0:T(8,128)(2,1)S(1)}, u32[]{:S(2)}, u32[]{:S(2)}) async-start(bf16[4,640,256]{2,1,0:T(8,128)(2,1)} %bitcast.7), calls=%async_computation.1 | async-start | bytes 2621440 | tf_op jit(solution)/shard_map/all_to_all | solution.py:401
  72.5 6.8 %collective-permute-start.16 = (bf16[256,128]{1,0:T(8,128)(2,1)}, bf16[256,128]{1,0:T(8,128)(2,1)S(1)}, u32[]{:S(2)}, u32[]{:S(2)}) collective-permute-start(bf16[256,128]{1,0:T(8,128)(2,1)} %get-tuple-element.49.refs_4_), channel_id=1, source_target_pairs={{2,0},{3,1},{0,2},{1,3},{6,4},{7,5},{4,6},{5,7},{10,8},{11,9},{8,1... | collective-permute-start | bytes 196616 | tf_op jit(solution)/shard_map/ppermute | solution.py:47
  73.8 5.8 %collective-permute-start.14 = (bf16[256,128]{1,0:T(8,128)(2,1)}, bf16[256,128]{1,0:T(8,128)(2,1)S(1)}, u32[]{:S(2)}, u32[]{:S(2)}) collective-permute-start(bf16[256,128]{1,0:T(8,128)(2,1)} %get-tuple-element.49.refs_4_), channel_id=1, source_target_pairs={{3,0},{0,1},{1,2},{2,3},{7,4},{4,5},{5,6},{6,7},{11,8},{8,9},{9,10... | collective-permute-start | bytes 196616 | tf_op jit(solution)/shard_map/ppermute | solution.py:47
  74.6 25.3 %collective-permute-start.12 = (bf16[256,384]{1,0:T(8,128)(2,1)}, bf16[256,384]{1,0:T(8,128)(2,1)S(1)}, u32[]{:S(2)}, u32[]{:S(2)}) collective-permute-start(bf16[256,384]{1,0:T(8,128)(2,1)} %get-tuple-element.51), channel_id=1, source_target_pairs={{0,0},{4,1},{8,2},{12,3},{1,4},{5,5},{9,6},{13,7},{2,8},{6,9},{10,... | collective-permute-start | bytes 589832 | tf_op jit(solution)/shard_map/ppermute | solution.py:432
  76.9 23.0 %collective-permute-start.13 = (bf16[256,384]{1,0:T(8,128)(2,1)}, bf16[256,384]{1,0:T(8,128)(2,1)S(1)}, u32[]{:S(2)}, u32[]{:S(2)}) collective-permute-start(bf16[256,384]{1,0:T(8,128)(2,1)} %get-tuple-element.51), channel_id=1, source_target_pairs={{0,1},{4,2},{8,3},{12,0},{1,5},{5,6},{9,7},{13,4},{2,9},{6,10},{10... | collective-permute-start | bytes 589832 | tf_op jit(solution)/shard_map/ppermute | solution.py:432
  79.4 20.6 %copy-start.11 = (bf16[256,128]{1,0:T(8,128)(2,1)}, bf16[256,128]{1,0:T(8,128)(2,1)S(1)}, u32[]{:S(2)}) copy-start(bf16[256,128]{1,0:T(8,128)(2,1)S(1)} %collective-permute-done.16.refs_6_) | copy-start | bytes 196612
  79.4 20.6 %collective-permute-start.17 = (bf16[256,384]{1,0:T(8,128)(2,1)}, bf16[256,384]{1,0:T(8,128)(2,1)S(1)}, u32[]{:S(2)}, u32[]{:S(2)}) collective-permute-start(bf16[256,384]{1,0:T(8,128)(2,1)} %get-tuple-element.51), channel_id=1, source_target_pairs={{0,3},{4,0},{8,1},{12,2},{1,7},{5,4},{9,5},{13,6},{2,11},{6,8},{10... | collective-permute-start | bytes 589832 | tf_op jit(solution)/shard_map/ppermute | solution.py:432
  79.6 20.4 %copy-start.12 = (bf16[256,128]{1,0:T(8,128)(2,1)}, bf16[256,128]{1,0:T(8,128)(2,1)S(1)}, u32[]{:S(2)}) copy-start(bf16[256,128]{1,0:T(8,128)(2,1)S(1)} %collective-permute-done.14.refs_5_) | copy-start | bytes 196612
  79.6 20.4 %collective-permute-start.15 = (bf16[256,384]{1,0:T(8,128)(2,1)}, bf16[256,384]{1,0:T(8,128)(2,1)S(1)}, u32[]{:S(2)}, u32[]{:S(2)}) collective-permute-start(bf16[256,384]{1,0:T(8,128)(2,1)} %get-tuple-element.51), channel_id=1, source_target_pairs={{0,2},{4,3},{8,0},{12,1},{1,6},{5,7},{9,4},{13,5},{2,10},{6,11},{1... | collective-permute-start | bytes 589832 | tf_op jit(solution)/shard_map/ppermute | solution.py:432
  81.4 18.5 %collective-permute-start.18 = (bf16[256,128]{1,0:T(8,128)(2,1)}, bf16[256,128]{1,0:T(8,128)(2,1)S(1)}, u32[]{:S(2)}, u32[]{:S(2)}) collective-permute-start(bf16[256,128]{1,0:T(8,128)(2,1)} %get-tuple-element.49.refs_4_), channel_id=1, source_target_pairs={{1,0},{2,1},{3,2},{0,3},{5,4},{6,5},{7,6},{4,7},{9,8},{10,9},{11,1... | collective-permute-start | bytes 196616 | tf_op jit(solution)/shard_map/ppermute | solution.py:47
  (17 other events, 38.6 us)

commit v5 on v4

--- a/solution.py
+++ b/solution.py
@@ -52,6 +52,9 @@
 
 
 def call(kernel, out_shape, operands, flops, scratch=(), in_specs=None, out_specs=None):
+    if operands[0] is None:
+        body, operands, in_specs = kernel, operands[1:], in_specs and in_specs[1:]
+        kernel = lambda *refs: body((lax.axis_index("stand"), lax.axis_index("soil")), *refs)
     if in_specs is None:
         in_specs = [SMEM if x.dtype == jnp.int32 else whole(x) for x in operands]
     outs = jax.tree.leaves(out_shape)
@@ -72,7 +75,24 @@
     return pl.BlockSpec((w_in.shape[0], WIDTH), lambda i: (0, index))
 
 
-def project_kernel(place, crossing, home, tokens, grad, w_query, w_out, key_tokens, w_key, w_value, packs, *refs):
+def project_kernel(place, crossing, home, tokens_hbm, grad_hbm, w_in_hbm, w_out_hbm, keys_hbm, packs, *refs):
+    *refs, tokens, grad, w_query, w_out, key_tokens, w_key, w_value, sems = refs
+    copies = [
+        pltpu.make_async_copy(source, target, sems.at[i])
+        for i, (source, target) in enumerate(
+            (
+                (tokens_hbm, tokens),
+                (w_in_hbm.at[:, :WIDTH], w_query),
+                (grad_hbm, grad),
+                (w_out_hbm, w_out),
+                (keys_hbm, key_tokens),
+                (w_in_hbm.at[:, WIDTH : 2 * WIDTH], w_key),
+                (w_in_hbm.at[:, 2 * WIDTH :], w_value),
+            )
+        )
+    ]
+    for copy in copies:
+        copy.start()
     slices, refs = refs[:HEADS], refs[HEADS:]
     outs, (keys, values) = refs[:HEADS], refs[HEADS:]
     lane = lax.broadcasted_iota(jnp.int32, (MASK_ROWS, 2 * DH), 1)
@@ -81,8 +101,10 @@
     for j in range(crossing.shape[1]):
         bit = jnp.where((crossing[0, j] > 0) | (home[0] == j), 1.0, 0.0)
         mask = jnp.where((lane == j) & (row == 0), bit, mask)
-    for half, product in enumerate((mm(tokens[...], w_query[...], NN), mm(grad[...], w_out[...], NT))):
-        product = product.astype(BF16)
+    for half, (left, right, dims) in enumerate(((tokens, w_query, NN), (grad, w_out, NT))):
+        copies[2 * half].wait()
+        copies[2 * half + 1].wait()
+        product = mm(left[...], right[...], dims).astype(BF16)
         for h in range(HEADS):
             packs[h * PACK : h * PACK + BLOCK, half * DH : (half + 1) * DH] = product[:, h * DH : (h + 1) * DH]
     part = tokens.shape[1] // HEADS
@@ -91,7 +113,10 @@
         columns = columns_of(lax.rem(place[0] + d, HEADS), part)
         slices[d][:, :part] = tokens[:, columns]
         slices[d][:, part:] = grad[:, columns]
+    copies[4].wait()
+    copies[5].wait()
     keys[...] = mm(key_tokens[...], w_key[...], NN).astype(BF16)
+    copies[6].wait()
     values[...] = mm(key_tokens[...], w_value[...], NN).astype(BF16)
     for d in range(HEADS):
         head = columns_of(lax.rem(place[1] + d, HEADS), DH)
@@ -107,12 +132,15 @@
         [shape(HEADS * PACK, 2 * DH)]
         + [shape(rows, 2 * width // HEADS)] * HEADS
         + [shape(count, 2 * DH)] * HEADS,
-        (place, crossing, home, query_tokens, out_grad, w_in, w_out, key_tokens, w_in, w_in),
+        (place, crossing, home, query_tokens, out_grad, w_in, w_out, key_tokens),
         4 * (rows + count) * width * WIDTH,
-        scratch=[pltpu.VMEM((count, WIDTH), BF16)] * 2,
-        in_specs=[SMEM] * 3
-        + [whole(query_tokens), whole(out_grad), third(w_in, 0), whole(w_out)]
-        + [whole(key_tokens), third(w_in, 1), third(w_in, 2)],
+        scratch=[pltpu.VMEM((count, WIDTH), BF16)] * 2
+        + [pltpu.VMEM((rows, width), BF16)] * 2
+        + [pltpu.VMEM((width, WIDTH), BF16), pltpu.VMEM((WIDTH, width), BF16)]
+        + [pltpu.VMEM((count, width), BF16)]
+        + [pltpu.VMEM((width, WIDTH), BF16)] * 2
+        + [pltpu.SemaphoreType.DMA((7,))],
+        in_specs=[SMEM] * 3 + [ANY] * 5,
     )
     return results[0], results[1 : HEADS + 1], results[HEADS + 1 :]
 
@@ -406,7 +434,7 @@
 
 
 def head_body(query_tokens, key_tokens, w_in, w_out, out_grad, crossing, home):
-    place = jnp.stack([lax.axis_index("stand"), lax.axis_index("soil")]).astype(jnp.int32)
+    place = None
     distances = range(1, HEADS)
     packs, slices, kvs = project(place, query_tokens, key_tokens, out_grad, w_in, w_out, crossing, home)
     packs = swapped(packs, "soil")

time: 108 us -> 108 us (level)
  transfers between devices with their start and end apart: 21 -> 21, of which waited for: 4 -> 4; matrix products, arithmetic and copies ran while one was open for 0% -> 0% of each run, Pallas kernels for 32% -> 33%
where the time goes in v5:
time: 108 us; the launch traced here: 107 us
  Pallas kernels  47.1 us (44%)
  starting transfers between devices  31.2 us (29%)
  waiting for transfers between devices  23.7 us (22%)
  local copies, waits for them, and re-layouts  3.62 us (3%)
  between operations  1.51 us (1%)
    pallas_call x7, Pallas kernels, call(): pl.pallas_call(kernel, out_shape=out_shape, grid=(1,), in_specs=in_specs,...  47.1 us
    ppermute x15, waiting for transfers between devices, sent(): return lax.ppermute(block, axis, step_from(axis, distance))  23.7 us
    ppermute x15, starting transfers between devices, sent(): return lax.ppermute(block, axis, step_from(axis, distance))  16.5 us
    all_to_all x2, starting transfers between devices, swapped(): return lax.all_to_all(block, axis, 0, 0, tiled=True)  7.95 us
    ppermute x4, starting transfers between devices, head_body(): crosswise.append(lax.ppermute(held, ('soil', 'stand'), route))  6.75 us
    unnamed x40, local copies, waits for them, and re-layouts  3.62 us
  transfers between devices with their start and end apart: 21, of which 4 were waited for; matrix products, arithmetic and copies ran while one was open for 0% of the time, Pallas kernels for 33%

profile of v5, /device:TPU:14, one launch (start us, length us, event | category | flops | bytes accessed | tf_op | source)
XLA Modules:
  0.0 107.1 jit_solution(1564219324169678240)
XLA Ops:
  1.3 5.6 %shard_map.110 = (bf16[576,256]{1,0:T(8,128)(2,1)}, bf16[128,512]{1,0:T(8,128)(2,1)}, bf16[128,512]{1,0:T(8,128)(2,1)}, bf16[128,512]{1,0:T(8,128)(2,1)}, bf16[1...) custom-call(s32[1,16]{1,0:T(1,128)} %refs_0_.2, ...), custom_call_target="tpu_custom_call" | custom-call | flops 1342177280 | bytes 7634978 | tf_op jit(solution)/shard_map/pallas_call | solution.py:62
  6.9 1.6 %collective-permute-start.6 = (bf16[128,512]{1,0:T(8,128)(2,1)}, bf16[128,512]{1,0:T(8,128)(2,1)S(1)}, u32[]{:S(2)}, u32[]{:S(2)}) collective-permute-start(bf16[128,512]{1,0:T(8,128)(2,1)} %get-tuple-element.44), channel_id=1, source_target_pairs={{3,0},{0,1},{1,2},{2,3},{7,4},{4,5},{5,6},{6,7},{11,8},{8,9},{9,10... | collective-permute-start | bytes 393224 | tf_op jit(solution)/shard_map/ppermute | solution.py:47
  8.5 3.9 %all-to-all-start = ((bf16[4,144,256]{2,1,0:T(8,128)(2,1)}), bf16[4,144,256]{2,1,0:T(8,128)(2,1)S(1)}, u32[]{:S(2)}, u32[]{:S(2)}) async-start(bf16[4,144,256]{2,1,0:T(8,128)(2,1)} %bitcast.10), calls=%async_computation | async-start | bytes 589824 | tf_op jit(solution)/shard_map/all_to_all | solution.py:429
  12.5 1.2 %collective-permute-start.7 = (bf16[128,512]{1,0:T(8,128)(2,1)}, bf16[128,512]{1,0:T(8,128)(2,1)S(1)}, u32[]{:S(2)}, u32[]{:S(2)}) collective-permute-start(bf16[128,512]{1,0:T(8,128)(2,1)} %get-tuple-element.45), channel_id=1, source_target_pairs={{2,0},{3,1},{0,2},{1,3},{6,4},{7,5},{4,6},{5,7},{10,8},{11,9},{8,1... | collective-permute-start | bytes 393224 | tf_op jit(solution)/shard_map/ppermute | solution.py:47
  13.7 1.8 %collective-permute-start.8 = (bf16[128,512]{1,0:T(8,128)(2,1)}, bf16[128,512]{1,0:T(8,128)(2,1)S(1)}, u32[]{:S(2)}, u32[]{:S(2)}) collective-permute-start(bf16[128,512]{1,0:T(8,128)(2,1)} %get-tuple-element.46), channel_id=1, source_target_pairs={{1,0},{2,1},{3,2},{0,3},{5,4},{6,5},{7,6},{4,7},{9,8},{10,9},{11,1... | collective-permute-start | bytes 393224 | tf_op jit(solution)/shard_map/ppermute | solution.py:47
  15.6 1.7 %collective-permute-start.3 = (bf16[512,256]{1,0:T(8,128)(2,1)}, bf16[512,256]{1,0:T(8,128)(2,1)S(1)}, u32[]{:S(2)}, u32[]{:S(2)}) collective-permute-start(bf16[512,256]{1,0:T(8,128)(2,1)} %get-tuple-element.35), channel_id=1, source_target_pairs={{4,0},{8,4},{12,8},{0,12},{5,1},{9,5},{13,9},{1,13},{6,2},{10,6},{... | collective-permute-start | bytes 786440 | tf_op jit(solution)/shard_map/ppermute | solution.py:47
  17.3 5.6 %collective-permute-done.7.refs_3_ = bf16[128,512]{1,0:T(8,128)(2,1)S(1)} collective-permute-done((bf16[128,512]{1,0:T(8,128)(2,1)}, bf16[128,512]{1,0:T(8,128)(2,1)S(1)}, u32[]{:S(2)}, u32[]{:S(2)}) %collective-permute-start.7) | collective-permute-done | bytes 131104 | tf_op jit(solution)/shard_map/ppermute | solution.py:47
  23.7 1.3 %collective-permute-start.5 = (bf16[576,256]{1,0:T(8,128)(2,1)S(1)}, bf16[576,256]{1,0:T(8,128)(2,1)S(1)}, u32[]{:S(2)}, u32[]{:S(2)}) collective-permute-start(bf16[576,256]{1,0:T(8,128)(2,1)S(1)} %bitcast.7), channel_id=1, source_target_pairs={{1,0},{2,1},{3,2},{0,3},{5,4},{6,5},{7,6},{4,7},{9,8},{10,9},{11,1... | collective-permute-start | bytes 884744 | tf_op jit(solution)/shard_map/ppermute | solution.py:47
  25.0 2.3 %shard_map.114.refs_5_ = bf16[512,768]{1,0:T(8,128)(2,1)} custom-call(bf16[512,1024]{1,0:T(8,128)(2,1)} %refs_0_.3, bf16[128,512]{1,0:T(8,128)(2,1)} %get-tuple-element.43.refs_1_, bf16[128,512]{1,0:T(8,128)(2,1)} %copy-done.8, bf16[128,512]{1,0:T(8,128)(2,1)} %copy-done.9, bf16[128,512]{1,0:T(8,128)(2,1)} %copy-done.10), custom_call_target="tpu_custom_call" | custom-call | bytes 2359296 | tf_op jit(solution)/shard_map/pallas_call | solution.py:62
  27.4 2.1 %collective-permute-start.9 = (bf16[512,768]{1,0:T(8,128)(2,1)}, bf16[512,768]{1,0:T(8,128)(2,1)}, u32[]{:S(2)}, u32[]{:S(2)}) collective-permute-start(bf16[512,768]{1,0:T(8,128)(2,1)} %shard_map.114.refs_5_), channel_id=1, source_target_pairs={{12,0},{0,4},{4,8},{8,12},{13,1},{1,5},{5,9},{9,13},{14,2},{2,6},{... | collective-permute-start | bytes 2359304 | tf_op jit(solution)/shard_map/ppermute | solution.py:47
  29.5 1.7 %collective-permute-start = (bf16[576,256]{1,0:T(8,128)(2,1)S(1)}, bf16[576,256]{1,0:T(8,128)(2,1)S(1)}, u32[]{:S(2)}, u32[]{:S(2)}) collective-permute-start(bf16[576,256]{1,0:T(8,128)(2,1)S(1)} %bitcast.8), channel_id=1, source_target_pairs={{2,0},{3,1},{0,2},{1,3},{6,4},{7,5},{4,6},{5,7},{10,8},{11,9},{8,1... | collective-permute-start | bytes 884744 | tf_op jit(solution)/shard_map/ppermute | solution.py:47
  31.2 7.8 %shard_map.111 = (bf16[512,256]{1,0:T(8,128)(2,1)}, f32[2048,256]{1,0:T(8,128)}) custom-call(bf16[576,256]{1,0:T(8,128)(2,1)} %bitcast.9, bf16[512,256]{1,0:T(8,128)(2,1)} %get-tuple-element.32.refs_1_.refs_2_, bf16[512,256]{1,0:T(8,128)(2,1)} %copy-done.17, bf16[512,256]{1,0:T(8,128)(2,1)} %copy-done.18, bf16[512,256]{1,0:T(8,128)(2,1)} %copy-done.19), custom_call_target="tpu_custom_call" | custom-call | flops 1610612736 | bytes 2654208 | tf_op jit(solution)/shard_map/pallas_call | solution.py:62
  39.2 1.4 %collective-permute-done.5.refs_1_ = bf16[576,256]{1,0:T(8,128)(2,1)S(1)} collective-permute-done((bf16[576,256]{1,0:T(8,128)(2,1)S(1)}, bf16[576,256]{1,0:T(8,128)(2,1)S(1)}, u32[]{:S(2)}, u32[]{:S(2)}) %collective-permute-start.5) | collective-permute-done | bytes 294944 | tf_op jit(solution)/shard_map/ppermute | solution.py:47
  41.3 11.6 %shard_map.112 = (bf16[512,256]{1,0:T(8,128)(2,1)}, bf16[512,256]{1,0:T(8,128)(2,1)}, f32[2048,256]{1,0:T(8,128)}) custom-call(bf16[576,256]{1,0:T(8,128)(2,1)} %copy-done.14, bf16[576,256]{1,0:T(8,128)(2,1)} %copy-done.15, bf16[512,256]{1,0:T(8,128)(2,1)} %get-tuple-element.32.refs_1_.refs_2_, bf16[512,256]{1,0:T(8,128)(2,1)} %copy-done.17, ...), custom_call_target="tpu_custom_call" | custom-call | flops 3221225472 | bytes 3211264 | tf_op jit(solution)/shard_map/pallas_call | solution.py:62
  53.7 9.0 %shard_map.113 = (bf16[512,256]{1,0:T(8,128)(2,1)}, bf16[2560,256]{1,0:T(8,128)(2,1)}) custom-call(bf16[576,256]{1,0:T(8,128)(2,1)} %copy-done.16, bf16[512,256]{1,0:T(8,128)(2,1)} %get-tuple-element.32.refs_1_.refs_2_, bf16[512,256]{1,0:T(8,128)(2,1)} %copy-done.17, bf16[512,256]{1,0:T(8,128)(2,1)} %copy-done.18, bf16[512,256]{1,0:T(8,128)(2,1)} %copy-done.19, ...), custom_call_target="tpu_custom_call" | custom-call | flops 1610612736 | bytes 5275648 | tf_op jit(solution)/shard_map/pallas_call | solution.py:62
  62.7 4.0 %all-to-all-start.1 = ((bf16[4,640,256]{2,1,0:T(8,128)(2,1)}), bf16[4,640,256]{2,1,0:T(8,128)(2,1)S(1)}, u32[]{:S(2)}, u32[]{:S(2)}) async-start(bf16[4,640,256]{2,1,0:T(8,128)(2,1)} %bitcast.5), calls=%async_computation.1 | async-start | bytes 2621440 | tf_op jit(solution)/shard_map/all_to_all | solution.py:429
  67.6 4.2 %shard_map.115 = (bf16[256,384]{1,0:T(8,128)(2,1)}, bf16[256,128]{1,0:T(8,128)(2,1)}) custom-call(bf16[2560,256]{1,0:T(8,128)(2,1)} %get-tuple-element.39.refs_0_, bf16[512,256]{1,0:T(8,128)(2,1)} %get-tuple-element.38.refs_7_.refs_1_, bf16[512,256]{1,0:T(8,128)(2,1)} %get-tuple-element.40.refs_2_, bf16[512,256]{1,0:T(8,128)(2,1)} %get-tuple-element.41.refs_3_, ...), custom_call_target="tpu_custom_call" | custom-call | flops 536870912 | bytes 5767168 | tf_op jit(solution)/shard_map/pallas_call | solution.py:62
  71.8 1.2 %collective-permute-start.16 = (bf16[256,128]{1,0:T(8,128)(2,1)}, bf16[256,128]{1,0:T(8,128)(2,1)S(1)}, u32[]{:S(2)}, u32[]{:S(2)}) collective-permute-start(bf16[256,128]{1,0:T(8,128)(2,1)} %get-tuple-element.49.refs_4_), channel_id=1, source_target_pairs={{2,0},{3,1},{0,2},{1,3},{6,4},{7,5},{4,6},{5,7},{10,8},{11,9},{8,1... | collective-permute-start | bytes 196616 | tf_op jit(solution)/shard_map/ppermute | solution.py:47
  73.9 2.3 %collective-permute-start.12 = (bf16[256,384]{1,0:T(8,128)(2,1)}, bf16[256,384]{1,0:T(8,128)(2,1)S(1)}, u32[]{:S(2)}, u32[]{:S(2)}) collective-permute-start(bf16[256,384]{1,0:T(8,128)(2,1)} %get-tuple-element.51), channel_id=1, source_target_pairs={{0,0},{4,1},{8,2},{12,3},{1,4},{5,5},{9,6},{13,7},{2,8},{6,9},{10,... | collective-permute-start | bytes 589832 | tf_op jit(solution)/shard_map/ppermute | solution.py:460
  76.2 2.4 %collective-permute-start.13 = (bf16[256,384]{1,0:T(8,128)(2,1)}, bf16[256,384]{1,0:T(8,128)(2,1)S(1)}, u32[]{:S(2)}, u32[]{:S(2)}) collective-permute-start(bf16[256,384]{1,0:T(8,128)(2,1)} %get-tuple-element.51), channel_id=1, source_target_pairs={{0,1},{4,2},{8,3},{12,0},{1,5},{5,6},{9,7},{13,4},{2,9},{6,10},{10... | collective-permute-start | bytes 589832 | tf_op jit(solution)/shard_map/ppermute | solution.py:460
  78.8 1.9 %collective-permute-start.15 = (bf16[256,384]{1,0:T(8,128)(2,1)}, bf16[256,384]{1,0:T(8,128)(2,1)S(1)}, u32[]{:S(2)}, u32[]{:S(2)}) collective-permute-start(bf16[256,384]{1,0:T(8,128)(2,1)} %get-tuple-element.51), channel_id=1, source_target_pairs={{0,2},{4,3},{8,0},{12,1},{1,6},{5,7},{9,4},{13,5},{2,10},{6,11},{1... | collective-permute-start | bytes 589832 | tf_op jit(solution)/shard_map/ppermute | solution.py:460
  80.7 2.6 %collective-permute-start.18 = (bf16[256,128]{1,0:T(8,128)(2,1)}, bf16[256,128]{1,0:T(8,128)(2,1)S(1)}, u32[]{:S(2)}, u32[]{:S(2)}) collective-permute-start(bf16[256,128]{1,0:T(8,128)(2,1)} %get-tuple-element.49.refs_4_), channel_id=1, source_target_pairs={{1,0},{2,1},{3,2},{0,3},{5,4},{6,5},{7,6},{4,7},{9,8},{10,9},{11,1... | collective-permute-start | bytes 196616 | tf_op jit(solution)/shard_map/ppermute | solution.py:47
  83.3 15.9 %collective-permute-done.18.refs_7_ = bf16[256,128]{1,0:T(8,128)(2,1)S(1)} collective-permute-done((bf16[256,128]{1,0:T(8,128)(2,1)}, bf16[256,128]{1,0:T(8,128)(2,1)S(1)}, u32[]{:S(2)}, u32[]{:S(2)}) %collective-permute-start.18) | collective-permute-done | bytes 65568 | tf_op jit(solution)/shard_map/ppermute | solution.py:47
  100.6 6.5 %shard_map.116 = (f32[256,1536]{1,0:T(8,128)}, f32[128,1024]{1,0:T(8,128)}, bf16[512,1024]{1,0:T(8,128)(2,1)}, bf16[128,1024]{1,0:T(8,128)(2,1)}, bf16[128,1024]{1,0:T(8,128)(2,1)}) custom-call(bf16[256,384]{1,0:T(8,128)(2,1)} %copy-done.4, bf16[256,384]{1,0:T(8,128)(2,1)} %copy-done.5, bf16[256,384]{1,0:T(8,128)(2,1)} %copy-done.7, ...), custom_call_target="tpu_custom_call" | custom-call | flops 1342177280 | bytes 15466496 | tf_op jit(solution)/shard_map/pallas_call | solution.py:62
  (65 shorter events, 5.8 us)
Async XLA Ops:
  6.9 8.7 %collective-permute-start.6 = (bf16[128,512]{1,0:T(8,128)(2,1)}, bf16[128,512]{1,0:T(8,128)(2,1)S(1)}, u32[]{:S(2)}, u32[]{:S(2)}) collective-permute-start(bf16[128,512]{1,0:T(8,128)(2,1)} %get-tuple-element.44), channel_id=1, source_target_pairs={{3,0},{0,1},{1,2},{2,3},{7,4},{4,5},{5,6},{6,7},{11,8},{8,9},{9,10... | collective-permute-start | bytes 393224 | tf_op jit(solution)/shard_map/ppermute | solution.py:47
  8.5 14.4 %all-to-all-start = ((bf16[4,144,256]{2,1,0:T(8,128)(2,1)}), bf16[4,144,256]{2,1,0:T(8,128)(2,1)S(1)}, u32[]{:S(2)}, u32[]{:S(2)}) async-start(bf16[4,144,256]{2,1,0:T(8,128)(2,1)} %bitcast.10), calls=%async_computation | async-start | bytes 589824 | tf_op jit(solution)/shard_map/all_to_all | solution.py:429
  12.5 10.5 %collective-permute-start.7 = (bf16[128,512]{1,0:T(8,128)(2,1)}, bf16[128,512]{1,0:T(8,128)(2,1)S(1)}, u32[]{:S(2)}, u32[]{:S(2)}) collective-permute-start(bf16[128,512]{1,0:T(8,128)(2,1)} %get-tuple-element.45), channel_id=1, source_target_pairs={{2,0},{3,1},{0,2},{1,3},{6,4},{7,5},{4,6},{5,7},{10,8},{11,9},{8,1... | collective-permute-start | bytes 393224 | tf_op jit(solution)/shard_map/ppermute | solution.py:47
  13.7 10.0 %collective-permute-start.8 = (bf16[128,512]{1,0:T(8,128)(2,1)}, bf16[128,512]{1,0:T(8,128)(2,1)S(1)}, u32[]{:S(2)}, u32[]{:S(2)}) collective-permute-start(bf16[128,512]{1,0:T(8,128)(2,1)} %get-tuple-element.46), channel_id=1, source_target_pairs={{1,0},{2,1},{3,2},{0,3},{5,4},{6,5},{7,6},{4,7},{9,8},{10,9},{11,1... | collective-permute-start | bytes 393224 | tf_op jit(solution)/shard_map/ppermute | solution.py:47
  15.5 11.8 %collective-permute-start.1 = (bf16[512,256]{1,0:T(8,128)(2,1)}, bf16[512,256]{1,0:T(8,128)(2,1)S(1)}, u32[]{:S(2)}, u32[]{:S(2)}) collective-permute-start(bf16[512,256]{1,0:T(8,128)(2,1)} %get-tuple-element.33), channel_id=1, source_target_pairs={{12,0},{0,4},{4,8},{8,12},{13,1},{1,5},{5,9},{9,13},{14,2},{2,6},{... | collective-permute-start | bytes 786440 | tf_op jit(solution)/shard_map/ppermute | solution.py:47
  15.5 11.8 %collective-permute-start.2 = (bf16[512,256]{1,0:T(8,128)(2,1)}, bf16[512,256]{1,0:T(8,128)(2,1)S(1)}, u32[]{:S(2)}, u32[]{:S(2)}) collective-permute-start(bf16[512,256]{1,0:T(8,128)(2,1)} %get-tuple-element.34), channel_id=1, source_target_pairs={{8,0},{12,4},{0,8},{4,12},{9,1},{13,5},{1,9},{5,13},{10,2},{14,6},... | collective-permute-start | bytes 786440 | tf_op jit(solution)/shard_map/ppermute | solution.py:47
  15.6 9.3 %copy-start.8 = (bf16[128,512]{1,0:T(8,128)(2,1)}, bf16[128,512]{1,0:T(8,128)(2,1)S(1)}, u32[]{:S(2)}) copy-start(bf16[128,512]{1,0:T(8,128)(2,1)S(1)} %collective-permute-done.6.refs_2_) | copy-start | bytes 393220
  15.6 13.9 %collective-permute-start.3 = (bf16[512,256]{1,0:T(8,128)(2,1)}, bf16[512,256]{1,0:T(8,128)(2,1)S(1)}, u32[]{:S(2)}, u32[]{:S(2)}) collective-permute-start(bf16[512,256]{1,0:T(8,128)(2,1)} %get-tuple-element.35), channel_id=1, source_target_pairs={{4,0},{8,4},{12,8},{0,12},{5,1},{9,5},{13,9},{1,13},{6,2},{10,6},{... | collective-permute-start | bytes 786440 | tf_op jit(solution)/shard_map/ppermute | solution.py:47
  22.9 16.1 %collective-permute-start.4 = (bf16[576,256]{1,0:T(8,128)(2,1)S(1)}, bf16[576,256]{1,0:T(8,128)(2,1)S(1)}, u32[]{:S(2)}, u32[]{:S(2)}) collective-permute-start(bf16[576,256]{1,0:T(8,128)(2,1)S(1)} %bitcast.6), channel_id=1, source_target_pairs={{3,0},{0,1},{1,2},{2,3},{7,4},{4,5},{5,6},{6,7},{11,8},{8,9},{9,10... | collective-permute-start | bytes 884744 | tf_op jit(solution)/shard_map/ppermute | solution.py:47
  23.7 16.9 %collective-permute-start.5 = (bf16[576,256]{1,0:T(8,128)(2,1)S(1)}, bf16[576,256]{1,0:T(8,128)(2,1)S(1)}, u32[]{:S(2)}, u32[]{:S(2)}) collective-permute-start(bf16[576,256]{1,0:T(8,128)(2,1)S(1)} %bitcast.7), channel_id=1, source_target_pairs={{1,0},{2,1},{3,2},{0,3},{5,4},{6,5},{7,6},{4,7},{9,8},{10,9},{11,1... | collective-permute-start | bytes 884744 | tf_op jit(solution)/shard_map/ppermute | solution.py:47
  27.3 39.4 %collective-permute-start.11 = (bf16[512,768]{1,0:T(8,128)(2,1)}, bf16[512,768]{1,0:T(8,128)(2,1)S(1)}, u32[]{:S(2)}, u32[]{:S(2)}) collective-permute-start(bf16[512,768]{1,0:T(8,128)(2,1)} %shard_map.114.refs_5_), channel_id=1, source_target_pairs={{4,0},{8,4},{12,8},{0,12},{5,1},{9,5},{13,9},{1,13},{6,2},{10,6},{... | collective-permute-start | bytes 2359304 | tf_op jit(solution)/shard_map/ppermute | solution.py:47
  27.4 39.4 %collective-permute-start.9 = (bf16[512,768]{1,0:T(8,128)(2,1)}, bf16[512,768]{1,0:T(8,128)(2,1)}, u32[]{:S(2)}, u32[]{:S(2)}) collective-permute-start(bf16[512,768]{1,0:T(8,128)(2,1)} %shard_map.114.refs_5_), channel_id=1, source_target_pairs={{12,0},{0,4},{4,8},{8,12},{13,1},{1,5},{5,9},{9,13},{14,2},{2,6},{... | collective-permute-start | bytes 2359304 | tf_op jit(solution)/shard_map/ppermute | solution.py:47
  29.5 23.5 %collective-permute-start = (bf16[576,256]{1,0:T(8,128)(2,1)S(1)}, bf16[576,256]{1,0:T(8,128)(2,1)S(1)}, u32[]{:S(2)}, u32[]{:S(2)}) collective-permute-start(bf16[576,256]{1,0:T(8,128)(2,1)S(1)} %bitcast.8), channel_id=1, source_target_pairs={{2,0},{3,1},{0,2},{1,3},{6,4},{7,5},{4,6},{5,7},{10,8},{11,9},{8,1... | collective-permute-start | bytes 884744 | tf_op jit(solution)/shard_map/ppermute | solution.py:47
  39.0 27.7 %collective-permute-start.10 = (bf16[512,768]{1,0:T(8,128)(2,1)S(1)}, bf16[512,768]{1,0:T(8,128)(2,1)}, u32[]{:S(2)}, u32[]{:S(2)}) collective-permute-start(bf16[512,768]{1,0:T(8,128)(2,1)S(1)} %copy-done.1), channel_id=1, source_target_pairs={{8,0},{12,4},{0,8},{4,12},{9,1},{13,5},{1,9},{5,13},{10,2},{14,6},... | collective-permute-start | bytes 2359304 | tf_op jit(solution)/shard_map/ppermute | solution.py:47
  62.7 36.5 %all-to-all-start.1 = ((bf16[4,640,256]{2,1,0:T(8,128)(2,1)}), bf16[4,640,256]{2,1,0:T(8,128)(2,1)S(1)}, u32[]{:S(2)}, u32[]{:S(2)}) async-start(bf16[4,640,256]{2,1,0:T(8,128)(2,1)} %bitcast.5), calls=%async_computation.1 | async-start | bytes 2621440 | tf_op jit(solution)/shard_map/all_to_all | solution.py:429
  71.8 6.8 %collective-permute-start.16 = (bf16[256,128]{1,0:T(8,128)(2,1)}, bf16[256,128]{1,0:T(8,128)(2,1)S(1)}, u32[]{:S(2)}, u32[]{:S(2)}) collective-permute-start(bf16[256,128]{1,0:T(8,128)(2,1)} %get-tuple-element.49.refs_4_), channel_id=1, source_target_pairs={{2,0},{3,1},{0,2},{1,3},{6,4},{7,5},{4,6},{5,7},{10,8},{11,9},{8,1... | collective-permute-start | bytes 196616 | tf_op jit(solution)/shard_map/ppermute | solution.py:47
  73.1 5.8 %collective-permute-start.14 = (bf16[256,128]{1,0:T(8,128)(2,1)}, bf16[256,128]{1,0:T(8,128)(2,1)S(1)}, u32[]{:S(2)}, u32[]{:S(2)}) collective-permute-start(bf16[256,128]{1,0:T(8,128)(2,1)} %get-tuple-element.49.refs_4_), channel_id=1, source_target_pairs={{3,0},{0,1},{1,2},{2,3},{7,4},{4,5},{5,6},{6,7},{11,8},{8,9},{9,10... | collective-permute-start | bytes 196616 | tf_op jit(solution)/shard_map/ppermute | solution.py:47
  73.9 25.3 %collective-permute-start.12 = (bf16[256,384]{1,0:T(8,128)(2,1)}, bf16[256,384]{1,0:T(8,128)(2,1)S(1)}, u32[]{:S(2)}, u32[]{:S(2)}) collective-permute-start(bf16[256,384]{1,0:T(8,128)(2,1)} %get-tuple-element.51), channel_id=1, source_target_pairs={{0,0},{4,1},{8,2},{12,3},{1,4},{5,5},{9,6},{13,7},{2,8},{6,9},{10,... | collective-permute-start | bytes 589832 | tf_op jit(solution)/shard_map/ppermute | solution.py:460
  76.2 23.0 %collective-permute-start.13 = (bf16[256,384]{1,0:T(8,128)(2,1)}, bf16[256,384]{1,0:T(8,128)(2,1)S(1)}, u32[]{:S(2)}, u32[]{:S(2)}) collective-permute-start(bf16[256,384]{1,0:T(8,128)(2,1)} %get-tuple-element.51), channel_id=1, source_target_pairs={{0,1},{4,2},{8,3},{12,0},{1,5},{5,6},{9,7},{13,4},{2,9},{6,10},{10... | collective-permute-start | bytes 589832 | tf_op jit(solution)/shard_map/ppermute | solution.py:460
  78.6 20.7 %copy-start.11 = (bf16[256,128]{1,0:T(8,128)(2,1)}, bf16[256,128]{1,0:T(8,128)(2,1)S(1)}, u32[]{:S(2)}) copy-start(bf16[256,128]{1,0:T(8,128)(2,1)S(1)} %collective-permute-done.16.refs_6_) | copy-start | bytes 196612
  78.6 20.6 %collective-permute-start.17 = (bf16[256,384]{1,0:T(8,128)(2,1)}, bf16[256,384]{1,0:T(8,128)(2,1)S(1)}, u32[]{:S(2)}, u32[]{:S(2)}) collective-permute-start(bf16[256,384]{1,0:T(8,128)(2,1)} %get-tuple-element.51), channel_id=1, source_target_pairs={{0,3},{4,0},{8,1},{12,2},{1,7},{5,4},{9,5},{13,6},{2,11},{6,8},{10... | collective-permute-start | bytes 589832 | tf_op jit(solution)/shard_map/ppermute | solution.py:460
  78.8 20.5 %copy-start.12 = (bf16[256,128]{1,0:T(8,128)(2,1)}, bf16[256,128]{1,0:T(8,128)(2,1)S(1)}, u32[]{:S(2)}) copy-start(bf16[256,128]{1,0:T(8,128)(2,1)S(1)} %collective-permute-done.14.refs_5_) | copy-start | bytes 196612
  78.8 20.4 %collective-permute-start.15 = (bf16[256,384]{1,0:T(8,128)(2,1)}, bf16[256,384]{1,0:T(8,128)(2,1)S(1)}, u32[]{:S(2)}, u32[]{:S(2)}) collective-permute-start(bf16[256,384]{1,0:T(8,128)(2,1)} %get-tuple-element.51), channel_id=1, source_target_pairs={{0,2},{4,3},{8,0},{12,1},{1,6},{5,7},{9,4},{13,5},{2,10},{6,11},{1... | collective-permute-start | bytes 589832 | tf_op jit(solution)/shard_map/ppermute | solution.py:460
  80.7 18.5 %collective-permute-start.18 = (bf16[256,128]{1,0:T(8,128)(2,1)}, bf16[256,128]{1,0:T(8,128)(2,1)S(1)}, u32[]{:S(2)}, u32[]{:S(2)}) collective-permute-start(bf16[256,128]{1,0:T(8,128)(2,1)} %get-tuple-element.49.refs_4_), channel_id=1, source_target_pairs={{1,0},{2,1},{3,2},{0,3},{5,4},{6,5},{7,6},{4,7},{9,8},{10,9},{11,1... | collective-permute-start | bytes 196616 | tf_op jit(solution)/shard_map/ppermute | solution.py:47
  (17 other events, 38.6 us)
